TPU v7x, 32 devices: a whole 2x2x4 slice. The times are simulated.
32 devices in a mesh: dp: 4 (over y, x), expert: 8 (over z, core).
Axes of the slice: x: 2, y: 2, z: 4, core: 2. Of those that a mesh axis runs over, the one named last changes fastest.
Arguments:
- tokens: bfloat16 [4096, 7168], P(('dp', 'expert')), may hold values from -6 to 6
- route_ids: int32 [4096, 8], P(('dp', 'expert')), may hold values from 0 to 255, as said below
- gate_weights: float32 [4096, 8], P(('dp', 'expert')), may hold values from 0.3 to 1.2
- gate_weight: bfloat16 [8, 7168, 1024], P('expert', 'dp'), may hold values from -0.0625 to 0.0625
- up_weight: bfloat16 [8, 7168, 1024], P('expert', 'dp'), may hold values from -0.0625 to 0.0625
- down_weight: bfloat16 [8, 7168, 1024], P('expert', 'dp'), may hold values from -0.1875 to 0.1875
- cotangent: bfloat16 [4096, 7168], P(('dp', 'expert')), may hold values from -3 to 3
Outputs:
- output: bfloat16 [4096, 7168], P(('dp', 'expert'))
- grad_tokens: bfloat16 [4096, 7168], P(('dp', 'expert'))
- grad_gate: bfloat16 [8, 7168, 1024], P('expert', 'dp')
- grad_up: bfloat16 [8, 7168, 1024], P('expert', 'dp')
- grad_down: bfloat16 [8, 7168, 1024], P('expert', 'dp')
Inputs may be any that keep to these rules, and one draw needn't show every extreme that they name: `route_ids`: each token's 8 numbers are different, and at most one of them is below 8. Among the 128 tokens of one device at most 4 name any one number below 8; for each index of dp, one number below 8 is named by exactly 4 tokens of every device with that index.
All inputs are finite; a program needn't handle non-finite values.
Results may differ from a plain program's by a relative error of at most 0.018.
Values may be sent and summed in bfloat16 or wider, within the bound.
No kernel may reach another device: no remote copies, remote signals or barrier semaphores. Data moves between devices by JAX's collectives and lax.ppermute only.
A program may use at most 128 MiB of HBM per device.

v0:
```python
import jax
import jax.numpy as jnp
from jax import lax
from jax.sharding import PartitionSpec as P

CAP = 4


def contract_last(left, right):
    return lax.dot_general(
        left, right, (((1,), (1,)), ((), ())), preferred_element_type=jnp.float32
    )


def contract_first(left, right):
    return lax.dot_general(
        left, right, (((0,), (0,)), ((), ())), preferred_element_type=jnp.float32
    )


def body(tokens, route_ids, gate_weights, gate_weight, up_weight, down_weight, cotangent):
    experts = lax.axis_size("expert")
    gate_mat = gate_weight[0]
    up_mat = up_weight[0]
    down_mat = down_weight[0]
    slice_width = gate_mat.shape[0]
    hidden_units = gate_mat.shape[1]
    labels = jnp.arange(experts, dtype=jnp.int32)
    matches = route_ids[:, :, None] == labels
    chosen = jnp.any(matches, axis=1).astype(jnp.int32)
    gate_of = jnp.sum(jnp.where(matches, gate_weights[:, :, None], 0.0), axis=1)
    ranks = jnp.cumsum(chosen, axis=0) - chosen
    placed = (chosen[:, :, None] == 1) & (ranks[:, :, None] == jnp.arange(CAP, dtype=jnp.int32))
    placer = placed.astype(jnp.bfloat16)
    slot_gate = jnp.sum(jnp.where(placed, gate_of[:, :, None], 0.0), axis=0)
    send_rows = jnp.einsum(
        "tjc,td->jcd", placer, tokens, preferred_element_type=jnp.float32
    ).astype(jnp.bfloat16)
    picked = jnp.einsum("tjc,td->jcd", placer, cotangent, preferred_element_type=jnp.float32)
    send_grads = (slot_gate[:, :, None] * picked).astype(jnp.bfloat16)
    recv_rows, recv_grads = (
        lax.all_to_all(
            lax.all_to_all(send_rows, "dp", split_axis=2, concat_axis=1, tiled=True),
            "expert",
            split_axis=0,
            concat_axis=0,
            tiled=True,
        ),
        lax.all_to_all(
            lax.all_to_all(send_grads, "dp", split_axis=2, concat_axis=1, tiled=True),
            "expert",
            split_axis=0,
            concat_axis=0,
            tiled=True,
        ),
    )
    layout = recv_rows.shape
    row_count = layout[0] * layout[1]
    flat_rows = recv_rows.reshape(row_count, slice_width)
    flat_grads = recv_grads.reshape(row_count, slice_width)
    row_block = flat_rows
    grad_block = flat_grads
    mine = lax.psum_scatter(
        jnp.concatenate(
            [
                jnp.dot(row_block, gate_mat, preferred_element_type=jnp.float32),
                jnp.dot(row_block, up_mat, preferred_element_type=jnp.float32),
                jnp.dot(grad_block, down_mat, preferred_element_type=jnp.float32),
            ],
            axis=1,
        ).astype(jnp.bfloat16),
        "dp",
        scatter_dimension=0,
        tiled=True,
    ).astype(jnp.float32)
    pre_gate = mine[:, :hidden_units]
    pre_up = mine[:, hidden_units : 2 * hidden_units]
    hidden_grad = mine[:, 2 * hidden_units :]
    squash = jax.nn.sigmoid(pre_gate)
    silu_gate = pre_gate * squash
    hidden = (silu_gate * pre_up).astype(jnp.bfloat16)
    gate_grad = (hidden_grad * pre_up * squash * (1.0 + pre_gate * (1.0 - squash))).astype(
        jnp.bfloat16
    )
    up_grad = (hidden_grad * silu_gate).astype(jnp.bfloat16)
    hidden, gate_grad, up_grad = (hidden, gate_grad, up_grad)
    hidden_part = lax.all_gather(hidden, "dp", axis=0, tiled=True)
    gate_part = lax.all_gather(gate_grad, "dp", axis=0, tiled=True)
    up_part = lax.all_gather(up_grad, "dp", axis=0, tiled=True)
    row_block = flat_rows
    grad_block = flat_grads
    out_part = contract_last(hidden_part, down_mat).astype(jnp.bfloat16)
    input_part = (contract_last(gate_part, gate_mat) + contract_last(up_part, up_mat)).astype(
        jnp.bfloat16
    )
    out_rows = out_part
    input_rows = input_part
    gate_total = contract_first(row_block, gate_part)
    up_total = contract_first(row_block, up_part)
    down_total = contract_first(grad_block, hidden_part)
    carry = (out_rows, input_rows, gate_total, up_total, down_total)
    out_rows, input_rows, gate_total, up_total, down_total = carry
    got_out, got_input = (
        lax.all_to_all(
            lax.all_to_all(out_rows.reshape(layout), "dp", split_axis=1, concat_axis=2, tiled=True),
            "expert",
            split_axis=0,
            concat_axis=0,
            tiled=True,
        ),
        lax.all_to_all(
            lax.all_to_all(
                input_rows.reshape(layout), "dp", split_axis=1, concat_axis=2, tiled=True
            ),
            "expert",
            split_axis=0,
            concat_axis=0,
            tiled=True,
        ),
    )
    weighted = slot_gate[:, :, None] * got_out.astype(jnp.float32)
    output = jnp.einsum(
        "tjc,jcd->td", placed.astype(jnp.float32), weighted, precision=lax.Precision.HIGHEST
    ).astype(jnp.bfloat16)
    grad_tokens = jnp.einsum(
        "tjc,jcd->td", placer, got_input, preferred_element_type=jnp.float32
    ).astype(jnp.bfloat16)
    return (
        output,
        grad_tokens,
        gate_total.astype(jnp.bfloat16)[None],
        up_total.astype(jnp.bfloat16)[None],
        down_total.astype(jnp.bfloat16)[None],
    )


def solution(mesh):
    return jax.shard_map(
        body,
        mesh=mesh,
        in_specs=(
            P(("dp", "expert"), None),
            P(("dp", "expert"), None),
            P(("dp", "expert"), None),
            P("expert", "dp", None),
            P("expert", "dp", None),
            P("expert", "dp", None),
            P(("dp", "expert"), None),
        ),
        out_specs=(
            P(("dp", "expert"), None),
            P(("dp", "expert"), None),
            P("expert", "dp", None),
            P("expert", "dp", None),
            P("expert", "dp", None),
        ),
        check_vma=False,
    )
```

profile of v0, /device:TPU:0, one launch (start us, length us, event | category | flops | bytes accessed | tf_op | source)
XLA Modules:
  0.0 243.5 jit_solution(8787925912496322918)
XLA Ops:
  7.2 0.8 fusion.44
  8.7 0.4 convolution_convert_fusion
  9.1 7.2 %copy.72 = bf16[8,4,7168]{0,1,2:T(4,128)(2,1)} copy(bf16[8,4,7168]{2,0,1:T(8,128)(2,1)S(1)} %convolution_convert_fusion) | data formatting | bytes 917504 | tf_op jit(solution)/shard_map/convert_element_type | solution.py:38
  16.3 10.2 %reshape.53 = bf16[4,2,28672]{2,1,0:T(2,128)(2,1)} reshape(bf16[7168,4,8]{2,1,0:T(4,128)(2,1)} %bitcast.83) | data formatting | bytes 917504
  26.5 5.2 %all-to-all-start = ((bf16[4,2,28672]{2,1,0:T(2,128)(2,1)}), bf16[4,2,28672]{2,1,0:T(2,128)(2,1)S(1)}, u32[]{:S(2)}, u32[]{:S(2)}) async-start(bf16[4,2,28672]{2,1,0:T(2,128)(2,1)} %reshape.53), calls=%async_computation | async-start | bytes 917504 | tf_op jit(solution)/shard_map/all_to_all | solution.py:43
  31.8 0.4 fusion.2
  32.2 7.2 %copy.76 = bf16[8,4,7168]{0,1,2:T(4,128)(2,1)} copy(bf16[8,4,7168]{2,0,1:T(8,128)(2,1)S(1)} %fusion.2) | data formatting | bytes 917504 | tf_op jit(solution)/shard_map/convert_element_type | solution.py:40
  39.4 10.1 %reshape.51 = bf16[4,2,28672]{2,1,0:T(2,128)(2,1)} reshape(bf16[7168,4,8]{2,1,0:T(4,128)(2,1)} %bitcast.84) | data formatting | bytes 917504
  49.5 4.2 %all-to-all-start.2 = ((bf16[4,2,28672]{2,1,0:T(2,128)(2,1)}), bf16[4,2,28672]{2,1,0:T(2,128)(2,1)S(1)}, u32[]{:S(2)}, u32[]{:S(2)}) async-start(bf16[4,2,28672]{2,1,0:T(2,128)(2,1)} %reshape.51), calls=%async_computation.2 | async-start | bytes 917504 | tf_op jit(solution)/shard_map/all_to_all | solution.py:50
  53.6 9.8 %reshape.54 = bf16[7168,4,8]{2,1,0:T(4,128)(2,1)} reshape(bf16[4,2,28672]{2,1,0:T(2,128)(2,1)S(1)} %all-to-all-done) | data formatting | bytes 917504
  63.4 8.7 %copy.74 = bf16[8,4,4,1792]{3,0,2,1:T(8,128)(2,1)S(1)} copy(bf16[8,4,4,1792]{0,2,3,1:T(4,128)(2,1)} %bitcast.85) | data formatting | bytes 917504 | tf_op jit(solution)/shard_map/all_to_all | solution.py:43
  72.1 0.8 copy.75
  73.0 4.9 %all-to-all-start.1 = ((bf16[8,16,1792]{2,1,0:T(8,128)(2,1)}), bf16[8,16,1792]{2,1,0:T(8,128)(2,1)S(1)}, u32[]{:S(2)}, u32[]{:S(2)}) async-start(bf16[8,16,1792]{2,1,0:T(8,128)(2,1)} %copy.75), calls=%async_computation.1 | async-start | bytes 917504 | tf_op jit(solution)/shard_map/all_to_all | solution.py:42
  77.9 9.8 %reshape.52 = bf16[7168,4,8]{2,1,0:T(4,128)(2,1)} reshape(bf16[4,2,28672]{2,1,0:T(2,128)(2,1)S(1)} %all-to-all-done.2) | data formatting | bytes 917504
  87.7 8.7 %copy.78 = bf16[8,4,4,1792]{3,0,2,1:T(8,128)(2,1)S(1)} copy(bf16[8,4,4,1792]{0,2,3,1:T(4,128)(2,1)} %bitcast.86) | data formatting | bytes 917504 | tf_op jit(solution)/shard_map/all_to_all | solution.py:50
  96.4 0.8 copy.79
  97.2 5.1 %all-to-all-start.3 = ((bf16[8,16,1792]{2,1,0:T(8,128)(2,1)}), bf16[8,16,1792]{2,1,0:T(8,128)(2,1)S(1)}, u32[]{:S(2)}, u32[]{:S(2)}) async-start(bf16[8,16,1792]{2,1,0:T(8,128)(2,1)} %copy.79), calls=%async_computation.3 | async-start | bytes 917504 | tf_op jit(solution)/shard_map/all_to_all | solution.py:49
  102.3 2.8 %fusion.32 = bf16[128,1024]{1,0:T(8,128)(2,1)S(1)} fusion(bf16[128,1792]{1,0:T(8,128)(2,1)S(1)} %bitcast.87, bf16[1,1792,1024]{2,1,0:T(8,128)(2,1)} %param.11), kind=kOutput, calls=%fused_computation.31 | convolution fusion | flops 469893120 | bytes 4390912 | tf_op jit(solution)/shard_map/dot_general | solution.py:67
  105.5 0.6 fusion.29
  106.1 10.1 %all-to-all-done.3 = bf16[8,16,1792]{2,1,0:T(8,128)(2,1)S(1)} async-done(((bf16[8,16,1792]{2,1,0:T(8,128)(2,1)}), bf16[8,16,1792]{2,1,0:T(8,128)(2,1)S(1)}, u32[]{:S(2)}, u32[]{:S(2)}) %all-to-all-start.3) | async-done | bytes 458784 | tf_op jit(solution)/shard_map/all_to_all | solution.py:49
  116.2 2.7 %fusion.35 = bf16[128,1024]{1,0:T(8,128)(2,1)S(1)} fusion(bf16[128,1792]{1,0:T(8,128)(2,1)S(1)} %bitcast.91, bf16[1,1792,1024]{2,1,0:T(8,128)(2,1)} %param.12), kind=kOutput, calls=%fused_computation.32 | convolution fusion | flops 469893120 | bytes 4390912 | tf_op jit(solution)/shard_map/dot_general | solution.py:68
  118.9 0.9 pad_maximum_fusion
  119.9 25.7 %reduce-scatter.2.cloned.1.call-done = bf16[32,3072]{1,0:T(8,128)(2,1)} async-done(((bf16[128,3072]{1,0:T(8,128)(2,1)}), bf16[32,3072]{1,0:T(8,128)(2,1)}) %reduce-scatter.2.cloned.1.call-update) | async-done | bytes 196624 | tf_op jit(solution)/shard_map/reduce_scatter | solution.py:63
  145.6 1.0 convert_element_type.62
  146.6 9.1 %all_gather.10 = bf16[128,1024]{1,0:T(8,128)(2,1)S(1)} all-gather(bf16[32,1024]{1,0:T(8,128)(2,1)S(1)} %get-tuple-element.5), channel_id=1, replica_groups=mesh['dp'=4,'expert'=8] {'dp'}, dimensions={0}, use_global_device_ids=true | all-gather | bytes 327680 | tf_op jit(solution)/shard_map/all_gather | solution.py:88
  155.7 8.4 %all_gather.9 = bf16[128,1024]{1,0:T(8,128)(2,1)S(1)} all-gather(bf16[32,1024]{1,0:T(8,128)(2,1)S(1)} %get-tuple-element.6), channel_id=1, replica_groups=mesh['dp'=4,'expert'=8] {'dp'}, dimensions={0}, use_global_device_ids=true | all-gather | bytes 327680 | tf_op jit(solution)/shard_map/all_gather | solution.py:87
  164.1 9.0 %all_gather.11 = bf16[128,1024]{1,0:T(8,128)(2,1)S(1)} all-gather(bf16[32,1024]{1,0:T(8,128)(2,1)S(1)} %get-tuple-element.7), channel_id=1, replica_groups=mesh['dp'=4,'expert'=8] {'dp'}, dimensions={0}, use_global_device_ids=true | all-gather | bytes 327680 | tf_op jit(solution)/shard_map/all_gather | solution.py:89
  173.2 3.4 %fusion.21 = bf16[128,1792]{1,0:T(8,128)(2,1)S(1)} fusion(bf16[128,1024]{1,0:T(8,128)(2,1)S(1)} %all_gather.9, bf16[1,1792,1024]{2,1,0:T(8,128)(2,1)} %param.12), kind=kOutput, calls=%fused_computation.26 | convolution fusion | flops 469991424 | bytes 4390912 | tf_op jit(solution)/shard_map/dot_general | solution.py:10
  176.5 0.9 copy.80
  177.4 3.5 %all-to-all-start.4 = ((bf16[8,16,1792]{2,0,1:T(8,128)(2,1)}), bf16[8,16,1792]{2,0,1:T(8,128)(2,1)S(1)}, u32[]{:S(2)}, u32[]{:S(2)}) async-start(bf16[8,16,1792]{2,0,1:T(8,128)(2,1)} %copy.80), calls=%async_computation.5 | async-start | bytes 917504 | tf_op jit(solution)/shard_map/all_to_all | solution.py:105
  180.9 3.5 %fusion.7 = f32[128,1792]{1,0:T(8,128)S(1)} fusion(bf16[128,1024]{1,0:T(8,128)(2,1)S(1)} %all_gather.11, bf16[1,1792,1024]{2,1,0:T(8,128)(2,1)} %param.11), kind=kOutput, calls=%fused_computation.14 | convolution fusion | flops 469762048 | bytes 4849664 | tf_op jit(solution)/shard_map/dot_general | solution.py:10
  184.5 1.4 fusion.24
  185.8 0.9 copy.84
  186.7 0.6 all-to-all-done.4
  187.4 3.5 %all-to-all-start.6 = ((bf16[8,16,1792]{2,0,1:T(8,128)(2,1)}), bf16[8,16,1792]{2,0,1:T(8,128)(2,1)S(1)}, u32[]{:S(2)}, u32[]{:S(2)}) async-start(bf16[8,16,1792]{2,0,1:T(8,128)(2,1)} %copy.84), calls=%async_computation.7 | async-start | bytes 917504 | tf_op jit(solution)/shard_map/all_to_all | solution.py:112
  191.2 0.9 reshape.50
  192.2 4.9 %all-to-all-done.6 = bf16[8,16,1792]{2,0,1:T(8,128)(2,1)S(1)} async-done(((bf16[8,16,1792]{2,0,1:T(8,128)(2,1)}), bf16[8,16,1792]{2,0,1:T(8,128)(2,1)S(1)}, u32[]{:S(2)}, u32[]{:S(2)}) %all-to-all-start.6) | async-done | bytes 458784 | tf_op jit(solution)/shard_map/all_to_all | solution.py:112
  197.1 4.6 %all-to-all-start.5 = ((bf16[8,4,7168]{2,1,0:T(4,128)(2,1)}), bf16[8,4,7168]{2,1,0:T(4,128)(2,1)S(1)}, u32[]{:S(2)}, u32[]{:S(2)}) async-start(bf16[8,4,7168]{2,1,0:T(4,128)(2,1)} %reshape.50), calls=%async_computation.6 | async-start | bytes 917504 | tf_op jit(solution)/shard_map/all_to_all | solution.py:104
  201.7 0.4 copy.85
  202.1 0.9 all_to_all.82
  203.0 12.6 %all-to-all-done.5 = bf16[8,4,7168]{2,1,0:T(4,128)(2,1)S(1)} async-done(((bf16[8,4,7168]{2,1,0:T(4,128)(2,1)}), bf16[8,4,7168]{2,1,0:T(4,128)(2,1)S(1)}, u32[]{:S(2)}, u32[]{:S(2)}) %all-to-all-start.5) | async-done | bytes 458784 | tf_op jit(solution)/shard_map/all_to_all | solution.py:104
  215.7 4.1 %all-to-all-start.7 = ((bf16[8,4,7168]{2,1,0:T(4,128)(2,1)}), bf16[8,4,7168]{2,1,0:T(4,128)(2,1)}, u32[]{:S(2)}, u32[]{:S(2)}) async-start(bf16[8,4,7168]{2,1,0:T(4,128)(2,1)} %all_to_all.82), calls=%async_computation.8 | async-start | bytes 917504 | tf_op jit(solution)/shard_map/all_to_all | solution.py:111
  219.8 3.0 %fusion.17 = bf16[1,1792,1024]{2,1,0:T(8,128)(2,1)} fusion(bf16[128,1792]{1,0:T(8,128)(2,1)S(1)} %bitcast.92, bf16[128,1024]{1,0:T(8,128)(2,1)S(1)} %all_gather.9), kind=kOutput, calls=%fused_computation.24 | convolution fusion | flops 471597056 | bytes 4390912 | tf_op jit(solution)/shard_map/dot_general | solution.py:16
  222.8 3.0 %fusion.15 = bf16[1,1792,1024]{2,1,0:T(8,128)(2,1)} fusion(bf16[128,1792]{1,0:T(8,128)(2,1)S(1)} %bitcast.89, bf16[128,1024]{1,0:T(8,128)(2,1)S(1)} %all_gather.10), kind=kOutput, calls=%fused_computation.22 | convolution fusion | flops 471597056 | bytes 4390912 | tf_op jit(solution)/shard_map/dot_general | solution.py:16
  225.7 3.0 %fusion.16 = bf16[1,1792,1024]{2,1,0:T(8,128)(2,1)} fusion(bf16[128,1792]{1,0:T(8,128)(2,1)S(1)} %bitcast.90, bf16[128,1024]{1,0:T(8,128)(2,1)S(1)} %all_gather.11), kind=kOutput, calls=%fused_computation.23 | convolution fusion | flops 471597056 | bytes 4390912 | tf_op jit(solution)/shard_map/dot_general | solution.py:16
  228.7 2.9 %fusion = bf16[128,7168]{1,0:T(8,128)(2,1)} fusion(bf16[8,4,7168]{2,1,0:T(4,128)(2,1)S(1)} %all-to-all-done.5, f32[8,4]{0,1:T(4,128)S(1)} %select_reduce_fusion.1, s32[128,8]{0,1:T(8,128)S(1)} %copy.71, pred[128,8]{0,1:T(8,128)(4,1)S(1)} %copy.70), kind=kOutput, calls=%fused_computation.2 | convolution fusion | flops 353705984 | bytes 2299008 | tf_op jit(solution)/shard_map/tjc,jcd->td/dot_general | solution.py:122
  231.7 2.1 all-to-all-done.7
  233.7 2.9 %fusion.1 = bf16[128,7168]{1,0:T(8,128)(2,1)} fusion(bf16[8,4,7168]{2,1,0:T(4,128)(2,1)} %all-to-all-done.7, s32[128,8]{0,1:T(8,128)S(1)} %copy.71, pred[128,8]{0,1:T(8,128)(4,1)S(1)} %copy.70), kind=kOutput, calls=%fused_computation.3 | convolution fusion | flops 59645952 | bytes 2298880 | tf_op jit(solution)/shard_map/tjc,jcd->td/dot_general | solution.py:125
  (29 shorter events, 1.6 us)
Async XLA Ops:
  7.2 1.5 copy-start
  16.3 15.4 %copy-start.5 = (s32[128,8]{0,1:T(8,128)S(1)}, s32[128,8]{0,1:T(8,128)}, u32[]{:S(2)}) copy-start(s32[128,8]{0,1:T(8,128)} %param.8) | copy-start | bytes 12292
  16.3 15.4 %copy-start.6 = (f32[128,8]{0,1:T(8,128)S(1)}, f32[128,8]{0,1:T(8,128)}, u32[]{:S(2)}) copy-start(f32[128,8]{0,1:T(8,128)} %param.9) | copy-start | bytes 12292
  16.3 15.5 %copy-start.4 = (bf16[128,7168]{1,0:T(8,128)(2,1)S(1)}, bf16[128,7168]{1,0:T(8,128)(2,1)}, u32[]{:S(2)}) copy-start(bf16[128,7168]{1,0:T(8,128)(2,1)} %param.13) | copy-start | bytes 5505028
  26.5 23.0 %all-to-all-start = ((bf16[4,2,28672]{2,1,0:T(2,128)(2,1)}), bf16[4,2,28672]{2,1,0:T(2,128)(2,1)S(1)}, u32[]{:S(2)}, u32[]{:S(2)}) async-start(bf16[4,2,28672]{2,1,0:T(2,128)(2,1)} %reshape.53), calls=%async_computation | async-start | bytes 917504 | tf_op jit(solution)/shard_map/all_to_all | solution.py:43
  49.5 23.5 %all-to-all-start.2 = ((bf16[4,2,28672]{2,1,0:T(2,128)(2,1)}), bf16[4,2,28672]{2,1,0:T(2,128)(2,1)S(1)}, u32[]{:S(2)}, u32[]{:S(2)}) async-start(bf16[4,2,28672]{2,1,0:T(2,128)(2,1)} %reshape.51), calls=%async_computation.2 | async-start | bytes 917504 | tf_op jit(solution)/shard_map/all_to_all | solution.py:50
  73.0 24.2 %all-to-all-start.1 = ((bf16[8,16,1792]{2,1,0:T(8,128)(2,1)}), bf16[8,16,1792]{2,1,0:T(8,128)(2,1)S(1)}, u32[]{:S(2)}, u32[]{:S(2)}) async-start(bf16[8,16,1792]{2,1,0:T(8,128)(2,1)} %copy.75), calls=%async_computation.1 | async-start | bytes 917504 | tf_op jit(solution)/shard_map/all_to_all | solution.py:42
  97.2 19.0 %all-to-all-start.3 = ((bf16[8,16,1792]{2,1,0:T(8,128)(2,1)}), bf16[8,16,1792]{2,1,0:T(8,128)(2,1)S(1)}, u32[]{:S(2)}, u32[]{:S(2)}) async-start(bf16[8,16,1792]{2,1,0:T(8,128)(2,1)} %copy.79), calls=%async_computation.3 | async-start | bytes 917504 | tf_op jit(solution)/shard_map/all_to_all | solution.py:49
  102.3 43.3 %reduce-scatter.2.cloned.1.call-start = ((), (), s32[]{:S(2)}) async-start(), calls=%async_computation.9 | async-start | bytes 983040 | tf_op jit(solution)/shard_map/reduce_scatter | solution.py:63
  102.3 3.1 %copy-start.2 = (bf16[1,1792,1024]{2,1,0:T(8,128)(2,1)S(1)}, bf16[1,1792,1024]{2,1,0:T(8,128)(2,1)}, u32[]{:S(2)}) copy-start(bf16[1,1792,1024]{2,1,0:T(8,128)(2,1)} %param.10) | copy-start | bytes 11010052
  177.4 9.9 %all-to-all-start.4 = ((bf16[8,16,1792]{2,0,1:T(8,128)(2,1)}), bf16[8,16,1792]{2,0,1:T(8,128)(2,1)S(1)}, u32[]{:S(2)}, u32[]{:S(2)}) async-start(bf16[8,16,1792]{2,0,1:T(8,128)(2,1)} %copy.80), calls=%async_computation.5 | async-start | bytes 917504 | tf_op jit(solution)/shard_map/all_to_all | solution.py:105
  180.9 3.5 %copy-start.3 = (bf16[1,1792,1024]{2,1,0:T(8,128)(2,1)S(1)}, bf16[1,1792,1024]{2,1,0:T(8,128)(2,1)}, u32[]{:S(2)}) copy-start(bf16[1,1792,1024]{2,1,0:T(8,128)(2,1)} %param.10) | copy-start | bytes 11010052
  187.4 9.8 %all-to-all-start.6 = ((bf16[8,16,1792]{2,0,1:T(8,128)(2,1)}), bf16[8,16,1792]{2,0,1:T(8,128)(2,1)S(1)}, u32[]{:S(2)}, u32[]{:S(2)}) async-start(bf16[8,16,1792]{2,0,1:T(8,128)(2,1)} %copy.84), calls=%async_computation.7 | async-start | bytes 917504 | tf_op jit(solution)/shard_map/all_to_all | solution.py:112
  197.1 18.5 %all-to-all-start.5 = ((bf16[8,4,7168]{2,1,0:T(4,128)(2,1)}), bf16[8,4,7168]{2,1,0:T(4,128)(2,1)S(1)}, u32[]{:S(2)}, u32[]{:S(2)}) async-start(bf16[8,4,7168]{2,1,0:T(4,128)(2,1)} %reshape.50), calls=%async_computation.6 | async-start | bytes 917504 | tf_op jit(solution)/shard_map/all_to_all | solution.py:104
  215.7 18.1 %all-to-all-start.7 = ((bf16[8,4,7168]{2,1,0:T(4,128)(2,1)}), bf16[8,4,7168]{2,1,0:T(4,128)(2,1)}, u32[]{:S(2)}, u32[]{:S(2)}) async-start(bf16[8,4,7168]{2,1,0:T(4,128)(2,1)} %all_to_all.82), calls=%async_computation.8 | async-start | bytes 917504 | tf_op jit(solution)/shard_map/all_to_all | solution.py:111
  222.8 13.9 %copy-start.1 = (bf16[128,7168]{1,0:T(8,128)(2,1)S(1)}, bf16[128,7168]{1,0:T(8,128)(2,1)}, u32[]{:S(2)}) copy-start(bf16[128,7168]{1,0:T(8,128)(2,1)} %param.7) | copy-start | bytes 5505028
Sparse Core Ops, SparseCore 0:
  120.0 25.5 reduce-scatter.1
where the time goes:
time: 245 us; the launch traced here: 243 us
  local copies, waits for them, and re-layouts  78.5 us (32%)
  waiting for transfers between devices  56.1 us (23%)
  starting transfers between devices  35.1 us (14%)
  matrix products  29.9 us (12%)
  blocking collectives  26.5 us (11%)
  between operations  14.2 us (6%)
  other arithmetic  3.11 us (1%)
    unnamed x18, local copies, waits for them, and re-layouts  40.4 us
    reduce_scatter x1, waiting for transfers between devices, body(): lax.psum_scatter(jnp.concatenate([jnp.dot(row_block, gate_mat, preferred_...  25.7 us
    all_to_all x1, waiting for transfers between devices, body(): lax.all_to_all(lax.all_to_all(out_rows.reshape(layout), 'dp', split_axis=...  12.6 us
    all_to_all x1, waiting for transfers between devices, body(): lax.all_to_all(lax.all_to_all(send_grads, 'dp', split_axis=2, concat_axis...  10.1 us
    all_to_all x2, local copies, waits for them, and re-layouts, body(): lax.all_to_all(send_grads, 'dp', split_axis=2, concat_axis=1, tiled=True)  9.54 us
    all_to_all x2, local copies, waits for them, and re-layouts, body(): lax.all_to_all(send_rows, 'dp', split_axis=2, concat_axis=1, tiled=True)  9.54 us
    all_gather x1, blocking collectives, body(): gate_part = lax.all_gather(gate_grad, 'dp', axis=0, tiled=True)  9.05 us
    all_gather x1, blocking collectives, body(): up_part = lax.all_gather(up_grad, 'dp', axis=0, tiled=True)  9.04 us
  transfers between devices with their start and end apart: 9, of which 6 were waited for; matrix products, arithmetic and copies ran while one was open for 33% of the time, Pallas kernels for 0%

commit v1 on v0

v1 whole, which is shorter than its diff:
```python
import functools

import jax
import jax.numpy as jnp
from jax import lax
from jax.experimental import pallas as pl
from jax.experimental.pallas import tpu as pltpu
from jax.sharding import PartitionSpec as P

CAP = 4
LANES = 128
F32 = jnp.float32
BF16 = jnp.bfloat16


def mm(left, right, left_dim=1, right_dim=0):
    return lax.dot_general(
        left, right, (((left_dim,), (right_dim,)), ((), ())), preferred_element_type=F32
    )


def iota(shape, dim):
    return lax.broadcasted_iota(jnp.int32, shape, dim)


def slots_of(ids, gates, experts):
    count = ids.shape[1]
    hit = ids < experts
    expert = jnp.sum(jnp.where(hit, ids, 0), axis=0, keepdims=True)
    held = jnp.max(jnp.where(hit, 1, 0), axis=0, keepdims=True) > 0
    gate = jnp.sum(jnp.where(hit, gates, 0.0), axis=0, keepdims=True)
    chosen = (iota((experts, count), 0) == expert) & held
    before = (iota((count, count), 0) < iota((count, count), 1)).astype(F32).astype(BF16)
    ranks = mm(chosen.astype(F32).astype(BF16), before)
    rank = jnp.sum(jnp.where(chosen, ranks, 0.0), axis=0, keepdims=True).astype(jnp.int32)
    slot = jnp.where(held, expert * (2 * CAP) + rank, -2 * CAP)
    rows = iota((experts * 2 * CAP, count), 0)
    row_hot = rows == slot
    grad_hot = rows == slot + CAP
    row_gate = jnp.sum(jnp.where(row_hot, gate, 0.0), axis=1, keepdims=True)
    grad_gate = jnp.sum(jnp.where(grad_hot, gate, 0.0), axis=1, keepdims=True)
    return row_hot.astype(F32).astype(BF16), grad_hot.astype(F32).astype(BF16), row_gate, grad_gate


def fill_rows(row_hot, grad_hot, grad_gate, tokens, cotangent):
    return (mm(row_hot, tokens) + grad_gate * mm(grad_hot, cotangent)).astype(BF16)


def combine(row_hot, grad_hot, row_gate, got):
    wide = got.astype(F32)
    is_row = iota(row_gate.shape, 0) % (2 * CAP) < CAP
    weighted = jnp.where(is_row, row_gate * wide, wide).astype(BF16)
    return mm(row_hot, weighted, 0, 0).astype(BF16), mm(grad_hot, weighted, 0, 0).astype(BF16)


def pickers(count):
    row = iota((count, 2 * count), 0)
    at = row // CAP * (2 * CAP) + row % CAP
    column = iota((count, 2 * count), 1)
    return (column == at).astype(F32).astype(BF16), (column == at + CAP).astype(F32).astype(BF16)


def nonlinear(partials, hidden):
    total = functools.reduce(lambda a, b: a + b, [part.astype(F32) for part in partials])
    pre_gate = total[:, :hidden]
    pre_up = total[:, hidden : 2 * hidden]
    hidden_grad = total[:, 2 * hidden :]
    squash = jax.nn.sigmoid(pre_gate)
    silu_gate = pre_gate * squash
    gate_grad = hidden_grad * pre_up * squash * (1.0 + pre_gate * (1.0 - squash))
    return jnp.concatenate(
        [
            gate_grad.astype(BF16),
            (hidden_grad * silu_gate).astype(BF16),
            (silu_gate * pre_up).astype(BF16),
        ],
        axis=1,
    )


def prep_kernel(experts, ids, gates, tokens, cotangent, out):
    row_hot, grad_hot, _, grad_gate = slots_of(ids[...], gates[...], experts)
    out[...] = fill_rows(row_hot, grad_hot, grad_gate, tokens[...], cotangent[...])


def prep(ids, gates, tokens, cotangent, experts, parts):
    count, width = tokens.shape
    piece = width // parts
    rows = experts * 2 * CAP
    if piece % LANES:
        row_hot, grad_hot, _, grad_gate = slots_of(ids, gates, experts)
        full = fill_rows(row_hot, grad_hot, grad_gate, tokens, cotangent)
        return full.reshape(rows, parts, piece).transpose(1, 0, 2)
    return pl.pallas_call(
        functools.partial(prep_kernel, experts),
        out_shape=jax.ShapeDtypeStruct((parts, rows, piece), BF16),
        grid=(parts,),
        in_specs=[
            pl.BlockSpec(ids.shape, lambda p: (0, 0)),
            pl.BlockSpec(gates.shape, lambda p: (0, 0)),
            pl.BlockSpec((count, piece), lambda p: (0, p)),
            pl.BlockSpec((count, piece), lambda p: (0, p)),
        ],
        out_specs=pl.BlockSpec((None, rows, piece), lambda p: (p, 0, 0)),
        name="prep",
    )(ids, gates, tokens, cotangent)


def finish_kernel(experts, ids, gates, got, out, grad):
    row_hot, grad_hot, row_gate, _ = slots_of(ids[...], gates[...], experts)
    out[...], grad[...] = combine(row_hot, grad_hot, row_gate, got[...])


def finish(ids, gates, got, experts):
    parts, rows, piece = got.shape
    count = ids.shape[1]
    if piece % LANES:
        row_hot, grad_hot, row_gate, _ = slots_of(ids, gates, experts)
        return combine(row_hot, grad_hot, row_gate, got.transpose(1, 0, 2).reshape(rows, parts * piece))
    shape = jax.ShapeDtypeStruct((count, parts * piece), BF16)
    spec = pl.BlockSpec((count, piece), lambda p: (0, p))
    return pl.pallas_call(
        functools.partial(finish_kernel, experts),
        out_shape=(shape, shape),
        grid=(parts,),
        in_specs=[
            pl.BlockSpec(ids.shape, lambda p: (0, 0)),
            pl.BlockSpec(gates.shape, lambda p: (0, 0)),
            pl.BlockSpec((None, rows, piece), lambda p: (p, 0, 0)),
        ],
        out_specs=(spec, spec),
        name="finish",
    )(ids, gates, got)


def forward_kernel(got, gate, up, down, pre_gate, pre_up, hidden_grad, rows, grads):
    @pl.when(pl.program_id(0) == 0)
    def _():
        pick_row, pick_grad = pickers(rows.shape[0])
        block = got[...]
        rows[...] = mm(pick_row, block).astype(BF16)
        grads[...] = mm(pick_grad, block).astype(BF16)

    pre_gate[...] = mm(rows[...], gate[...]).astype(BF16)
    pre_up[...] = mm(rows[...], up[...]).astype(BF16)
    hidden_grad[...] = mm(grads[...], down[...]).astype(BF16)


def forward(got, gate, up, down):
    total, piece = got.shape
    count = total // 2
    hidden = gate.shape[1]
    if piece % LANES:
        pick_row, pick_grad = pickers(count)
        rows = mm(pick_row, got).astype(BF16)
        grads = mm(pick_grad, got).astype(BF16)
        pre = jnp.concatenate([mm(rows, gate), mm(rows, up), mm(grads, down)], axis=1)
        return pre.astype(BF16), rows, grads
    step = 256
    weight = pl.BlockSpec((piece, step), lambda n: (0, n))
    kept = pl.BlockSpec((count, piece), lambda n: (0, 0))
    shape = jax.ShapeDtypeStruct((count, hidden), BF16)
    part = pl.BlockSpec((count, step), lambda n: (0, n))
    pre_gate, pre_up, hidden_grad, rows, grads = pl.pallas_call(
        forward_kernel,
        out_shape=(shape, shape, shape)
        + (jax.ShapeDtypeStruct((count, piece), BF16),) * 2,
        grid=(hidden // step,),
        in_specs=[pl.BlockSpec((total, piece), lambda n: (0, 0)), weight, weight, weight],
        out_specs=(part, part, part, kept, kept),
        name="forward",
    )(got, gate, up, down)
    return jnp.concatenate([pre_gate, pre_up, hidden_grad], axis=1), rows, grads


def middle_kernel(hidden, partials, out):
    out[...] = nonlinear([partials[k] for k in range(partials.shape[0])], hidden)


def middle(partials, hidden):
    _, rows, width = partials.shape
    return pl.pallas_call(
        functools.partial(middle_kernel, hidden),
        out_shape=jax.ShapeDtypeStruct((rows, width), BF16),
        name="middle",
    )(partials)


def backward_rows(acts, gate, up, down):
    hidden = gate.shape[1]
    out = mm(acts[:, 2 * hidden :], down, 1, 1).astype(BF16)
    back = (mm(acts[:, :hidden], gate, 1, 1) + mm(acts[:, hidden : 2 * hidden], up, 1, 1)).astype(BF16)
    pick_row, pick_grad = pickers(acts.shape[0])
    return (mm(pick_row, out, 0, 0) + mm(pick_grad, back, 0, 0)).astype(BF16)


def backward_kernel(acts, gate, up, down, out):
    out[...] = backward_rows(acts[...], gate[...], up[...], down[...])


def backward(acts, gate, up, down):
    count, width = acts.shape
    piece, hidden = gate.shape
    if piece % LANES:
        return backward_rows(acts, gate, up, down)
    step = 256
    weight = pl.BlockSpec((step, hidden), lambda d: (d, 0))
    return pl.pallas_call(
        backward_kernel,
        out_shape=jax.ShapeDtypeStruct((2 * count, piece), BF16),
        grid=(piece // step,),
        in_specs=[pl.BlockSpec((count, width), lambda d: (0, 0)), weight, weight, weight],
        out_specs=pl.BlockSpec((2 * count, step), lambda d: (0, d)),
        name="backward",
    )(acts, gate, up, down)


def weights_kernel(rows, grads, acts, gate, up, down):
    hidden = gate.shape[1]
    gate[...] = mm(rows[...], acts[:, :hidden], 0, 0).astype(BF16)
    up[...] = mm(rows[...], acts[:, hidden : 2 * hidden], 0, 0).astype(BF16)
    down[...] = mm(grads[...], acts[:, 2 * hidden :], 0, 0).astype(BF16)


def weights(rows, grads, acts, hidden):
    count, piece = rows.shape
    if piece % LANES:
        return (
            mm(rows, acts[:, :hidden], 0, 0).astype(BF16),
            mm(rows, acts[:, hidden : 2 * hidden], 0, 0).astype(BF16),
            mm(grads, acts[:, 2 * hidden :], 0, 0).astype(BF16),
        )
    step = 256
    shape = jax.ShapeDtypeStruct((piece, hidden), BF16)
    spec = pl.BlockSpec((step, hidden), lambda d: (d, 0))
    kept = pl.BlockSpec((count, step), lambda d: (0, d))
    return pl.pallas_call(
        weights_kernel,
        out_shape=(shape, shape, shape),
        grid=(piece // step,),
        in_specs=[kept, kept, pl.BlockSpec(acts.shape, lambda d: (0, 0))],
        out_specs=(spec, spec, spec),
        name="weights",
    )(rows, grads, acts)


def body(tokens, route_ids, gate_weights, gate_weight, up_weight, down_weight, cotangent):
    experts = lax.axis_size("expert")
    parts = lax.axis_size("dp")
    both = ("dp", "expert")
    gate, up, down = gate_weight[0], up_weight[0], down_weight[0]
    piece, hidden = gate.shape
    ids, gates = route_ids.T, gate_weights.T
    block = 2 * CAP

    sent = prep(ids, gates, tokens, cotangent, experts, parts)
    sent = sent.reshape(parts * experts, block, piece)
    got = lax.all_to_all(sent, both, 0, 0, tiled=True)
    pre, rows, grads = forward(got.reshape(parts * experts * block, piece), gate, up, down)
    mine = lax.all_to_all(pre.reshape(parts, experts * CAP, 3 * hidden), "dp", 0, 0, tiled=True)
    acts = lax.all_gather(middle(mine, hidden), "dp", axis=0, tiled=True)
    back = backward(acts, gate, up, down)
    back = lax.all_to_all(back.reshape(parts * experts, block, piece), both, 0, 0, tiled=True)
    totals = weights(rows, grads, acts, hidden)
    output, grad_tokens = finish(ids, gates, back.reshape(parts, experts * block, piece), experts)
    return (output, grad_tokens) + tuple(total[None] for total in totals)


def solution(mesh):
    rows = P(("dp", "expert"), None)
    held = P("expert", "dp", None)
    return jax.shard_map(
        body,
        mesh=mesh,
        in_specs=(rows, rows, rows, held, held, held, rows),
        out_specs=(rows, rows, held, held, held),
        check_vma=False,
    )
```

time: 245 us -> 119 us (0.49)
  local copies, waits for them, and re-layouts: 78.5 us -> 0.94 us
  waiting for transfers between devices: 56.1 us -> 17.1 us
  Pallas kernels: 0 us -> 37.1 us
  starting transfers between devices: 35.1 us -> 2.64 us
  blocking collectives: 26.5 us -> 58.5 us
  matrix products: 29.9 us -> 0 us
  between operations: 14.2 us -> 0.65 us
    all_to_all x0 -> x2, blocking collectives: none -> 46.7 us  [the longest x1 32.1 us: body(): got = lax.all_to_all(sent, both, 0, 0, tiled=True)]
    unnamed x18 -> x2, local copies, waits for them, and re-layouts: 40.4 us -> 0.94 us
    pallas_call x0 -> x6, Pallas kernels: none -> 37.1 us  [the longest x1 10.7 us: backward(): pl.pallas_call(backward_kernel, out_shape=jax.ShapeDtypeStruct((2 * count...]
    all_to_all x8 -> x1, starting transfers between devices: 35.1 us -> 2.64 us  [body(): lax.all_to_all(back.reshape(parts * experts, block, piece), both, 0, 0, t...]
    dot_general x13 -> x0, matrix products: 29.9 us -> none  [the longest x3 8.94 us: contract_first(): lax.dot_general(left, right, (((0,), (0,)), ((), ())), preferred_element_...]
    reduce_scatter x1 -> x0, waiting for transfers between devices: 25.7 us -> none  [body(): lax.psum_scatter(jnp.concatenate([jnp.dot(row_block, gate_mat, preferred_...]
    all_to_all x8 -> x0, local copies, waits for them, and re-layouts: 21.7 us -> none  [the longest x2 9.54 us: body(): lax.all_to_all(send_grads, 'dp', split_axis=2, concat_axis=1, tiled=True)]
    all_gather x3 -> x1, blocking collectives: 26.5 us -> 11.8 us  [body(): acts = lax.all_gather(middle(mine, hidden), 'dp', axis=0, tiled=True)]
  transfers between devices with their start and end apart: 9 -> 1, of which waited for: 6 -> 1; matrix products, arithmetic and copies ran while one was open for 33% -> 0% of each run, Pallas kernels for 0% -> 6%
where the time goes in v1:
time: 119 us; the launch traced here: 118 us
  blocking collectives  58.5 us (49%)
  Pallas kernels  37.1 us (31%)
  waiting for transfers between devices  17.1 us (14%)
  starting transfers between devices  2.64 us (2%)
    all_to_all x1, blocking collectives, body(): got = lax.all_to_all(sent, both, 0, 0, tiled=True)  32.1 us
    all_to_all x1, waiting for transfers between devices, body(): lax.all_to_all(back.reshape(parts * experts, block, piece), both, 0, 0, t...  17.1 us
    all_to_all x1, blocking collectives, body(): lax.all_to_all(pre.reshape(parts, experts * CAP, 3 * hidden), 'dp', 0, 0,...  14.6 us
    all_gather x1, blocking collectives, body(): acts = lax.all_gather(middle(mine, hidden), 'dp', axis=0, tiled=True)  11.8 us
    pallas_call x1, Pallas kernels, backward(): pl.pallas_call(backward_kernel, out_shape=jax.ShapeDtypeStruct((2 * count...  10.7 us
    pallas_call x1, Pallas kernels, weights(): pl.pallas_call(weights_kernel, out_shape=(shape, shape, shape), grid=(pie...  7.57 us
    pallas_call x1, Pallas kernels, forward(): pl.pallas_call(forward_kernel, out_shape=(shape, shape, shape) + (jax.Sha...  7.34 us
    pallas_call x1, Pallas kernels, finish(): pl.pallas_call(functools.partial(finish_kernel, experts), out_shape=(shap...  4.9 us
  transfers between devices with their start and end apart: 1, of which 1 were waited for; matrix products, arithmetic and copies ran while one was open for 0% of the time, Pallas kernels for 6%

profile of v1, /device:TPU:0, one launch (start us, length us, event | category | flops | bytes accessed | tf_op | source)
XLA Modules:
  0.0 118.1 jit_solution(7463701249683472338)
XLA Ops:
  0.6 4.6 %prep.1 = bf16[4,64,1792]{2,1,0:T(8,128)(2,1)} custom-call(s32[8,128]{1,0:T(8,128)} %bitcast.24, f32[8,128]{1,0:T(8,128)} %bitcast.26, bf16[128,7168]{1,0:T(8,128)(2,1)} %tokens.1, bf16[128,7168]{1,0:T(8,128)(2,1)} %cotangent.1), custom_call_target="tpu_custom_call" | custom-call | tf_op jit(solution)/shard_map/prep/pallas_call | solution.py:94
  5.2 32.1 %all_to_all.15 = bf16[32,8,1792]{2,1,0:T(8,128)(2,1)} all-to-all(bf16[32,8,1792]{2,1,0:T(8,128)(2,1)} %bitcast.22), channel_id=1, replica_groups=mesh['dp'=4,'expert'=8] {'dp','expert'}, dimensions={0} | all-to-all | bytes 1835008 | tf_op jit(solution)/shard_map/all_to_all | solution.py:258
  37.3 7.3 %forward.1 = (bf16[128,1024]{1,0:T(8,128)(2,1)}, bf16[128,1024]{1,0:T(8,128)(2,1)}, bf16[128,1024]{1,0:T(8,128)(2,1)}, bf16[128,1792]{1,0:T(8,128)(2,1)}, bf16[128,1792]{1,0:T(8,128)(2,1)}) custom-call(bf16[256,1792]{1,0:T(8,128)(2,1)} %bitcast.20, bf16[1792,1024]{1,0:T(8,128)(2,1)} %bitcast.13, bf16[1792,1024]{1,0:T(8,128)(2,1)} %bitcast.15, ...), custom_call_target="tpu_custom_call" | custom-call | tf_op jit(solution)/shard_map/forward/pallas_call | solution.py:164
  44.7 1.2 pad_maximum_fusion
  45.8 14.6 %all_to_all.16.partials = bf16[4,32,3072]{2,1,0:T(8,128)(2,1)} all-to-all(bf16[4,32,3072]{2,1,0:T(8,128)(2,1)S(1)} %bitcast.23), channel_id=1, replica_groups=mesh['dp'=4,'expert'=8] {'dp'}, dimensions={0} | all-to-all | bytes 1572864 | tf_op jit(solution)/shard_map/all_to_all | solution.py:260
  60.5 2.0 %middle.1 = bf16[32,3072]{1,0:T(8,128)(2,1)} custom-call(bf16[4,32,3072]{2,1,0:T(8,128)(2,1)} %all_to_all.16.partials), custom_call_target="tpu_custom_call" | custom-call | tf_op jit(solution)/shard_map/middle/pallas_call | solution.py:182
  62.4 11.8 %all_gather.3.acts = bf16[128,3072]{1,0:T(8,128)(2,1)} all-gather(bf16[32,3072]{1,0:T(8,128)(2,1)} %middle.1), channel_id=1, replica_groups=mesh['dp'=4,'expert'=8] {'dp'}, dimensions={0}, use_global_device_ids=true | all-gather | bytes 983040 | tf_op jit(solution)/shard_map/all_gather | solution.py:261
  74.2 10.7 %backward.1 = bf16[256,1792]{1,0:T(8,128)(2,1)} custom-call(bf16[128,3072]{1,0:T(8,128)(2,1)} %all_gather.3.acts, bf16[1792,1024]{1,0:T(8,128)(2,1)} %bitcast.14, bf16[1792,1024]{1,0:T(8,128)(2,1)} %bitcast.16, bf16[1792,1024]{1,0:T(8,128)(2,1)} %bitcast.18), custom_call_target="tpu_custom_call" | custom-call | tf_op jit(solution)/shard_map/backward/pallas_call | solution.py:208
  84.9 2.6 %all-to-all-start.2 = ((bf16[32,8,1792]{2,1,0:T(8,128)(2,1)}), bf16[32,8,1792]{2,1,0:T(8,128)(2,1)S(1)}, u32[]{:S(2)}, u32[]{:S(2)}) async-start(bf16[32,8,1792]{2,1,0:T(8,128)(2,1)} %bitcast.19), calls=%async_computation.2 | async-start | bytes 1835008 | tf_op jit(solution)/shard_map/all_to_all | solution.py:263
  87.6 7.6 %weights.1 = (bf16[1792,1024]{1,0:T(8,128)(2,1)}, bf16[1792,1024]{1,0:T(8,128)(2,1)}, bf16[1792,1024]{1,0:T(8,128)(2,1)}) custom-call(bf16[128,1792]{1,0:T(8,128)(2,1)} %get-tuple-element.20.rows, bf16[128,1792]{1,0:T(8,128)(2,1)} %get-tuple-element.21.grads, bf16[128,3072]{1,0:T(8,128)(2,1)} %all_gather.3.acts), custom_call_target="tpu_custom_call" | custom-call | tf_op jit(solution)/shard_map/weights/pallas_call | solution.py:237
  95.2 17.1 %all-to-all-done.2 = bf16[32,8,1792]{2,1,0:T(8,128)(2,1)S(1)} async-done(((bf16[32,8,1792]{2,1,0:T(8,128)(2,1)}), bf16[32,8,1792]{2,1,0:T(8,128)(2,1)S(1)}, u32[]{:S(2)}, u32[]{:S(2)}) %all-to-all-start.2) | async-done | bytes 917536 | tf_op jit(solution)/shard_map/all_to_all | solution.py:263
  112.2 0.0 copy-start
  112.2 0.9 copy-done
  113.2 4.9 %finish.1 = (bf16[128,7168]{1,0:T(8,128)(2,1)}, bf16[128,7168]{1,0:T(8,128)(2,1)}) custom-call(s32[8,128]{1,0:T(8,128)} %bitcast.25, f32[8,128]{1,0:T(8,128)} %bitcast.27, bf16[4,64,1792]{2,1,0:T(8,128)(2,1)} %bitcast.21), custom_call_target="tpu_custom_call" | custom-call | tf_op jit(solution)/shard_map/finish/pallas_call | solution.py:122
Async XLA Ops:
  84.9 27.3 %all-to-all-start.2 = ((bf16[32,8,1792]{2,1,0:T(8,128)(2,1)}), bf16[32,8,1792]{2,1,0:T(8,128)(2,1)S(1)}, u32[]{:S(2)}, u32[]{:S(2)}) async-start(bf16[32,8,1792]{2,1,0:T(8,128)(2,1)} %bitcast.19), calls=%async_computation.2 | async-start | bytes 1835008 | tf_op jit(solution)/shard_map/all_to_all | solution.py:263
  112.2 0.9 copy-start

commit v2 on v1

v2 whole, which is shorter than its diff:
```python
import functools

import jax
import jax.numpy as jnp
from jax import lax
from jax.experimental import pallas as pl
from jax.experimental.pallas import tpu as pltpu
from jax.sharding import PartitionSpec as P

CAP = 4
LANES = 128
F32 = jnp.float32
BF16 = jnp.bfloat16


def mm(left, right, left_dim=1, right_dim=0):
    return lax.dot_general(
        left, right, (((left_dim,), (right_dim,)), ((), ())), preferred_element_type=F32
    )


def iota(shape, dim):
    return lax.broadcasted_iota(jnp.int32, shape, dim)


def slots_of(ids, gates, experts):
    count = ids.shape[1]
    hit = ids < experts
    expert = jnp.sum(jnp.where(hit, ids, 0), axis=0, keepdims=True)
    held = jnp.max(jnp.where(hit, 1, 0), axis=0, keepdims=True) > 0
    gate = jnp.sum(jnp.where(hit, gates, 0.0), axis=0, keepdims=True)
    chosen = (iota((experts, count), 0) == expert) & held
    before = (iota((count, count), 0) < iota((count, count), 1)).astype(F32).astype(BF16)
    ranks = mm(chosen.astype(F32).astype(BF16), before)
    rank = jnp.sum(jnp.where(chosen, ranks, 0.0), axis=0, keepdims=True).astype(jnp.int32)
    slot = jnp.where(held, expert * (2 * CAP) + rank, -2 * CAP)
    rows = iota((experts * 2 * CAP, count), 0)
    row_hot = rows == slot
    grad_hot = rows == slot + CAP
    row_gate = jnp.sum(jnp.where(row_hot, gate, 0.0), axis=1, keepdims=True)
    grad_gate = jnp.sum(jnp.where(grad_hot, gate, 0.0), axis=1, keepdims=True)
    return row_hot.astype(F32).astype(BF16), grad_hot.astype(F32).astype(BF16), row_gate, grad_gate


def fill_rows(row_hot, grad_hot, grad_gate, tokens, cotangent):
    return (mm(row_hot, tokens) + grad_gate * mm(grad_hot, cotangent)).astype(BF16)


def combine(row_hot, grad_hot, row_gate, got):
    wide = got.astype(F32)
    is_row = iota(row_gate.shape, 0) % (2 * CAP) < CAP
    weighted = jnp.where(is_row, row_gate * wide, wide).astype(BF16)
    return mm(row_hot, weighted, 0, 0).astype(BF16), mm(grad_hot, weighted, 0, 0).astype(BF16)


def pickers(count):
    row = iota((count, 2 * count), 0)
    at = row // CAP * (2 * CAP) + row % CAP
    column = iota((count, 2 * count), 1)
    return (column == at).astype(F32).astype(BF16), (column == at + CAP).astype(F32).astype(BF16)


def nonlinear(partials, hidden):
    total = functools.reduce(lambda a, b: a + b, [part.astype(F32) for part in partials])
    pre_gate = total[:, :hidden]
    pre_up = total[:, hidden : 2 * hidden]
    hidden_grad = total[:, 2 * hidden :]
    squash = jax.nn.sigmoid(pre_gate)
    silu_gate = pre_gate * squash
    gate_grad = hidden_grad * pre_up * squash * (1.0 + pre_gate * (1.0 - squash))
    return jnp.concatenate(
        [
            gate_grad.astype(BF16),
            (hidden_grad * silu_gate).astype(BF16),
            (silu_gate * pre_up).astype(BF16),
        ],
        axis=1,
    )


ROOM = pltpu.CompilerParams(vmem_limit_bytes=16 * 2**20)
IN_VMEM = pl.BlockSpec(memory_space=pltpu.VMEM)
IN_HBM = pl.BlockSpec(memory_space=pltpu.HBM)
DMA = pltpu.SemaphoreType.DMA


def in_hbm(x):
    return pltpu.with_memory_space_constraint(x, pltpu.HBM)


def like(shape):
    return jax.ShapeDtypeStruct(shape, BF16)


def prep_kernel(experts, ids, gates, tokens, cotangent, out, row_hot, grad_hot, row_gate, held, sems):
    parts, _, piece = out.shape
    copies = [
        [
            pltpu.make_async_copy(
                full.at[:, pl.ds(p * piece, piece)], held.at[k, p], sems.at[k, p]
            )
            for k, full in enumerate((tokens, cotangent))
        ]
        for p in range(parts)
    ]
    for pair in copies:
        for copy in pair:
            copy.start()
    row_hot[...], grad_hot[...], row_gate[...], grad_gate = slots_of(ids[...], gates[...], experts)
    for p, pair in enumerate(copies):
        for copy in pair:
            copy.wait()
        out[p] = fill_rows(row_hot[...], grad_hot[...], grad_gate, held[0, p], held[1, p])


def prep(ids, gates, tokens, cotangent, experts, parts):
    count, width = tokens.shape
    piece = width // parts
    rows = experts * 2 * CAP
    if piece % LANES:
        row_hot, grad_hot, row_gate, grad_gate = slots_of(ids, gates, experts)
        full = fill_rows(row_hot, grad_hot, grad_gate, tokens, cotangent)
        return full.reshape(rows, parts, piece).transpose(1, 0, 2), row_hot, grad_hot, row_gate
    hot = like((rows, count))
    return pl.pallas_call(
        functools.partial(prep_kernel, experts),
        out_shape=(like((parts, rows, piece)), hot, hot, jax.ShapeDtypeStruct((rows, 1), F32)),
        in_specs=[IN_VMEM, IN_VMEM, IN_HBM, IN_HBM],
        out_specs=(IN_VMEM,) * 4,
        scratch_shapes=[pltpu.VMEM((2, parts, count, piece), BF16), DMA((2, parts))],
        compiler_params=ROOM,
        name="prep",
    )(in_hbm(ids), in_hbm(gates), in_hbm(tokens), in_hbm(cotangent))


def finish_kernel(row_hot, grad_hot, row_gate, got, out, grad):
    block = got[pl.program_id(0)]
    out[...], grad[...] = combine(row_hot[...], grad_hot[...], row_gate[...], block)


def finish(row_hot, grad_hot, row_gate, got):
    parts, rows, piece = got.shape
    count = row_hot.shape[1]
    if piece % LANES:
        return combine(row_hot, grad_hot, row_gate, got.transpose(1, 0, 2).reshape(rows, parts * piece))
    shape = like((count, parts * piece))
    spec = pl.BlockSpec((count, piece), lambda p: (0, p))
    return pl.pallas_call(
        finish_kernel,
        out_shape=(shape, shape),
        grid=(parts,),
        in_specs=[IN_VMEM] * 4,
        out_specs=(spec, spec),
        compiler_params=ROOM,
        name="finish",
    )(row_hot, grad_hot, row_gate, got)


def split_rows(block):
    pick_row, pick_grad = pickers(block.shape[0] // 2)
    return mm(pick_row, block).astype(BF16), mm(pick_grad, block).astype(BF16)


def forward_kernel(got, gate, up, down, pre, rows, grads, held_up, held_down, sems):
    hidden = gate.shape[1]
    fetch_up = pltpu.make_async_copy(up, held_up, sems.at[0])
    fetch_down = pltpu.make_async_copy(down, held_down, sems.at[1])
    fetch_up.start()
    fetch_down.start()
    row_part, grad_part = split_rows(got[...])
    rows[...], grads[...] = row_part, grad_part
    pre[:, :hidden] = mm(row_part, gate[...]).astype(BF16)
    fetch_up.wait()
    pre[:, hidden : 2 * hidden] = mm(row_part, held_up[...]).astype(BF16)
    fetch_down.wait()
    pre[:, 2 * hidden :] = mm(grad_part, held_down[...]).astype(BF16)


def forward(got, gate, up, down):
    total, piece = got.shape
    count = total // 2
    hidden = gate.shape[1]
    if piece % LANES:
        rows, grads = split_rows(got)
        pre = jnp.concatenate([mm(rows, gate), mm(rows, up), mm(grads, down)], axis=1)
        return pre.astype(BF16), rows, grads, up, down
    kept = like((count, piece))
    return pl.pallas_call(
        forward_kernel,
        out_shape=(like((count, 3 * hidden)), kept, kept, like(up.shape), like(down.shape)),
        in_specs=[IN_VMEM, IN_VMEM, IN_HBM, IN_HBM],
        out_specs=(IN_VMEM,) * 5,
        scratch_shapes=[DMA((2,))],
        compiler_params=ROOM,
        name="forward",
    )(got, gate, in_hbm(up), in_hbm(down))


def middle_kernel(hidden, partials, out):
    out[...] = nonlinear([partials[k] for k in range(partials.shape[0])], hidden)


def middle(partials, hidden):
    _, rows, width = partials.shape
    return pl.pallas_call(
        functools.partial(middle_kernel, hidden),
        out_shape=like((rows, width)),
        in_specs=[IN_VMEM],
        out_specs=IN_VMEM,
        compiler_params=ROOM,
        name="middle",
    )(partials)


def backward_rows(acts, gate, up, down):
    hidden = gate.shape[1]
    pick_row, pick_grad = pickers(acts.shape[0])
    gate_grad = mm(pick_grad, acts[:, :hidden], 0, 0).astype(BF16)
    up_grad = mm(pick_grad, acts[:, hidden : 2 * hidden], 0, 0).astype(BF16)
    active = mm(pick_row, acts[:, 2 * hidden :], 0, 0).astype(BF16)
    total = mm(down, active, 1, 1) + mm(gate, gate_grad, 1, 1) + mm(up, up_grad, 1, 1)
    return total.astype(BF16).T


def backward_kernel(acts, gate, up, down, out):
    out[...] = backward_rows(acts[...], gate[...], up[...], down[...])


def backward(acts, gate, up, down):
    piece = gate.shape[0]
    if piece % LANES:
        return backward_rows(acts, gate, up, down)
    return pl.pallas_call(
        backward_kernel,
        out_shape=like((2 * acts.shape[0], piece)),
        in_specs=[IN_VMEM] * 4,
        out_specs=IN_VMEM,
        compiler_params=ROOM,
        name="backward",
    )(acts, gate, up, down)


def weights_kernel(rows, grads, acts, gate, up, down):
    hidden = gate.shape[1]
    gate[...] = mm(rows[...], acts[:, :hidden], 0, 0).astype(BF16)
    up[...] = mm(rows[...], acts[:, hidden : 2 * hidden], 0, 0).astype(BF16)
    down[...] = mm(grads[...], acts[:, 2 * hidden :], 0, 0).astype(BF16)


def weights(rows, grads, acts, hidden):
    count, piece = rows.shape
    if piece % LANES:
        return (
            mm(rows, acts[:, :hidden], 0, 0).astype(BF16),
            mm(rows, acts[:, hidden : 2 * hidden], 0, 0).astype(BF16),
            mm(grads, acts[:, 2 * hidden :], 0, 0).astype(BF16),
        )
    step = 2 * LANES
    shape = like((piece, hidden))
    spec = pl.BlockSpec((step, hidden), lambda d: (d, 0))
    kept = pl.BlockSpec((count, step), lambda d: (0, d))
    return pl.pallas_call(
        weights_kernel,
        out_shape=(shape, shape, shape),
        grid=(piece // step,),
        in_specs=[kept, kept, pl.BlockSpec(acts.shape, lambda d: (0, 0))],
        out_specs=(spec, spec, spec),
        compiler_params=ROOM,
        name="weights",
    )(rows, grads, acts)


def body(tokens, route_ids, gate_weights, gate_weight, up_weight, down_weight, cotangent):
    experts = lax.axis_size("expert")
    parts = lax.axis_size("dp")
    both = ("dp", "expert")
    gate, up, down = gate_weight[0], up_weight[0], down_weight[0]
    piece, hidden = gate.shape
    ids, gates = route_ids.T, gate_weights.T
    block = 2 * CAP

    sent, row_hot, grad_hot, row_gate = prep(ids, gates, tokens, cotangent, experts, parts)
    sent = sent.reshape(parts * experts, block, piece)
    got = lax.all_to_all(sent, both, 0, 0, tiled=True)
    got = got.reshape(parts * experts * block, piece)
    pre, rows, grads, up, down = forward(got, gate, up, down)
    mine = lax.all_to_all(pre.reshape(parts, experts * CAP, 3 * hidden), "dp", 0, 0, tiled=True)
    acts = lax.all_gather(middle(mine, hidden), "dp", axis=0, tiled=True)
    back = backward(acts, gate, up, down)
    back = lax.all_to_all(back.reshape(parts * experts, block, piece), both, 0, 0, tiled=True)
    totals = weights(rows, grads, acts, hidden)
    back = back.reshape(parts, experts * block, piece)
    output, grad_tokens = finish(row_hot, grad_hot, row_gate, back)
    return (output, grad_tokens) + tuple(total[None] for total in totals)


def solution(mesh):
    rows = P(("dp", "expert"), None)
    held = P("expert", "dp", None)
    return jax.shard_map(
        body,
        mesh=mesh,
        in_specs=(rows, rows, rows, held, held, held, rows),
        out_specs=(rows, rows, held, held, held),
        check_vma=False,
    )
```

time: 119 us -> 100 us (0.84)
  Pallas kernels: 37.1 us -> 21.4 us
  blocking collectives: 58.5 us -> 57.1 us
  waiting for transfers between devices: 17.1 us -> 18.3 us
    pallas_call x5, Pallas kernels: 29.5 us -> 15 us  [the longest x1 4.59 us: backward(): pl.pallas_call(backward_kernel, out_shape=like((2 * acts.shape[0], piece)...]
where the time goes in v2:
time: 100 us
  blocking collectives  57.1 us (57%)
  Pallas kernels  21.4 us (21%)
  waiting for transfers between devices  18.3 us (18%)
  starting transfers between devices  2.64 us (3%)
    all_to_all x1, blocking collectives, body(): got = lax.all_to_all(sent, both, 0, 0, tiled=True)  31.8 us
    all_to_all x1, waiting for transfers between devices, body(): lax.all_to_all(back.reshape(parts * experts, block, piece), both, 0, 0, t...  18.3 us
    all_to_all x1, blocking collectives, body(): lax.all_to_all(pre.reshape(parts, experts * CAP, 3 * hidden), 'dp', 0, 0,...  13.9 us
    all_gather x1, blocking collectives, body(): acts = lax.all_gather(middle(mine, hidden), 'dp', axis=0, tiled=True)  11.3 us
    pallas_call x1, Pallas kernels, weights(): pl.pallas_call(weights_kernel, out_shape=(shape, shape, shape), grid=(pie...  6.39 us
    pallas_call x1, Pallas kernels, backward(): pl.pallas_call(backward_kernel, out_shape=like((2 * acts.shape[0], piece)...  4.59 us
    pallas_call x1, Pallas kernels, forward(): pl.pallas_call(forward_kernel, out_shape=(like((count, 3 * hidden)), kept...  3.84 us
    pallas_call x1, Pallas kernels, prep(): pl.pallas_call(functools.partial(prep_kernel, experts), out_shape=(like((...  3.41 us
  transfers between devices with their start and end apart: 1, of which 1 were waited for; matrix products, arithmetic and copies ran while one was open for 0% of the time, Pallas kernels for 6%

profile of v2, /device:TPU:0, one launch (start us, length us, event | category | flops | bytes accessed | tf_op | source)
XLA Modules:
  0.0 100.1 jit_solution(17389562813116753743)
XLA Ops:
  0.6 0.0 copy-start
  0.6 3.4 %prep.1 = (bf16[4,64,1792]{2,1,0:T(8,128)(2,1)S(1)}, bf16[64,128]{1,0:T(8,128)(2,1)S(1)}, bf16[64,128]{1,0:T(8,128)(2,1)S(1)}, f32[64,1]{1,0:T(8,128)S(1)}) custom-call(s32[8,128]{1,0:T(8,128)} %bitcast.21, f32[8,128]{1,0:T(8,128)} %bitcast.22, bf16[128,7168]{1,0:T(8,128)(2,1)} %tokens.1, bf16[128,7168]{1,0:T(8,128)(2,1)} %cotangent.1), custom_call_target="tpu_custom_call" | custom-call | tf_op jit(solution)/shard_map/prep/pallas_call | solution.py:125
  4.1 31.8 %all_to_all.15 = bf16[32,8,1792]{2,1,0:T(8,128)(2,1)S(1)} all-to-all(bf16[32,8,1792]{2,1,0:T(8,128)(2,1)S(1)} %bitcast.17), channel_id=1, replica_groups=mesh['dp'=4,'expert'=8] {'dp','expert'}, dimensions={0} | all-to-all | bytes 1835008 | tf_op jit(solution)/shard_map/all_to_all | solution.py:284
  35.8 0.0 copy-done
  35.8 3.8 %forward.1 = (bf16[128,3072]{1,0:T(8,128)(2,1)S(1)}, bf16[128,1792]{1,0:T(8,128)(2,1)S(1)}, bf16[128,1792]{1,0:T(8,128)(2,1)S(1)}, bf16[1792,1024]{1,0:T(8,128)(2,1)S(1)}, bf16[1792,1024]{1,0:T(8,128)(2,1)S(1)}) custom-call(bf16[256,1792]{1,0:T(8,128)(2,1)S(1)} %bitcast.15, bf16[1792,1024]{1,0:T(8,128)(2,1)S(1)} %bitcast.13, bf16[1792,1024]{1,0:T(8,128)(2,1)} %bitcast.19, ...), custom_call_target="tpu_custom_call" | custom-call | tf_op jit(solution)/shard_map/forward/pallas_call | solution.py:188
  39.7 13.9 %all_to_all.16.partials = bf16[4,32,3072]{2,1,0:T(8,128)(2,1)S(1)} all-to-all(bf16[4,32,3072]{2,1,0:T(8,128)(2,1)S(1)} %bitcast.18), channel_id=1, replica_groups=mesh['dp'=4,'expert'=8] {'dp'}, dimensions={0} | all-to-all | bytes 1572864 | tf_op jit(solution)/shard_map/all_to_all | solution.py:287
  53.6 0.1 middle.1
  53.8 11.3 %all_gather.3.acts = bf16[128,3072]{1,0:T(8,128)(2,1)S(1)} all-gather(bf16[32,3072]{1,0:T(8,128)(2,1)S(1)} %middle.1), channel_id=1, replica_groups=mesh['dp'=4,'expert'=8] {'dp'}, dimensions={0}, use_global_device_ids=true | all-gather | bytes 983040 | tf_op jit(solution)/shard_map/all_gather | solution.py:288
  65.1 4.6 %backward.1 = bf16[256,1792]{1,0:T(8,128)(2,1)} custom-call(bf16[128,3072]{1,0:T(8,128)(2,1)S(1)} %all_gather.3.acts, bf16[1792,1024]{1,0:T(8,128)(2,1)S(1)} %bitcast.14, bf16[1792,1024]{1,0:T(8,128)(2,1)S(1)} %get-tuple-element.24.up, bf16[1792,1024]{1,0:T(8,128)(2,1)S(1)} %get-tuple-element.25.down), custom_call_target="tpu_custom_call" | custom-call | tf_op jit(solution)/shard_map/backward/pallas_call | solution.py:233
  69.7 2.6 %all-to-all-start.2 = ((bf16[32,8,1792]{2,1,0:T(8,128)(2,1)}), bf16[32,8,1792]{2,1,0:T(8,128)(2,1)S(1)}, u32[]{:S(2)}, u32[]{:S(2)}) async-start(bf16[32,8,1792]{2,1,0:T(8,128)(2,1)} %bitcast.8), calls=%async_computation.2 | async-start | bytes 1835008 | tf_op jit(solution)/shard_map/all_to_all | solution.py:290
  72.4 6.4 %weights.1 = (bf16[1792,1024]{1,0:T(8,128)(2,1)}, bf16[1792,1024]{1,0:T(8,128)(2,1)}, bf16[1792,1024]{1,0:T(8,128)(2,1)}) custom-call(bf16[128,1792]{1,0:T(8,128)(2,1)S(1)} %get-tuple-element.28.rows, bf16[128,1792]{1,0:T(8,128)(2,1)S(1)} %get-tuple-element.29.grads, bf16[128,3072]{1,0:T(8,128)(2,1)S(1)} %all_gather.3.acts), custom_call_target="tpu_custom_call" | custom-call | tf_op jit(solution)/shard_map/weights/pallas_call | solution.py:262
  78.7 18.3 %all-to-all-done.2 = bf16[32,8,1792]{2,1,0:T(8,128)(2,1)S(1)} async-done(((bf16[32,8,1792]{2,1,0:T(8,128)(2,1)}), bf16[32,8,1792]{2,1,0:T(8,128)(2,1)S(1)}, u32[]{:S(2)}, u32[]{:S(2)}) %all-to-all-start.2) | async-done | bytes 917536 | tf_op jit(solution)/shard_map/all_to_all | solution.py:290
  97.0 3.0 %finish.1 = (bf16[128,7168]{1,0:T(8,128)(2,1)}, bf16[128,7168]{1,0:T(8,128)(2,1)}) custom-call(bf16[64,128]{1,0:T(8,128)(2,1)S(1)} %get-tuple-element.19.row_hot, bf16[64,128]{1,0:T(8,128)(2,1)S(1)} %get-tuple-element.20.grad_hot, f32[64,1]{1,0:T(8,128)S(1)} %get-tuple-element.21.row_gate, bf16[4,64,1792]{2,1,0:T(8,128)(2,1)S(1)} %bitcast.16), custom_call_target="tpu_custom_call" | custom-call | tf_op jit(solution)/shard_map/finish/pallas_call | solution.py:148
Async XLA Ops:
  0.6 35.2 %copy-start = (bf16[1,1792,1024]{2,1,0:T(8,128)(2,1)S(1)}, bf16[1,1792,1024]{2,1,0:T(8,128)(2,1)}, u32[]{:S(2)}) copy-start(bf16[1,1792,1024]{2,1,0:T(8,128)(2,1)} %param.10) | copy-start | bytes 11010052
  69.7 27.3 %all-to-all-start.2 = ((bf16[32,8,1792]{2,1,0:T(8,128)(2,1)}), bf16[32,8,1792]{2,1,0:T(8,128)(2,1)S(1)}, u32[]{:S(2)}, u32[]{:S(2)}) async-start(bf16[32,8,1792]{2,1,0:T(8,128)(2,1)} %bitcast.8), calls=%async_computation.2 | async-start | bytes 1835008 | tf_op jit(solution)/shard_map/all_to_all | solution.py:290

commit v3 on v2

v3 whole, which is shorter than its diff:
```python
import functools

import jax
import jax.numpy as jnp
from jax import lax
from jax.experimental import pallas as pl
from jax.experimental.pallas import tpu as pltpu
from jax.sharding import PartitionSpec as P


CAP = 4
LANES = 128
F32 = jnp.float32
BF16 = jnp.bfloat16


def mm(left, right, left_dim=1, right_dim=0):
    return lax.dot_general(
        left, right, (((left_dim,), (right_dim,)), ((), ())), preferred_element_type=F32
    )


def iota(shape, dim):
    return lax.broadcasted_iota(jnp.int32, shape, dim)


def slots_of(ids, gates, experts):
    count = ids.shape[1]
    hit = ids < experts
    expert = jnp.sum(jnp.where(hit, ids, 0), axis=0, keepdims=True)
    held = jnp.max(jnp.where(hit, 1, 0), axis=0, keepdims=True) > 0
    gate = jnp.sum(jnp.where(hit, gates, 0.0), axis=0, keepdims=True)
    chosen = (iota((experts, count), 0) == expert) & held
    before = (iota((count, count), 0) < iota((count, count), 1)).astype(F32).astype(BF16)
    ranks = mm(chosen.astype(F32).astype(BF16), before)
    rank = jnp.sum(jnp.where(chosen, ranks, 0.0), axis=0, keepdims=True).astype(jnp.int32)
    slot = jnp.where(held, expert * (2 * CAP) + rank, -2 * CAP)
    rows = iota((experts * 2 * CAP, count), 0)
    row_hot = rows == slot
    grad_hot = rows == slot + CAP
    row_gate = jnp.sum(jnp.where(row_hot, gate, 0.0), axis=1, keepdims=True)
    grad_gate = jnp.sum(jnp.where(grad_hot, gate, 0.0), axis=1, keepdims=True)
    return row_hot.astype(F32).astype(BF16), grad_hot.astype(F32).astype(BF16), row_gate, grad_gate


def fill_rows(row_hot, grad_hot, grad_gate, tokens, cotangent):
    return (mm(row_hot, tokens) + grad_gate * mm(grad_hot, cotangent)).astype(BF16)


def combine(row_hot, grad_hot, row_gate, got):
    wide = got.astype(F32)
    is_row = iota(row_gate.shape, 0) % (2 * CAP) < CAP
    weighted = jnp.where(is_row, row_gate * wide, wide).astype(BF16)
    return mm(row_hot, weighted, 0, 0).astype(BF16), mm(grad_hot, weighted, 0, 0).astype(BF16)


def pickers(count, me=0, group=None):
    row = iota((count, 2 * count), 0)
    if group is not None:
        row = ((row // group) ^ me) * group + row % group
    at = row // CAP * (2 * CAP) + row % CAP
    column = iota((count, 2 * count), 1)
    return (column == at).astype(F32).astype(BF16), (column == at + CAP).astype(F32).astype(BF16)


def add_up(parts):
    return functools.reduce(lambda a, b: a + b, [part.astype(F32) for part in parts])


def hidden_of(pre, hidden):
    pre_gate = pre[:, :hidden]
    return (pre_gate * jax.nn.sigmoid(pre_gate) * pre[:, hidden:]).astype(BF16)


def grads_of(pre, hidden_grad, hidden):
    pre_gate = pre[:, :hidden]
    pre_up = pre[:, hidden:]
    squash = jax.nn.sigmoid(pre_gate)
    gate_grad = hidden_grad * pre_up * squash * (1.0 + pre_gate * (1.0 - squash))
    up_grad = hidden_grad * (pre_gate * squash)
    return jnp.concatenate([gate_grad.astype(BF16), up_grad.astype(BF16)], axis=1)


def plain_middle(me, got, gate, up, down):
    count = got.shape[0] // 2
    hidden = gate.shape[1]
    pick_row, pick_grad = pickers(count)
    rows = mm(pick_row, got).astype(BF16)
    grads = mm(pick_grad, got).astype(BF16)
    pre = jnp.concatenate([mm(rows, gate), mm(rows, up), mm(grads, down)], axis=1).astype(BF16)
    parts = lax.axis_size("dp")
    mine = lax.all_to_all(pre.reshape(parts, count // parts, 3 * hidden), "dp", 0, 0, tiled=True)
    total = add_up([mine[k] for k in range(parts)])
    pair = total[:, : 2 * hidden]
    acts = jnp.concatenate(
        [grads_of(pair, total[:, 2 * hidden :], hidden), hidden_of(pair, hidden)], axis=1
    )
    acts = lax.all_gather(acts, "dp", axis=0, tiled=True)
    gate_grad, up_grad, active = (acts[:, i * hidden : (i + 1) * hidden] for i in range(3))
    out = mm(active, down, 1, 1).astype(BF16)
    back = (mm(gate_grad, gate, 1, 1) + mm(up_grad, up, 1, 1)).astype(BF16)
    sent = (mm(pick_row, out, 0, 0) + mm(pick_grad, back, 0, 0)).astype(BF16)
    totals = (
        mm(rows, gate_grad, 0, 0).astype(BF16),
        mm(rows, up_grad, 0, 0).astype(BF16),
        mm(grads, active, 0, 0).astype(BF16),
    )
    return sent, totals


ROOM = pltpu.CompilerParams(vmem_limit_bytes=16 * 2**20)
IN_VMEM = pl.BlockSpec(memory_space=pltpu.VMEM)
IN_HBM = pl.BlockSpec(memory_space=pltpu.HBM)
IN_SMEM = pl.BlockSpec(memory_space=pltpu.SMEM)
DMA = pltpu.SemaphoreType.DMA


def in_hbm(x):
    return pltpu.with_memory_space_constraint(x, pltpu.HBM)


def like(shape):
    return jax.ShapeDtypeStruct(shape, BF16)


def prep_kernel(experts, me, ids, gates, tokens, cotangent, out, row_hot, grad_hot, row_gate, held, sems):
    del me
    parts, _, piece = out.shape
    copies = [
        [
            pltpu.make_async_copy(
                full.at[:, pl.ds(p * piece, piece)], held.at[k, p], sems.at[k, p]
            )
            for k, full in enumerate((tokens, cotangent))
        ]
        for p in range(parts)
    ]
    for pair in copies:
        for copy in pair:
            copy.start()
    row_hot[...], grad_hot[...], row_gate[...], grad_gate = slots_of(ids[...], gates[...], experts)
    for p, pair in enumerate(copies):
        for copy in pair:
            copy.wait()
        out[p] = fill_rows(row_hot[...], grad_hot[...], grad_gate, held[0, p], held[1, p])


def prep(me, ids, gates, tokens, cotangent, experts, parts):
    count, width = tokens.shape
    piece = width // parts
    rows = experts * 2 * CAP
    if piece % LANES:
        row_hot, grad_hot, row_gate, grad_gate = slots_of(ids, gates, experts)
        full = fill_rows(row_hot, grad_hot, grad_gate, tokens, cotangent)
        return full.reshape(rows, parts, piece).transpose(1, 0, 2), row_hot, grad_hot, row_gate
    hot = like((rows, count))
    return pl.pallas_call(
        functools.partial(prep_kernel, experts),
        out_shape=(like((parts, rows, piece)), hot, hot, jax.ShapeDtypeStruct((rows, 1), F32)),
        in_specs=[IN_SMEM, IN_VMEM, IN_VMEM, IN_HBM, IN_HBM],
        out_specs=(IN_VMEM,) * 4,
        scratch_shapes=[pltpu.VMEM((2, parts, count, piece), BF16), DMA((2, parts))],
        compiler_params=ROOM,
        name="prep",
    )(me, in_hbm(ids), in_hbm(gates), in_hbm(tokens), in_hbm(cotangent))


def finish_kernel(row_hot, grad_hot, row_gate, got, out, grad):
    block = got[pl.program_id(0)]
    out[...], grad[...] = combine(row_hot[...], grad_hot[...], row_gate[...], block)


def finish(row_hot, grad_hot, row_gate, got):
    parts, rows, piece = got.shape
    count = row_hot.shape[1]
    if piece % LANES:
        return combine(row_hot, grad_hot, row_gate, got.transpose(1, 0, 2).reshape(rows, parts * piece))
    shape = like((count, parts * piece))
    spec = pl.BlockSpec((count, piece), lambda p: (0, p))
    return pl.pallas_call(
        finish_kernel,
        out_shape=(shape, shape),
        grid=(parts,),
        in_specs=[IN_VMEM] * 4,
        out_specs=(spec, spec),
        compiler_params=ROOM,
        name="finish",
    )(row_hot, grad_hot, row_gate, got)


def blocks_of(value, refs):
    group = refs[0].shape[0]
    for k, ref in enumerate(refs):
        ref[...] = value[k * group : (k + 1) * group]


def rows_kernel(parts, me, got, gate, up, rows, *rest):
    sent, (held_up, sem) = rest[:parts], rest[parts:]
    fetch = pltpu.make_async_copy(up, held_up, sem)
    fetch.start()
    count = rows.shape[0]
    pick, _ = pickers(count, me[0], count // parts)
    part = mm(pick, got[...]).astype(BF16)
    rows[...] = part
    first = mm(part, gate[...]).astype(BF16)
    fetch.wait()
    blocks_of(jnp.concatenate([first, mm(part, held_up[...]).astype(BF16)], axis=1), sent)


def grads_kernel(parts, me, got, down, rows, *rest):
    sent, (held_down, sem) = rest[:parts], rest[parts:]
    fetch = pltpu.make_async_copy(down, held_down, sem)
    fetch.start()
    count = rows.shape[0]
    _, pick = pickers(count, me[0], count // parts)
    part = mm(pick, got[...]).astype(BF16)
    rows[...] = part
    fetch.wait()
    blocks_of(mm(part, held_down[...]).astype(BF16), sent)


def hidden_kernel(hidden, count, *refs):
    refs[-1][...] = hidden_of(add_up([part[...] for part in refs[:count]]), hidden)


def grad_kernel(hidden, count, *refs):
    pre = add_up([part[...] for part in refs[:count]])
    hidden_grad = add_up([part[...] for part in refs[count : 2 * count]])
    refs[-1][...] = grads_of(pre, hidden_grad, hidden)


def stacked(refs):
    return jnp.concatenate([ref[...] for ref in refs], axis=0)


def output_kernel(parts, me, *refs):
    active = stacked(refs[:parts])
    down, out = refs[parts:]
    pick, _ = pickers(active.shape[0], me[0], active.shape[0] // parts)
    spread = mm(pick, active, 0, 0).astype(BF16)
    out[...] = mm(down[...], spread, 1, 1).astype(BF16).T


def back_kernel(parts, me, *refs):
    acts = stacked(refs[:parts])
    gate, up, first, out = refs[parts:]
    hidden = gate.shape[1]
    _, pick = pickers(acts.shape[0], me[0], acts.shape[0] // parts)
    spread = mm(pick, acts, 0, 0).astype(BF16)
    total = mm(gate[...], spread[:, :hidden], 1, 1) + mm(up[...], spread[:, hidden:], 1, 1)
    out[...] = total.astype(BF16).T + first[...]


def weights_kernel(parts, rows, grads, *refs):
    actives, acts = refs[:parts], refs[parts : 2 * parts]
    gate, up, down, held_active, held = refs[2 * parts :]
    hidden = gate.shape[1]

    @pl.when(pl.program_id(0) == 0)
    def _():
        held_active[...] = stacked(actives)
        held[...] = stacked(acts)

    gate[...] = mm(rows[...], held[:, :hidden], 0, 0).astype(BF16)
    up[...] = mm(rows[...], held[:, hidden:], 0, 0).astype(BF16)
    down[...] = mm(grads[...], held_active[...], 0, 0).astype(BF16)


def run(kernel, outs, args, hbm=(), scratch=()):
    specs = [
        IN_SMEM
        if x.shape == (1,)
        else IN_HBM
        if i in hbm
        else IN_VMEM
        for i, x in enumerate(args)
    ]
    return pl.pallas_call(
        kernel,
        out_shape=tuple(like(shape) for shape in outs),
        in_specs=specs,
        out_specs=(IN_VMEM,) * len(outs),
        scratch_shapes=list(scratch),
        compiler_params=ROOM,
    )(*(in_hbm(x) if i in hbm else x for i, x in enumerate(args)))


def to_all(blocks):
    parts = len(blocks)
    moved = {
        k: lax.ppermute(blocks[k], "dp", [(i, i ^ k) for i in range(parts)])
        for k in range(parts - 1, 0, -1)
    }
    return [blocks[0]] + [moved[k] for k in range(1, parts)]


def tiled_middle(me, got, gate, up, down):
    total, piece = got.shape
    count = total // 2
    hidden = gate.shape[1]
    parts = lax.axis_size("dp")
    group = count // parts
    part = functools.partial

    held = [pltpu.VMEM((piece, hidden), BF16), DMA]
    rows, *sent = run(
        part(rows_kernel, parts),
        ((count, piece),) + ((group, 2 * hidden),) * parts,
        (me, got, gate, up),
        hbm=(3,),
        scratch=held,
    )
    pre = to_all(sent)
    grads, *sent = run(
        part(grads_kernel, parts),
        ((count, piece),) + ((group, hidden),) * parts,
        (me, got, down),
        hbm=(2,),
        scratch=held,
    )
    hidden_grad = to_all(sent)
    (active,) = run(part(hidden_kernel, hidden, parts), ((group, hidden),), (*pre, sent[0]))
    actives = to_all([active] * parts)
    (acts,) = run(part(grad_kernel, hidden, parts), ((group, 2 * hidden),), (*pre, *hidden_grad, active))
    acts = to_all([acts] * parts)
    (first,) = run(part(output_kernel, parts), ((total, piece),), (me, *actives, down))
    (back,) = run(part(back_kernel, parts), ((total, piece),), (me, *acts, gate, up, first))

    step = 2 * LANES
    spec = pl.BlockSpec((step, hidden), lambda d: (d, 0))
    kept = pl.BlockSpec((count, step), lambda d: (0, d))
    totals = pl.pallas_call(
        part(weights_kernel, parts),
        out_shape=(like((piece, hidden)),) * 3,
        grid=(piece // step,),
        in_specs=[kept, kept] + [IN_VMEM] * (2 * parts),
        out_specs=(spec, spec, spec),
        scratch_shapes=[pltpu.VMEM((count, hidden), BF16), pltpu.VMEM((count, 2 * hidden), BF16)],
        compiler_params=ROOM,
        name="weights",
    )(rows, grads, *actives, *acts)
    return back, totals


def body(tokens, route_ids, gate_weights, gate_weight, up_weight, down_weight, cotangent):
    experts = lax.axis_size("expert")
    parts = lax.axis_size("dp")
    both = ("dp", "expert")
    gate, up, down = gate_weight[0], up_weight[0], down_weight[0]
    piece = gate.shape[0]
    ids, gates = route_ids.T, gate_weights.T
    block = 2 * CAP

    me = lax.axis_index("dp").astype(jnp.int32).reshape(1)
    sent, row_hot, grad_hot, row_gate = prep(me, ids, gates, tokens, cotangent, experts, parts)
    sent = sent.reshape(parts * experts, block, piece)
    got = lax.all_to_all(sent, both, 0, 0, tiled=True)
    got = got.reshape(parts * experts * block, piece)
    tiled = piece % (2 * LANES) == 0 and parts & (parts - 1) == 0
    back, totals = (tiled_middle if tiled else plain_middle)(me, got, gate, up, down)
    back = lax.all_to_all(back.reshape(parts * experts, block, piece), both, 0, 0, tiled=True)
    back = back.reshape(parts, experts * block, piece)
    output, grad_tokens = finish(row_hot, grad_hot, row_gate, back)
    return (output, grad_tokens) + tuple(total[None] for total in totals)


def solution(mesh):
    rows = P(("dp", "expert"), None)
    held = P("expert", "dp", None)
    return jax.shard_map(
        body,
        mesh=mesh,
        in_specs=(rows, rows, rows, held, held, held, rows),
        out_specs=(rows, rows, held, held, held),
        check_vma=False,
    )
```

time: 100 us -> 98.2 us (0.982)
  blocking collectives: 57.1 us -> 31.8 us
  starting transfers between devices: 2.64 us -> 16.3 us
  waiting for transfers between devices: 18.3 us -> 25.1 us
  Pallas kernels: 21.4 us -> 23.8 us
    all_to_all x1 -> x0, blocking collectives: 13.9 us -> none  [body(): lax.all_to_all(pre.reshape(parts, experts * CAP, 3 * hidden), 'dp', 0, 0,...]
    ppermute x0 -> x12, starting transfers between devices: none -> 13.7 us  [to_all(): lax.ppermute(blocks[k], 'dp', [(i, i ^ k) for i in range(parts)])]
    all_gather x1 -> x0, blocking collectives: 11.3 us -> none  [body(): acts = lax.all_gather(middle(mine, hidden), 'dp', axis=0, tiled=True)]
    ppermute x0 -> x12, waiting for transfers between devices: none -> 6.4 us  [to_all(): lax.ppermute(blocks[k], 'dp', [(i, i ^ k) for i in range(parts)])]
    pallas_call x4 -> x7, Pallas kernels: 15 us -> 17.4 us  [the longest x6 11.5 us: run(): pl.pallas_call(kernel, out_shape=tuple((like(shape) for shape in outs)),...]
  transfers between devices with their start and end apart: 1 -> 13, of which waited for: 1 -> 6; matrix products, arithmetic and copies ran while one was open for 0% -> 0% of each run, Pallas kernels for 6% -> 11%
where the time goes in v3:
time: 98.2 us; the launch traced here: 97.9 us
  blocking collectives  31.8 us (32%)
  waiting for transfers between devices  25.1 us (26%)
  Pallas kernels  23.8 us (24%)
  starting transfers between devices  16.3 us (17%)
    all_to_all x1, blocking collectives, body(): got = lax.all_to_all(sent, both, 0, 0, tiled=True)  31.8 us
    all_to_all x1, waiting for transfers between devices, body(): lax.all_to_all(back.reshape(parts * experts, block, piece), both, 0, 0, t...  18.7 us
    ppermute x12, starting transfers between devices, to_all(): lax.ppermute(blocks[k], 'dp', [(i, i ^ k) for i in range(parts)])  13.7 us
    pallas_call x6, Pallas kernels, run(): pl.pallas_call(kernel, out_shape=tuple((like(shape) for shape in outs)),...  11.5 us
    ppermute x12, waiting for transfers between devices, to_all(): lax.ppermute(blocks[k], 'dp', [(i, i ^ k) for i in range(parts)])  6.4 us
    pallas_call x1, Pallas kernels, tiled_middle(): pl.pallas_call(part(weights_kernel, parts), out_shape=(like((piece, hidde...  5.92 us
    pallas_call x1, Pallas kernels, prep(): pl.pallas_call(functools.partial(prep_kernel, experts), out_shape=(like((...  3.41 us
    pallas_call x1, Pallas kernels, finish(): pl.pallas_call(finish_kernel, out_shape=(shape, shape), grid=(parts,), in...  3.05 us
  transfers between devices with their start and end apart: 13, of which 6 were waited for; matrix products, arithmetic and copies ran while one was open for 0% of the time, Pallas kernels for 11%

profile of v3, /device:TPU:0, one launch (start us, length us, event | category | flops | bytes accessed | tf_op | source)
XLA Modules:
  0.0 97.9 jit_solution(16189361107736720610)
XLA Ops:
  0.6 0.0 copy-start.1
  0.6 3.4 %prep.1 = (bf16[4,64,1792]{2,1,0:T(8,128)(2,1)S(1)}, bf16[64,128]{1,0:T(8,128)(2,1)S(1)}, bf16[64,128]{1,0:T(8,128)(2,1)S(1)}, f32[64,1]{1,0:T(8,128)S(1)}) custom-call(s32[1]{0:T(128)} %bitcast.me, s32[8,128]{1,0:T(8,128)} %bitcast.23, f32[8,128]{1,0:T(8,128)} %bitcast.24, bf16[128,7168]{1,0:T(8,128)(2,1)} %tokens.1, bf16[128,7168]{1,0:T(8,128)(2,1)} %cotangent.1), custom_call_target="tpu_custom_call" | custom-call | tf_op jit(solution)/shard_map/prep/pallas_call | solution.py:157
  4.1 31.8 %all_to_all.10 = bf16[32,8,1792]{2,1,0:T(8,128)(2,1)S(1)} all-to-all(bf16[32,8,1792]{2,1,0:T(8,128)(2,1)S(1)} %bitcast.22), channel_id=1, replica_groups=mesh['dp'=4,'expert'=8] {'dp','expert'}, dimensions={0} | all-to-all | bytes 1835008 | tf_op jit(solution)/shard_map/all_to_all | solution.py:357
  35.9 0.0 copy-done.1
  35.9 3.4 %shard_map.110 = (bf16[128,1792]{1,0:T(8,128)(2,1)S(1)}, bf16[32,2048]{1,0:T(8,128)(2,1)S(1)}, bf16[32,2048]{1,0:T(8,128)(2,1)S(1)}, bf16[32,2048]{1,0:T(8,128)(2,1)S(1)}, bf16[32,2048]{1,0:T(8,128)(2,1)S(1)}) custom-call(s32[1]{0:T(128)} %bitcast.me, bf16[256,1792]{1,0:T(8,128)(2,1)S(1)} %bitcast.19, bf16[1792,1024]{1,0:T(8,128)(2,1)S(1)} %bitcast.15, ...), custom_call_target="tpu_custom_call" | custom-call | tf_op jit(solution)/shard_map/pallas_call | solution.py:278
  39.2 0.0 copy-start
  39.3 0.1 collective-permute-start
  39.3 1.1 %collective-permute-start.1 = (bf16[32,2048]{1,0:T(8,128)(2,1)S(1)}, bf16[32,2048]{1,0:T(8,128)(2,1)S(1)}, u32[]{:S(2)}, u32[]{:S(2)}) collective-permute-start(bf16[32,2048]{1,0:T(8,128)(2,1)S(1)} %get-tuple-element.30), channel_id=1, source_target_pairs={{0,16},{8,24},{16,0},{24,8},{1,17},{9,25},{17,1},{25,9},{2,18},{10... | collective-permute-start | bytes 393224 | tf_op jit(solution)/shard_map/ppermute | solution.py:291
  40.4 2.4 %collective-permute-start.2 = (bf16[32,2048]{1,0:T(8,128)(2,1)S(1)}, bf16[32,2048]{1,0:T(8,128)(2,1)S(1)}, u32[]{:S(2)}, u32[]{:S(2)}) collective-permute-start(bf16[32,2048]{1,0:T(8,128)(2,1)S(1)} %get-tuple-element.31), channel_id=1, source_target_pairs={{0,24},{8,16},{16,8},{24,0},{1,25},{9,17},{17,9},{25,1},{2,26},{10... | collective-permute-start | bytes 393224 | tf_op jit(solution)/shard_map/ppermute | solution.py:291
  42.8 2.7 %shard_map.111 = (bf16[128,1792]{1,0:T(8,128)(2,1)S(1)}, bf16[32,1024]{1,0:T(8,128)(2,1)S(1)}, bf16[32,1024]{1,0:T(8,128)(2,1)S(1)}, bf16[32,1024]{1,0:T(8,128)(2,1)S(1)}, bf16[32,1024]{1,0:T(8,128)(2,1)S(1)}) custom-call(s32[1]{0:T(128)} %bitcast.me, bf16[256,1792]{1,0:T(8,128)(2,1)S(1)} %bitcast.20, bf16[1792,1024]{1,0:T(8,128)(2,1)} %bitcast.13), custom_call_target="tpu_custom_call" | custom-call | tf_op jit(solution)/shard_map/pallas_call | solution.py:278
  45.5 0.0 copy-start.2
  45.5 0.1 collective-permute-start.3
  45.7 1.0 %collective-permute-start.4 = (bf16[32,1024]{1,0:T(8,128)(2,1)S(1)}, bf16[32,1024]{1,0:T(8,128)(2,1)S(1)}, u32[]{:S(2)}, u32[]{:S(2)}) collective-permute-start(bf16[32,1024]{1,0:T(8,128)(2,1)S(1)} %get-tuple-element.34), channel_id=1, source_target_pairs={{0,16},{8,24},{16,0},{24,8},{1,17},{9,25},{17,1},{25,9},{2,18},{10... | collective-permute-start | bytes 196616 | tf_op jit(solution)/shard_map/ppermute | solution.py:291
  46.7 0.0 collective-permute-done.refs_1_
  46.7 2.4 %collective-permute-start.5 = (bf16[32,1024]{1,0:T(8,128)(2,1)S(1)}, bf16[32,1024]{1,0:T(8,128)(2,1)S(1)}, u32[]{:S(2)}, u32[]{:S(2)}) collective-permute-start(bf16[32,1024]{1,0:T(8,128)(2,1)S(1)} %get-tuple-element.35), channel_id=1, source_target_pairs={{0,24},{8,16},{16,8},{24,0},{1,25},{9,17},{17,9},{25,1},{2,26},{10... | collective-permute-start | bytes 196616 | tf_op jit(solution)/shard_map/ppermute | solution.py:291
  49.1 0.0 collective-permute-done.1.refs_2_
  49.1 0.0 collective-permute-done.2.refs_3_
  49.1 0.1 shard_map.112.refs_8_.refs_0_
  49.2 0.6 collective-permute-start.10
  49.8 0.7 collective-permute-done.3.refs_5_
  50.5 0.3 collective-permute-done.4.refs_6_
  50.8 1.2 %collective-permute-done.5.refs_7_ = bf16[32,1024]{1,0:T(8,128)(2,1)S(1)} collective-permute-done((bf16[32,1024]{1,0:T(8,128)(2,1)S(1)}, bf16[32,1024]{1,0:T(8,128)(2,1)S(1)}, u32[]{:S(2)}, u32[]{:S(2)}) %collective-permute-start.5) | collective-permute-done | bytes 65568 | tf_op jit(solution)/shard_map/ppermute | solution.py:291
  52.0 0.1 shard_map.113.refs_0_.refs_4_
  52.1 1.6 %collective-permute-start.6 = (bf16[32,2048]{1,0:T(8,128)(2,1)S(1)}, bf16[32,2048]{1,0:T(8,128)(2,1)S(1)}, u32[]{:S(2)}, u32[]{:S(2)}) collective-permute-start(bf16[32,2048]{1,0:T(8,128)(2,1)S(1)} %shard_map.113.refs_0_.refs_4_), channel_id=1, source_target_pairs={{0,8},{8,0},{16,24},{24,16},{1,9},{9,1},{17,25},{25,17},{2,10},{10... | collective-permute-start | bytes 393224 | tf_op jit(solution)/shard_map/ppermute | solution.py:291
  53.7 1.4 %collective-permute-start.7 = (bf16[32,2048]{1,0:T(8,128)(2,1)S(1)}, bf16[32,2048]{1,0:T(8,128)(2,1)S(1)}, u32[]{:S(2)}, u32[]{:S(2)}) collective-permute-start(bf16[32,2048]{1,0:T(8,128)(2,1)S(1)} %shard_map.113.refs_0_.refs_4_), channel_id=1, source_target_pairs={{0,16},{8,24},{16,0},{24,8},{1,17},{9,25},{17,1},{25,9},{2,18},{10... | collective-permute-start | bytes 393224 | tf_op jit(solution)/shard_map/ppermute | solution.py:291
  55.1 0.5 collective-permute-start.8
  55.7 2.4 %collective-permute-start.11 = (bf16[32,1024]{1,0:T(8,128)(2,1)S(1)}, bf16[32,1024]{1,0:T(8,128)(2,1)S(1)}, u32[]{:S(2)}, u32[]{:S(2)}) collective-permute-start(bf16[32,1024]{1,0:T(8,128)(2,1)S(1)} %shard_map.112.refs_8_.refs_0_), channel_id=1, source_target_pairs={{0,24},{8,16},{16,8},{24,0},{1,25},{9,17},{17,9},{25,1},{2,26},{10... | collective-permute-start | bytes 196616 | tf_op jit(solution)/shard_map/ppermute | solution.py:291
  58.1 0.0 collective-permute-done.10.refs_2_
  58.1 0.1 collective-permute-start.9
  58.2 3.8 %collective-permute-done.11.refs_3_ = bf16[32,1024]{1,0:T(8,128)(2,1)S(1)} collective-permute-done((bf16[32,1024]{1,0:T(8,128)(2,1)S(1)}, bf16[32,1024]{1,0:T(8,128)(2,1)S(1)}, u32[]{:S(2)}, u32[]{:S(2)}) %collective-permute-start.11) | collective-permute-done | bytes 65568 | tf_op jit(solution)/shard_map/ppermute | solution.py:291
  61.9 0.4 collective-permute-done.9.refs_1_
  62.3 0.0 copy-done
  62.3 1.5 %shard_map.114.refs_6_ = bf16[256,1792]{1,0:T(8,128)(2,1)S(1)} custom-call(s32[1]{0:T(128)} %bitcast.me, bf16[32,1024]{1,0:T(8,128)(2,1)S(1)} %shard_map.112.refs_8_.refs_0_, bf16[32,1024]{1,0:T(8,128)(2,1)S(1)} %collective-permute-done.9.refs_1_, bf16[32,1024]{1,0:T(8,128)(2,1)S(1)} %collective-permute-done.10.refs_2_, ...), custom_call_target="tpu_custom_call" | custom-call | tf_op jit(solution)/shard_map/pallas_call | solution.py:278
  63.9 0.0 collective-permute-done.6.refs_1_.refs_5_
  63.9 0.0 collective-permute-done.7.refs_2_.refs_6_
  63.9 0.0 collective-permute-done.8.refs_3_.refs_7_
  63.9 0.0 copy-done.2
  63.9 3.6 %shard_map.115 = bf16[256,1792]{1,0:T(8,128)(2,1)} custom-call(s32[1]{0:T(128)} %bitcast.me, bf16[32,2048]{1,0:T(8,128)(2,1)S(1)} %shard_map.113.refs_0_.refs_4_, bf16[32,2048]{1,0:T(8,128)(2,1)S(1)} %collective-permute-done.6.refs_1_.refs_5_, bf16[32,2048]{1,0:T(8,128)(2,1)S(1)} %collective-permute-done.7.refs_2_.refs_6_, ...), custom_call_target="tpu_custom_call" | custom-call | tf_op jit(solution)/shard_map/pallas_call | solution.py:278
  67.5 2.6 %all-to-all-start.1 = ((bf16[32,8,1792]{2,1,0:T(8,128)(2,1)}), bf16[32,8,1792]{2,1,0:T(8,128)(2,1)S(1)}, u32[]{:S(2)}, u32[]{:S(2)}) async-start(bf16[32,8,1792]{2,1,0:T(8,128)(2,1)} %bitcast.8), calls=%async_computation.1 | async-start | bytes 1835008 | tf_op jit(solution)/shard_map/all_to_all | solution.py:361
  70.2 5.9 %weights.1 = (bf16[1792,1024]{1,0:T(8,128)(2,1)}, bf16[1792,1024]{1,0:T(8,128)(2,1)}, bf16[1792,1024]{1,0:T(8,128)(2,1)}) custom-call(bf16[128,1792]{1,0:T(8,128)(2,1)S(1)} %get-tuple-element.38.rows, bf16[128,1792]{1,0:T(8,128)(2,1)S(1)} %get-tuple-element.39.grads, bf16[32,1024]{1,0:T(8,128)(2,1)S(1)} %shard_map.112.refs_8_.refs_0_, ...), custom_call_target="tpu_custom_call" | custom-call | tf_op jit(solution)/shard_map/weights/pallas_call | solution.py:332
  76.1 18.7 %all-to-all-done.1 = bf16[32,8,1792]{2,1,0:T(8,128)(2,1)S(1)} async-done(((bf16[32,8,1792]{2,1,0:T(8,128)(2,1)}), bf16[32,8,1792]{2,1,0:T(8,128)(2,1)S(1)}, u32[]{:S(2)}, u32[]{:S(2)}) %all-to-all-start.1) | async-done | bytes 917536 | tf_op jit(solution)/shard_map/all_to_all | solution.py:361
  94.8 3.0 %finish.1 = (bf16[128,7168]{1,0:T(8,128)(2,1)}, bf16[128,7168]{1,0:T(8,128)(2,1)}) custom-call(bf16[64,128]{1,0:T(8,128)(2,1)S(1)} %get-tuple-element.24.row_hot, bf16[64,128]{1,0:T(8,128)(2,1)S(1)} %get-tuple-element.25.grad_hot, f32[64,1]{1,0:T(8,128)S(1)} %get-tuple-element.26.row_gate, bf16[4,64,1792]{2,1,0:T(8,128)(2,1)S(1)} %bitcast.21), custom_call_target="tpu_custom_call" | custom-call | tf_op jit(solution)/shard_map/finish/pallas_call | solution.py:180
Async XLA Ops:
  0.6 35.2 %copy-start.1 = (bf16[1,1792,1024]{2,1,0:T(8,128)(2,1)S(1)}, bf16[1,1792,1024]{2,1,0:T(8,128)(2,1)}, u32[]{:S(2)}) copy-start(bf16[1,1792,1024]{2,1,0:T(8,128)(2,1)} %param.10) | copy-start | bytes 11010052
  39.2 23.1 %copy-start = (bf16[1,1792,1024]{2,1,0:T(8,128)(2,1)S(1)}, bf16[1,1792,1024]{2,1,0:T(8,128)(2,1)}, u32[]{:S(2)}) copy-start(bf16[1,1792,1024]{2,1,0:T(8,128)(2,1)} %param.12) | copy-start | bytes 11010052
  39.3 7.5 %collective-permute-start = (bf16[32,2048]{1,0:T(8,128)(2,1)S(1)}, bf16[32,2048]{1,0:T(8,128)(2,1)S(1)}, u32[]{:S(2)}, u32[]{:S(2)}) collective-permute-start(bf16[32,2048]{1,0:T(8,128)(2,1)S(1)} %get-tuple-element.29), channel_id=1, source_target_pairs={{0,8},{8,0},{16,24},{24,16},{1,9},{9,1},{17,25},{25,17},{2,10},{10... | collective-permute-start | bytes 393224 | tf_op jit(solution)/shard_map/ppermute | solution.py:291
  39.3 9.8 %collective-permute-start.1 = (bf16[32,2048]{1,0:T(8,128)(2,1)S(1)}, bf16[32,2048]{1,0:T(8,128)(2,1)S(1)}, u32[]{:S(2)}, u32[]{:S(2)}) collective-permute-start(bf16[32,2048]{1,0:T(8,128)(2,1)S(1)} %get-tuple-element.30), channel_id=1, source_target_pairs={{0,16},{8,24},{16,0},{24,8},{1,17},{9,25},{17,1},{25,9},{2,18},{10... | collective-permute-start | bytes 393224 | tf_op jit(solution)/shard_map/ppermute | solution.py:291
  40.4 8.7 %collective-permute-start.2 = (bf16[32,2048]{1,0:T(8,128)(2,1)S(1)}, bf16[32,2048]{1,0:T(8,128)(2,1)S(1)}, u32[]{:S(2)}, u32[]{:S(2)}) collective-permute-start(bf16[32,2048]{1,0:T(8,128)(2,1)S(1)} %get-tuple-element.31), channel_id=1, source_target_pairs={{0,24},{8,16},{16,8},{24,0},{1,25},{9,17},{17,9},{25,1},{2,26},{10... | collective-permute-start | bytes 393224 | tf_op jit(solution)/shard_map/ppermute | solution.py:291
  45.5 18.4 %copy-start.2 = (bf16[1,1792,1024]{2,1,0:T(8,128)(2,1)S(1)}, bf16[1,1792,1024]{2,1,0:T(8,128)(2,1)}, u32[]{:S(2)}) copy-start(bf16[1,1792,1024]{2,1,0:T(8,128)(2,1)} %param.11) | copy-start | bytes 11010052
  45.5 5.0 %collective-permute-start.3 = (bf16[32,1024]{1,0:T(8,128)(2,1)S(1)}, bf16[32,1024]{1,0:T(8,128)(2,1)S(1)}, u32[]{:S(2)}, u32[]{:S(2)}) collective-permute-start(bf16[32,1024]{1,0:T(8,128)(2,1)S(1)} %get-tuple-element.33), channel_id=1, source_target_pairs={{0,8},{8,0},{16,24},{24,16},{1,9},{9,1},{17,25},{25,17},{2,10},{10... | collective-permute-start | bytes 196616 | tf_op jit(solution)/shard_map/ppermute | solution.py:291
  45.7 5.1 %collective-permute-start.4 = (bf16[32,1024]{1,0:T(8,128)(2,1)S(1)}, bf16[32,1024]{1,0:T(8,128)(2,1)S(1)}, u32[]{:S(2)}, u32[]{:S(2)}) collective-permute-start(bf16[32,1024]{1,0:T(8,128)(2,1)S(1)} %get-tuple-element.34), channel_id=1, source_target_pairs={{0,16},{8,24},{16,0},{24,8},{1,17},{9,25},{17,1},{25,9},{2,18},{10... | collective-permute-start | bytes 196616 | tf_op jit(solution)/shard_map/ppermute | solution.py:291
  46.7 5.3 %collective-permute-start.5 = (bf16[32,1024]{1,0:T(8,128)(2,1)S(1)}, bf16[32,1024]{1,0:T(8,128)(2,1)S(1)}, u32[]{:S(2)}, u32[]{:S(2)}) collective-permute-start(bf16[32,1024]{1,0:T(8,128)(2,1)S(1)} %get-tuple-element.35), channel_id=1, source_target_pairs={{0,24},{8,16},{16,8},{24,0},{1,25},{9,17},{17,9},{25,1},{2,26},{10... | collective-permute-start | bytes 196616 | tf_op jit(solution)/shard_map/ppermute | solution.py:291
  49.2 8.9 %collective-permute-start.10 = (bf16[32,1024]{1,0:T(8,128)(2,1)S(1)}, bf16[32,1024]{1,0:T(8,128)(2,1)S(1)}, u32[]{:S(2)}, u32[]{:S(2)}) collective-permute-start(bf16[32,1024]{1,0:T(8,128)(2,1)S(1)} %shard_map.112.refs_8_.refs_0_), channel_id=1, source_target_pairs={{0,16},{8,24},{16,0},{24,8},{1,17},{9,25},{17,1},{25,9},{2,18},{10... | collective-permute-start | bytes 196616 | tf_op jit(solution)/shard_map/ppermute | solution.py:291
  52.1 11.8 %collective-permute-start.6 = (bf16[32,2048]{1,0:T(8,128)(2,1)S(1)}, bf16[32,2048]{1,0:T(8,128)(2,1)S(1)}, u32[]{:S(2)}, u32[]{:S(2)}) collective-permute-start(bf16[32,2048]{1,0:T(8,128)(2,1)S(1)} %shard_map.113.refs_0_.refs_4_), channel_id=1, source_target_pairs={{0,8},{8,0},{16,24},{24,16},{1,9},{9,1},{17,25},{25,17},{2,10},{10... | collective-permute-start | bytes 393224 | tf_op jit(solution)/shard_map/ppermute | solution.py:291
  53.7 10.2 %collective-permute-start.7 = (bf16[32,2048]{1,0:T(8,128)(2,1)S(1)}, bf16[32,2048]{1,0:T(8,128)(2,1)S(1)}, u32[]{:S(2)}, u32[]{:S(2)}) collective-permute-start(bf16[32,2048]{1,0:T(8,128)(2,1)S(1)} %shard_map.113.refs_0_.refs_4_), channel_id=1, source_target_pairs={{0,16},{8,24},{16,0},{24,8},{1,17},{9,25},{17,1},{25,9},{2,18},{10... | collective-permute-start | bytes 393224 | tf_op jit(solution)/shard_map/ppermute | solution.py:291
  55.1 8.8 %collective-permute-start.8 = (bf16[32,2048]{1,0:T(8,128)(2,1)S(1)}, bf16[32,2048]{1,0:T(8,128)(2,1)S(1)}, u32[]{:S(2)}, u32[]{:S(2)}) collective-permute-start(bf16[32,2048]{1,0:T(8,128)(2,1)S(1)} %shard_map.113.refs_0_.refs_4_), channel_id=1, source_target_pairs={{0,24},{8,16},{16,8},{24,0},{1,25},{9,17},{17,9},{25,1},{2,26},{10... | collective-permute-start | bytes 393224 | tf_op jit(solution)/shard_map/ppermute | solution.py:291
  55.7 6.2 %collective-permute-start.11 = (bf16[32,1024]{1,0:T(8,128)(2,1)S(1)}, bf16[32,1024]{1,0:T(8,128)(2,1)S(1)}, u32[]{:S(2)}, u32[]{:S(2)}) collective-permute-start(bf16[32,1024]{1,0:T(8,128)(2,1)S(1)} %shard_map.112.refs_8_.refs_0_), channel_id=1, source_target_pairs={{0,24},{8,16},{16,8},{24,0},{1,25},{9,17},{17,9},{25,1},{2,26},{10... | collective-permute-start | bytes 196616 | tf_op jit(solution)/shard_map/ppermute | solution.py:291
  58.1 4.3 %collective-permute-start.9 = (bf16[32,1024]{1,0:T(8,128)(2,1)S(1)}, bf16[32,1024]{1,0:T(8,128)(2,1)S(1)}, u32[]{:S(2)}, u32[]{:S(2)}) collective-permute-start(bf16[32,1024]{1,0:T(8,128)(2,1)S(1)} %shard_map.112.refs_8_.refs_0_), channel_id=1, source_target_pairs={{0,8},{8,0},{16,24},{24,16},{1,9},{9,1},{17,25},{25,17},{2,10},{10... | collective-permute-start | bytes 196616 | tf_op jit(solution)/shard_map/ppermute | solution.py:291
  67.5 27.3 %all-to-all-start.1 = ((bf16[32,8,1792]{2,1,0:T(8,128)(2,1)}), bf16[32,8,1792]{2,1,0:T(8,128)(2,1)S(1)}, u32[]{:S(2)}, u32[]{:S(2)}) async-start(bf16[32,8,1792]{2,1,0:T(8,128)(2,1)} %bitcast.8), calls=%async_computation.1 | async-start | bytes 1835008 | tf_op jit(solution)/shard_map/all_to_all | solution.py:361

commit v4 on v3

--- a/solution.py
+++ b/solution.py
@@ -165,9 +165,19 @@
     )(me, in_hbm(ids), in_hbm(gates), in_hbm(tokens), in_hbm(cotangent))
 
 
-def finish_kernel(row_hot, grad_hot, row_gate, got, out, grad):
-    block = got[pl.program_id(0)]
-    out[...], grad[...] = combine(row_hot[...], grad_hot[...], row_gate[...], block)
+def finish_kernel(row_hot, grad_hot, row_gate, got, out, grad, held, sems):
+    parts, _, piece = got.shape
+    copies = []
+    for p in range(parts):
+        held[0, p], held[1, p] = combine(row_hot[...], grad_hot[...], row_gate[...], got[p])
+        for k, full in enumerate((out, grad)):
+            copy = pltpu.make_async_copy(
+                held.at[k, p], full.at[:, pl.ds(p * piece, piece)], sems.at[k, p]
+            )
+            copy.start()
+            copies.append(copy)
+    for copy in copies:
+        copy.wait()
 
 
 def finish(row_hot, grad_hot, row_gate, got):
@@ -175,14 +185,13 @@
     count = row_hot.shape[1]
     if piece % LANES:
         return combine(row_hot, grad_hot, row_gate, got.transpose(1, 0, 2).reshape(rows, parts * piece))
-    shape = like((count, parts * piece))
-    spec = pl.BlockSpec((count, piece), lambda p: (0, p))
+    shape = pltpu.HBM((count, parts * piece), BF16)
     return pl.pallas_call(
         finish_kernel,
         out_shape=(shape, shape),
-        grid=(parts,),
         in_specs=[IN_VMEM] * 4,
-        out_specs=(spec, spec),
+        out_specs=(IN_HBM, IN_HBM),
+        scratch_shapes=[pltpu.VMEM((2, parts, count, piece), BF16), DMA((2, parts))],
         compiler_params=ROOM,
         name="finish",
     )(row_hot, grad_hot, row_gate, got)
@@ -207,16 +216,12 @@
     blocks_of(jnp.concatenate([first, mm(part, held_up[...]).astype(BF16)], axis=1), sent)
 
 
-def grads_kernel(parts, me, got, down, rows, *rest):
-    sent, (held_down, sem) = rest[:parts], rest[parts:]
-    fetch = pltpu.make_async_copy(down, held_down, sem)
-    fetch.start()
+def grads_kernel(parts, me, got, down, rows, *sent):
     count = rows.shape[0]
     _, pick = pickers(count, me[0], count // parts)
     part = mm(pick, got[...]).astype(BF16)
     rows[...] = part
-    fetch.wait()
-    blocks_of(mm(part, held_down[...]).astype(BF16), sent)
+    blocks_of(mm(part, down[...]).astype(BF16), sent)
 
 
 def hidden_kernel(hidden, count, *refs):
@@ -233,22 +238,31 @@
     return jnp.concatenate([ref[...] for ref in refs], axis=0)
 
 
+def weave(count, me, group):
+    row = iota((2 * count, 2 * count), 0)
+    kind = row // CAP % 2
+    place = row // (2 * CAP) * CAP + row % CAP
+    source = kind * count + ((place // group) ^ me) * group + place % group
+    return (iota((2 * count, 2 * count), 1) == source).astype(F32).astype(BF16)
+
+
 def output_kernel(parts, me, *refs):
     active = stacked(refs[:parts])
-    down, out = refs[parts:]
-    pick, _ = pickers(active.shape[0], me[0], active.shape[0] // parts)
-    spread = mm(pick, active, 0, 0).astype(BF16)
-    out[...] = mm(down[...], spread, 1, 1).astype(BF16).T
-
-
-def back_kernel(parts, me, *refs):
+    down, gate, up, out, gate_turned, up_turned, woven = refs[parts:]
+    count = active.shape[0]
+    out[...] = mm(active, down[...], 1, 1).astype(BF16)
+    woven[...] = weave(count, me[0], count // parts)
+    gate_turned[...] = gate[...].T
+    up_turned[...] = up[...].T
+
+
+def back_kernel(parts, *refs):
     acts = stacked(refs[:parts])
-    gate, up, first, out = refs[parts:]
-    hidden = gate.shape[1]
-    _, pick = pickers(acts.shape[0], me[0], acts.shape[0] // parts)
-    spread = mm(pick, acts, 0, 0).astype(BF16)
-    total = mm(gate[...], spread[:, :hidden], 1, 1) + mm(up[...], spread[:, hidden:], 1, 1)
-    out[...] = total.astype(BF16).T + first[...]
+    gate_turned, up_turned, first, woven, out = refs[parts:]
+    hidden = gate_turned.shape[0]
+    total = mm(acts[:, :hidden], gate_turned[...]) + mm(acts[:, hidden:], up_turned[...])
+    both = jnp.concatenate([first[...], total.astype(BF16)], axis=0)
+    out[...] = mm(woven[...], both).astype(BF16)
 
 
 def weights_kernel(parts, rows, grads, *refs):
@@ -311,20 +325,17 @@
         scratch=held,
     )
     pre = to_all(sent)
-    grads, *sent = run(
-        part(grads_kernel, parts),
-        ((count, piece),) + ((group, hidden),) * parts,
-        (me, got, down),
-        hbm=(2,),
-        scratch=held,
-    )
+    grads, *sent = run(part(grads_kernel, parts), ((count, piece),) + ((group, hidden),) * parts, (me, got, down))
     hidden_grad = to_all(sent)
     (active,) = run(part(hidden_kernel, hidden, parts), ((group, hidden),), (*pre, sent[0]))
     actives = to_all([active] * parts)
     (acts,) = run(part(grad_kernel, hidden, parts), ((group, 2 * hidden),), (*pre, *hidden_grad, active))
     acts = to_all([acts] * parts)
-    (first,) = run(part(output_kernel, parts), ((total, piece),), (me, *actives, down))
-    (back,) = run(part(back_kernel, parts), ((total, piece),), (me, *acts, gate, up, first))
+    turned = (hidden, piece)
+    first, gate_turned, up_turned, woven = run(
+        part(output_kernel, parts), ((count, piece), turned, turned, (total, total)), (me, *actives, down, gate, up)
+    )
+    (back,) = run(part(back_kernel, parts), ((total, piece),), (*acts, gate_turned, up_turned, first, woven))
 
     step = 2 * LANES
     spec = pl.BlockSpec((step, hidden), lambda d: (d, 0))

time: 98.2 us -> 96.2 us (0.980)
  Pallas kernels: 23.8 us -> 21.2 us
    pallas_call x6, Pallas kernels: 11.5 us -> 9.49 us  [run(): pl.pallas_call(kernel, out_shape=tuple((like(shape) for shape in outs)),...]
  transfers between devices with their start and end apart: 13 -> 13, of which waited for: 6 -> 6; matrix products, arithmetic and copies ran while one was open for 0% -> 0% of each run, Pallas kernels for 11% -> 10%
where the time goes in v4:
time: 96.2 us; the launch traced here: 96 us
  blocking collectives  31.8 us (33%)
  waiting for transfers between devices  25.7 us (27%)
  Pallas kernels  21.2 us (22%)
  starting transfers between devices  16.6 us (17%)
    all_to_all x1, blocking collectives, body(): got = lax.all_to_all(sent, both, 0, 0, tiled=True)  31.8 us
    all_to_all x1, waiting for transfers between devices, body(): lax.all_to_all(back.reshape(parts * experts, block, piece), both, 0, 0, t...  18.7 us
    ppermute x12, starting transfers between devices, to_all(): lax.ppermute(blocks[k], 'dp', [(i, i ^ k) for i in range(parts)])  14 us
    pallas_call x6, Pallas kernels, run(): pl.pallas_call(kernel, out_shape=tuple((like(shape) for shape in outs)),...  9.49 us
    ppermute x12, waiting for transfers between devices, to_all(): lax.ppermute(blocks[k], 'dp', [(i, i ^ k) for i in range(parts)])  6.97 us
    pallas_call x1, Pallas kernels, tiled_middle(): pl.pallas_call(part(weights_kernel, parts), out_shape=(like((piece, hidde...  5.91 us
    pallas_call x1, Pallas kernels, prep(): pl.pallas_call(functools.partial(prep_kernel, experts), out_shape=(like((...  3.41 us
    all_to_all x1, starting transfers between devices, body(): lax.all_to_all(back.reshape(parts * experts, block, piece), both, 0, 0, t...  2.64 us
  transfers between devices with their start and end apart: 13, of which 6 were waited for; matrix products, arithmetic and copies ran while one was open for 0% of the time, Pallas kernels for 10%

profile of v4, /device:TPU:0, one launch (start us, length us, event | category | flops | bytes accessed | tf_op | source)
XLA Modules:
  0.0 96.0 jit_solution(13840173448814863985)
XLA Ops:
  0.6 0.0 copy-start
  0.6 3.4 %prep.1 = (bf16[4,64,1792]{2,1,0:T(8,128)(2,1)S(1)}, bf16[64,128]{1,0:T(8,128)(2,1)S(1)}, bf16[64,128]{1,0:T(8,128)(2,1)S(1)}, f32[64,1]{1,0:T(8,128)S(1)}) custom-call(s32[1]{0:T(128)} %bitcast.me, s32[8,128]{1,0:T(8,128)} %bitcast.23, f32[8,128]{1,0:T(8,128)} %bitcast.24, bf16[128,7168]{1,0:T(8,128)(2,1)} %tokens.1, bf16[128,7168]{1,0:T(8,128)(2,1)} %cotangent.1), custom_call_target="tpu_custom_call" | custom-call | tf_op jit(solution)/shard_map/prep/pallas_call | solution.py:157
  4.1 31.8 %all_to_all.10 = bf16[32,8,1792]{2,1,0:T(8,128)(2,1)S(1)} all-to-all(bf16[32,8,1792]{2,1,0:T(8,128)(2,1)S(1)} %bitcast.22), channel_id=1, replica_groups=mesh['dp'=4,'expert'=8] {'dp','expert'}, dimensions={0} | all-to-all | bytes 1835008 | tf_op jit(solution)/shard_map/all_to_all | solution.py:368
  35.9 0.0 copy-done
  35.9 0.0 copy-start.2
  35.9 3.7 %shard_map.110 = (bf16[128,1792]{1,0:T(8,128)(2,1)S(1)}, bf16[32,2048]{1,0:T(8,128)(2,1)S(1)}, bf16[32,2048]{1,0:T(8,128)(2,1)S(1)}, bf16[32,2048]{1,0:T(8,128)(2,1)S(1)}, bf16[32,2048]{1,0:T(8,128)(2,1)S(1)}) custom-call(s32[1]{0:T(128)} %bitcast.me, bf16[256,1792]{1,0:T(8,128)(2,1)S(1)} %bitcast.19, bf16[1792,1024]{1,0:T(8,128)(2,1)S(1)} %bitcast.13, ...), custom_call_target="tpu_custom_call" | custom-call | tf_op jit(solution)/shard_map/pallas_call | solution.py:292
  39.6 0.0 copy-start.1
  39.6 0.1 collective-permute-start
  39.7 1.1 %collective-permute-start.1 = (bf16[32,2048]{1,0:T(8,128)(2,1)S(1)}, bf16[32,2048]{1,0:T(8,128)(2,1)S(1)}, u32[]{:S(2)}, u32[]{:S(2)}) collective-permute-start(bf16[32,2048]{1,0:T(8,128)(2,1)S(1)} %get-tuple-element.34), channel_id=1, source_target_pairs={{0,16},{8,24},{16,0},{24,8},{1,17},{9,25},{17,1},{25,9},{2,18},{10... | collective-permute-start | bytes 393224 | tf_op jit(solution)/shard_map/ppermute | solution.py:305
  40.8 2.4 %collective-permute-start.2 = (bf16[32,2048]{1,0:T(8,128)(2,1)S(1)}, bf16[32,2048]{1,0:T(8,128)(2,1)S(1)}, u32[]{:S(2)}, u32[]{:S(2)}) collective-permute-start(bf16[32,2048]{1,0:T(8,128)(2,1)S(1)} %get-tuple-element.35), channel_id=1, source_target_pairs={{0,24},{8,16},{16,8},{24,0},{1,25},{9,17},{17,9},{25,1},{2,26},{10... | collective-permute-start | bytes 393224 | tf_op jit(solution)/shard_map/ppermute | solution.py:305
  43.1 0.0 copy-done.2
  43.1 0.8 shard_map.111
  43.9 0.1 collective-permute-start.3
  44.1 1.0 %collective-permute-start.4 = (bf16[32,1024]{1,0:T(8,128)(2,1)S(1)}, bf16[32,1024]{1,0:T(8,128)(2,1)S(1)}, u32[]{:S(2)}, u32[]{:S(2)}) collective-permute-start(bf16[32,1024]{1,0:T(8,128)(2,1)S(1)} %get-tuple-element.38), channel_id=1, source_target_pairs={{0,16},{8,24},{16,0},{24,8},{1,17},{9,25},{17,1},{25,9},{2,18},{10... | collective-permute-start | bytes 196616 | tf_op jit(solution)/shard_map/ppermute | solution.py:305
  45.1 0.4 collective-permute-done.refs_1_
  45.5 2.0 %collective-permute-start.5 = (bf16[32,1024]{1,0:T(8,128)(2,1)S(1)}, bf16[32,1024]{1,0:T(8,128)(2,1)S(1)}, u32[]{:S(2)}, u32[]{:S(2)}) collective-permute-start(bf16[32,1024]{1,0:T(8,128)(2,1)S(1)} %get-tuple-element.39), channel_id=1, source_target_pairs={{0,24},{8,16},{16,8},{24,0},{1,25},{9,17},{17,9},{25,1},{2,26},{10... | collective-permute-start | bytes 196616 | tf_op jit(solution)/shard_map/ppermute | solution.py:305
  47.5 1.1 %collective-permute-done.1.refs_2_ = bf16[32,2048]{1,0:T(8,128)(2,1)S(1)} collective-permute-done((bf16[32,2048]{1,0:T(8,128)(2,1)S(1)}, bf16[32,2048]{1,0:T(8,128)(2,1)S(1)}, u32[]{:S(2)}, u32[]{:S(2)}) %collective-permute-start.1) | collective-permute-done | bytes 131104 | tf_op jit(solution)/shard_map/ppermute | solution.py:305
  48.6 0.2 collective-permute-done.2.refs_3_
  48.8 0.1 shard_map.112.refs_8_.refs_0_
  48.9 1.7 %collective-permute-start.11 = (bf16[32,1024]{1,0:T(8,128)(2,1)S(1)}, bf16[32,1024]{1,0:T(8,128)(2,1)S(1)}, u32[]{:S(2)}, u32[]{:S(2)}) collective-permute-start(bf16[32,1024]{1,0:T(8,128)(2,1)S(1)} %shard_map.112.refs_8_.refs_0_), channel_id=1, source_target_pairs={{0,24},{8,16},{16,8},{24,0},{1,25},{9,17},{17,9},{25,1},{2,26},{10... | collective-permute-start | bytes 196616 | tf_op jit(solution)/shard_map/ppermute | solution.py:305
  50.6 0.0 collective-permute-done.3.refs_5_
  50.6 0.7 collective-permute-done.4.refs_6_
  51.3 0.0 collective-permute-done.5.refs_7_
  51.3 0.1 shard_map.113.refs_0_.refs_4_
  51.5 1.5 %collective-permute-start.8 = (bf16[32,2048]{1,0:T(8,128)(2,1)S(1)}, bf16[32,2048]{1,0:T(8,128)(2,1)S(1)}, u32[]{:S(2)}, u32[]{:S(2)}) collective-permute-start(bf16[32,2048]{1,0:T(8,128)(2,1)S(1)} %shard_map.113.refs_0_.refs_4_), channel_id=1, source_target_pairs={{0,24},{8,16},{16,8},{24,0},{1,25},{9,17},{17,9},{25,1},{2,26},{10... | collective-permute-start | bytes 393224 | tf_op jit(solution)/shard_map/ppermute | solution.py:305
  53.0 1.6 %collective-permute-start.7 = (bf16[32,2048]{1,0:T(8,128)(2,1)S(1)}, bf16[32,2048]{1,0:T(8,128)(2,1)S(1)}, u32[]{:S(2)}, u32[]{:S(2)}) collective-permute-start(bf16[32,2048]{1,0:T(8,128)(2,1)S(1)} %shard_map.113.refs_0_.refs_4_), channel_id=1, source_target_pairs={{0,16},{8,24},{16,0},{24,8},{1,17},{9,25},{17,1},{25,9},{2,18},{10... | collective-permute-start | bytes 393224 | tf_op jit(solution)/shard_map/ppermute | solution.py:305
  54.6 0.4 collective-permute-start.6
  55.0 0.7 collective-permute-start.10
  55.8 0.0 collective-permute-done.11.refs_3_
  55.8 1.3 %collective-permute-start.9 = (bf16[32,1024]{1,0:T(8,128)(2,1)S(1)}, bf16[32,1024]{1,0:T(8,128)(2,1)S(1)}, u32[]{:S(2)}, u32[]{:S(2)}) collective-permute-start(bf16[32,1024]{1,0:T(8,128)(2,1)S(1)} %shard_map.112.refs_8_.refs_0_), channel_id=1, source_target_pairs={{0,8},{8,0},{16,24},{24,16},{1,9},{9,1},{17,25},{25,17},{2,10},{10... | collective-permute-start | bytes 196616 | tf_op jit(solution)/shard_map/ppermute | solution.py:305
  57.1 4.5 %collective-permute-done.10.refs_2_ = bf16[32,1024]{1,0:T(8,128)(2,1)S(1)} collective-permute-done((bf16[32,1024]{1,0:T(8,128)(2,1)S(1)}, bf16[32,1024]{1,0:T(8,128)(2,1)S(1)}, u32[]{:S(2)}, u32[]{:S(2)}) %collective-permute-start.10) | collective-permute-done | bytes 65568 | tf_op jit(solution)/shard_map/ppermute | solution.py:305
  61.6 0.0 collective-permute-done.9.refs_1_
  61.6 0.0 copy-done.1
  61.6 2.4 %shard_map.114 = (bf16[128,1792]{1,0:T(8,128)(2,1)S(1)}, bf16[1024,1792]{1,0:T(8,128)(2,1)S(1)}, bf16[1024,1792]{1,0:T(8,128)(2,1)S(1)}, bf16[256,256]{1,0:T(8,128)(2,1)S(1)}) custom-call(s32[1]{0:T(128)} %bitcast.me, bf16[32,1024]{1,0:T(8,128)(2,1)S(1)} %shard_map.112.refs_8_.refs_0_, bf16[32,1024]{1,0:T(8,128)(2,1)S(1)} %collective-permute-done.9.refs_1_, ...), custom_call_target="tpu_custom_call" | custom-call | tf_op jit(solution)/shard_map/pallas_call | solution.py:292
  64.0 0.0 collective-permute-done.8.refs_3_.refs_7_
  64.0 0.0 collective-permute-done.7.refs_2_.refs_6_
  64.0 0.0 collective-permute-done.6.refs_1_.refs_5_
  64.0 2.3 %shard_map.115 = bf16[256,1792]{1,0:T(8,128)(2,1)} custom-call(bf16[32,2048]{1,0:T(8,128)(2,1)S(1)} %shard_map.113.refs_0_.refs_4_, bf16[32,2048]{1,0:T(8,128)(2,1)S(1)} %collective-permute-done.6.refs_1_.refs_5_, bf16[32,2048]{1,0:T(8,128)(2,1)S(1)} %collective-permute-done.7.refs_2_.refs_6_, bf16[32,2048]{1,0:T(8,128)(2,1)S(1)} %collective-permute-done.8.refs_3_.refs_7_, ...), custom_call_target="tpu_custom_call" | custom-call | tf_op jit(solution)/shard_map/pallas_call | solution.py:292
  66.4 2.6 %all-to-all-start.1 = ((bf16[32,8,1792]{2,1,0:T(8,128)(2,1)}), bf16[32,8,1792]{2,1,0:T(8,128)(2,1)S(1)}, u32[]{:S(2)}, u32[]{:S(2)}) async-start(bf16[32,8,1792]{2,1,0:T(8,128)(2,1)} %bitcast.8), calls=%async_computation.1 | async-start | bytes 1835008 | tf_op jit(solution)/shard_map/all_to_all | solution.py:372
  69.0 5.9 %weights.1 = (bf16[1792,1024]{1,0:T(8,128)(2,1)}, bf16[1792,1024]{1,0:T(8,128)(2,1)}, bf16[1792,1024]{1,0:T(8,128)(2,1)}) custom-call(bf16[128,1792]{1,0:T(8,128)(2,1)S(1)} %get-tuple-element.46.rows, bf16[128,1792]{1,0:T(8,128)(2,1)S(1)} %get-tuple-element.47.grads, bf16[32,1024]{1,0:T(8,128)(2,1)S(1)} %shard_map.112.refs_8_.refs_0_, ...), custom_call_target="tpu_custom_call" | custom-call | tf_op jit(solution)/shard_map/weights/pallas_call | solution.py:343
  74.9 18.7 %all-to-all-done.1 = bf16[32,8,1792]{2,1,0:T(8,128)(2,1)S(1)} async-done(((bf16[32,8,1792]{2,1,0:T(8,128)(2,1)}), bf16[32,8,1792]{2,1,0:T(8,128)(2,1)S(1)}, u32[]{:S(2)}, u32[]{:S(2)}) %all-to-all-start.1) | async-done | bytes 917536 | tf_op jit(solution)/shard_map/all_to_all | solution.py:372
  93.7 2.4 %finish.1 = (bf16[128,7168]{1,0:T(8,128)(2,1)}, bf16[128,7168]{1,0:T(8,128)(2,1)}) custom-call(bf16[64,128]{1,0:T(8,128)(2,1)S(1)} %get-tuple-element.28.row_hot, bf16[64,128]{1,0:T(8,128)(2,1)S(1)} %get-tuple-element.29.grad_hot, f32[64,1]{1,0:T(8,128)S(1)} %get-tuple-element.30.row_gate, bf16[4,64,1792]{2,1,0:T(8,128)(2,1)S(1)} %bitcast.21), custom_call_target="tpu_custom_call" | custom-call | tf_op jit(solution)/shard_map/finish/pallas_call | solution.py:189
Async XLA Ops:
  0.6 35.2 %copy-start = (bf16[1,1792,1024]{2,1,0:T(8,128)(2,1)S(1)}, bf16[1,1792,1024]{2,1,0:T(8,128)(2,1)}, u32[]{:S(2)}) copy-start(bf16[1,1792,1024]{2,1,0:T(8,128)(2,1)} %param.10) | copy-start | bytes 11010052
  35.9 7.3 %copy-start.2 = (bf16[1,1792,1024]{2,1,0:T(8,128)(2,1)S(1)}, bf16[1,1792,1024]{2,1,0:T(8,128)(2,1)}, u32[]{:S(2)}) copy-start(bf16[1,1792,1024]{2,1,0:T(8,128)(2,1)} %param.12) | copy-start | bytes 11010052
  39.6 22.0 %copy-start.1 = (bf16[1,1792,1024]{2,1,0:T(8,128)(2,1)S(1)}, bf16[1,1792,1024]{2,1,0:T(8,128)(2,1)}, u32[]{:S(2)}) copy-start(bf16[1,1792,1024]{2,1,0:T(8,128)(2,1)} %param.11) | copy-start | bytes 11010052
  39.6 5.9 %collective-permute-start = (bf16[32,2048]{1,0:T(8,128)(2,1)S(1)}, bf16[32,2048]{1,0:T(8,128)(2,1)S(1)}, u32[]{:S(2)}, u32[]{:S(2)}) collective-permute-start(bf16[32,2048]{1,0:T(8,128)(2,1)S(1)} %get-tuple-element.33), channel_id=1, source_target_pairs={{0,8},{8,0},{16,24},{24,16},{1,9},{9,1},{17,25},{25,17},{2,10},{10... | collective-permute-start | bytes 393224 | tf_op jit(solution)/shard_map/ppermute | solution.py:305
  39.7 8.9 %collective-permute-start.1 = (bf16[32,2048]{1,0:T(8,128)(2,1)S(1)}, bf16[32,2048]{1,0:T(8,128)(2,1)S(1)}, u32[]{:S(2)}, u32[]{:S(2)}) collective-permute-start(bf16[32,2048]{1,0:T(8,128)(2,1)S(1)} %get-tuple-element.34), channel_id=1, source_target_pairs={{0,16},{8,24},{16,0},{24,8},{1,17},{9,25},{17,1},{25,9},{2,18},{10... | collective-permute-start | bytes 393224 | tf_op jit(solution)/shard_map/ppermute | solution.py:305
  40.8 8.1 %collective-permute-start.2 = (bf16[32,2048]{1,0:T(8,128)(2,1)S(1)}, bf16[32,2048]{1,0:T(8,128)(2,1)S(1)}, u32[]{:S(2)}, u32[]{:S(2)}) collective-permute-start(bf16[32,2048]{1,0:T(8,128)(2,1)S(1)} %get-tuple-element.35), channel_id=1, source_target_pairs={{0,24},{8,16},{16,8},{24,0},{1,25},{9,17},{17,9},{25,1},{2,26},{10... | collective-permute-start | bytes 393224 | tf_op jit(solution)/shard_map/ppermute | solution.py:305
  43.9 6.7 %collective-permute-start.3 = (bf16[32,1024]{1,0:T(8,128)(2,1)S(1)}, bf16[32,1024]{1,0:T(8,128)(2,1)S(1)}, u32[]{:S(2)}, u32[]{:S(2)}) collective-permute-start(bf16[32,1024]{1,0:T(8,128)(2,1)S(1)} %get-tuple-element.37), channel_id=1, source_target_pairs={{0,8},{8,0},{16,24},{24,16},{1,9},{9,1},{17,25},{25,17},{2,10},{10... | collective-permute-start | bytes 196616 | tf_op jit(solution)/shard_map/ppermute | solution.py:305
  44.1 7.2 %collective-permute-start.4 = (bf16[32,1024]{1,0:T(8,128)(2,1)S(1)}, bf16[32,1024]{1,0:T(8,128)(2,1)S(1)}, u32[]{:S(2)}, u32[]{:S(2)}) collective-permute-start(bf16[32,1024]{1,0:T(8,128)(2,1)S(1)} %get-tuple-element.38), channel_id=1, source_target_pairs={{0,16},{8,24},{16,0},{24,8},{1,17},{9,25},{17,1},{25,9},{2,18},{10... | collective-permute-start | bytes 196616 | tf_op jit(solution)/shard_map/ppermute | solution.py:305
  45.5 5.8 %collective-permute-start.5 = (bf16[32,1024]{1,0:T(8,128)(2,1)S(1)}, bf16[32,1024]{1,0:T(8,128)(2,1)S(1)}, u32[]{:S(2)}, u32[]{:S(2)}) collective-permute-start(bf16[32,1024]{1,0:T(8,128)(2,1)S(1)} %get-tuple-element.39), channel_id=1, source_target_pairs={{0,24},{8,16},{16,8},{24,0},{1,25},{9,17},{17,9},{25,1},{2,26},{10... | collective-permute-start | bytes 196616 | tf_op jit(solution)/shard_map/ppermute | solution.py:305
  48.9 6.9 %collective-permute-start.11 = (bf16[32,1024]{1,0:T(8,128)(2,1)S(1)}, bf16[32,1024]{1,0:T(8,128)(2,1)S(1)}, u32[]{:S(2)}, u32[]{:S(2)}) collective-permute-start(bf16[32,1024]{1,0:T(8,128)(2,1)S(1)} %shard_map.112.refs_8_.refs_0_), channel_id=1, source_target_pairs={{0,24},{8,16},{16,8},{24,0},{1,25},{9,17},{17,9},{25,1},{2,26},{10... | collective-permute-start | bytes 196616 | tf_op jit(solution)/shard_map/ppermute | solution.py:305
  51.5 12.5 %collective-permute-start.8 = (bf16[32,2048]{1,0:T(8,128)(2,1)S(1)}, bf16[32,2048]{1,0:T(8,128)(2,1)S(1)}, u32[]{:S(2)}, u32[]{:S(2)}) collective-permute-start(bf16[32,2048]{1,0:T(8,128)(2,1)S(1)} %shard_map.113.refs_0_.refs_4_), channel_id=1, source_target_pairs={{0,24},{8,16},{16,8},{24,0},{1,25},{9,17},{17,9},{25,1},{2,26},{10... | collective-permute-start | bytes 393224 | tf_op jit(solution)/shard_map/ppermute | solution.py:305
  53.0 11.0 %collective-permute-start.7 = (bf16[32,2048]{1,0:T(8,128)(2,1)S(1)}, bf16[32,2048]{1,0:T(8,128)(2,1)S(1)}, u32[]{:S(2)}, u32[]{:S(2)}) collective-permute-start(bf16[32,2048]{1,0:T(8,128)(2,1)S(1)} %shard_map.113.refs_0_.refs_4_), channel_id=1, source_target_pairs={{0,16},{8,24},{16,0},{24,8},{1,17},{9,25},{17,1},{25,9},{2,18},{10... | collective-permute-start | bytes 393224 | tf_op jit(solution)/shard_map/ppermute | solution.py:305
  54.6 9.4 %collective-permute-start.6 = (bf16[32,2048]{1,0:T(8,128)(2,1)S(1)}, bf16[32,2048]{1,0:T(8,128)(2,1)S(1)}, u32[]{:S(2)}, u32[]{:S(2)}) collective-permute-start(bf16[32,2048]{1,0:T(8,128)(2,1)S(1)} %shard_map.113.refs_0_.refs_4_), channel_id=1, source_target_pairs={{0,8},{8,0},{16,24},{24,16},{1,9},{9,1},{17,25},{25,17},{2,10},{10... | collective-permute-start | bytes 393224 | tf_op jit(solution)/shard_map/ppermute | solution.py:305
  55.0 6.5 %collective-permute-start.10 = (bf16[32,1024]{1,0:T(8,128)(2,1)S(1)}, bf16[32,1024]{1,0:T(8,128)(2,1)S(1)}, u32[]{:S(2)}, u32[]{:S(2)}) collective-permute-start(bf16[32,1024]{1,0:T(8,128)(2,1)S(1)} %shard_map.112.refs_8_.refs_0_), channel_id=1, source_target_pairs={{0,16},{8,24},{16,0},{24,8},{1,17},{9,25},{17,1},{25,9},{2,18},{10... | collective-permute-start | bytes 196616 | tf_op jit(solution)/shard_map/ppermute | solution.py:305
  55.8 5.8 %collective-permute-start.9 = (bf16[32,1024]{1,0:T(8,128)(2,1)S(1)}, bf16[32,1024]{1,0:T(8,128)(2,1)S(1)}, u32[]{:S(2)}, u32[]{:S(2)}) collective-permute-start(bf16[32,1024]{1,0:T(8,128)(2,1)S(1)} %shard_map.112.refs_8_.refs_0_), channel_id=1, source_target_pairs={{0,8},{8,0},{16,24},{24,16},{1,9},{9,1},{17,25},{25,17},{2,10},{10... | collective-permute-start | bytes 196616 | tf_op jit(solution)/shard_map/ppermute | solution.py:305
  66.4 27.3 %all-to-all-start.1 = ((bf16[32,8,1792]{2,1,0:T(8,128)(2,1)}), bf16[32,8,1792]{2,1,0:T(8,128)(2,1)S(1)}, u32[]{:S(2)}, u32[]{:S(2)}) async-start(bf16[32,8,1792]{2,1,0:T(8,128)(2,1)} %bitcast.8), calls=%async_computation.1 | async-start | bytes 1835008 | tf_op jit(solution)/shard_map/all_to_all | solution.py:372

commit v5 on v4

--- a/solution.py
+++ b/solution.py
@@ -81,7 +81,7 @@
     return jnp.concatenate([gate_grad.astype(BF16), up_grad.astype(BF16)], axis=1)
 
 
-def plain_middle(me, got, gate, up, down):
+def plain_middle(got, gate, up, down):
     count = got.shape[0] // 2
     hidden = gate.shape[1]
     pick_row, pick_grad = pickers(count)
@@ -111,7 +111,6 @@
 ROOM = pltpu.CompilerParams(vmem_limit_bytes=16 * 2**20)
 IN_VMEM = pl.BlockSpec(memory_space=pltpu.VMEM)
 IN_HBM = pl.BlockSpec(memory_space=pltpu.HBM)
-IN_SMEM = pl.BlockSpec(memory_space=pltpu.SMEM)
 DMA = pltpu.SemaphoreType.DMA
 
 
@@ -123,9 +122,27 @@
     return jax.ShapeDtypeStruct(shape, BF16)
 
 
-def prep_kernel(experts, me, ids, gates, tokens, cotangent, out, row_hot, grad_hot, row_gate, held, sems):
-    del me
+def prep_kernel(
+    experts,
+    ids,
+    gates,
+    tokens,
+    cotangent,
+    out,
+    row_hot,
+    grad_hot,
+    row_gate,
+    held_ids,
+    held_gates,
+    held,
+    small,
+    sems,
+):
     parts, _, piece = out.shape
+    routes = [
+        pltpu.make_async_copy(ids, held_ids, small.at[0]),
+        pltpu.make_async_copy(gates, held_gates, small.at[1]),
+    ]
     copies = [
         [
             pltpu.make_async_copy(
@@ -135,17 +152,20 @@
         ]
         for p in range(parts)
     ]
-    for pair in copies:
-        for copy in pair:
-            copy.start()
-    row_hot[...], grad_hot[...], row_gate[...], grad_gate = slots_of(ids[...], gates[...], experts)
+    for copy in routes + [copy for pair in copies for copy in pair]:
+        copy.start()
+    for copy in routes:
+        copy.wait()
+    row_hot[...], grad_hot[...], row_gate[...], grad_gate = slots_of(
+        held_ids[...], held_gates[...], experts
+    )
     for p, pair in enumerate(copies):
         for copy in pair:
             copy.wait()
         out[p] = fill_rows(row_hot[...], grad_hot[...], grad_gate, held[0, p], held[1, p])
 
 
-def prep(me, ids, gates, tokens, cotangent, experts, parts):
+def prep(ids, gates, tokens, cotangent, experts, parts):
     count, width = tokens.shape
     piece = width // parts
     rows = experts * 2 * CAP
@@ -157,12 +177,18 @@
     return pl.pallas_call(
         functools.partial(prep_kernel, experts),
         out_shape=(like((parts, rows, piece)), hot, hot, jax.ShapeDtypeStruct((rows, 1), F32)),
-        in_specs=[IN_SMEM, IN_VMEM, IN_VMEM, IN_HBM, IN_HBM],
+        in_specs=[IN_HBM] * 4,
         out_specs=(IN_VMEM,) * 4,
-        scratch_shapes=[pltpu.VMEM((2, parts, count, piece), BF16), DMA((2, parts))],
+        scratch_shapes=[
+            pltpu.VMEM(ids.shape, ids.dtype),
+            pltpu.VMEM(gates.shape, gates.dtype),
+            pltpu.VMEM((2, parts, count, piece), BF16),
+            DMA((2,)),
+            DMA((2, parts)),
+        ],
         compiler_params=ROOM,
         name="prep",
-    )(me, in_hbm(ids), in_hbm(gates), in_hbm(tokens), in_hbm(cotangent))
+    )(in_hbm(ids), in_hbm(gates), in_hbm(tokens), in_hbm(cotangent))
 
 
 def finish_kernel(row_hot, grad_hot, row_gate, got, out, grad, held, sems):
@@ -203,25 +229,29 @@
         ref[...] = value[k * group : (k + 1) * group]
 
 
-def rows_kernel(parts, me, got, gate, up, rows, *rest):
-    sent, (held_up, sem) = rest[:parts], rest[parts:]
+def rows_kernel(parts, got, gate, up, rows, held_up, *rest):
+    sent, sem = rest[:parts], rest[parts]
     fetch = pltpu.make_async_copy(up, held_up, sem)
     fetch.start()
-    count = rows.shape[0]
-    pick, _ = pickers(count, me[0], count // parts)
+    count, hidden = rows.shape[0], gate.shape[1]
+    pick, _ = pickers(count, lax.axis_index("dp"), count // parts)
     part = mm(pick, got[...]).astype(BF16)
     rows[...] = part
-    first = mm(part, gate[...]).astype(BF16)
+    blocks_of(mm(part, gate[...]).astype(BF16), [ref.at[:, :hidden] for ref in sent])
     fetch.wait()
-    blocks_of(jnp.concatenate([first, mm(part, held_up[...]).astype(BF16)], axis=1), sent)
-
-
-def grads_kernel(parts, me, got, down, rows, *sent):
+    blocks_of(mm(part, held_up[...]).astype(BF16), [ref.at[:, hidden:] for ref in sent])
+
+
+def grads_kernel(parts, got, down, after, rows, held_down, *rest):
+    sent, sem = rest[:parts], rest[parts]
+    fetch = pltpu.make_async_copy(down, held_down, sem)
+    fetch.start()
     count = rows.shape[0]
-    _, pick = pickers(count, me[0], count // parts)
+    _, pick = pickers(count, lax.axis_index("dp"), count // parts)
     part = mm(pick, got[...]).astype(BF16)
     rows[...] = part
-    blocks_of(mm(part, down[...]).astype(BF16), sent)
+    fetch.wait()
+    blocks_of(mm(part, held_down[...]).astype(BF16), sent)
 
 
 def hidden_kernel(hidden, count, *refs):
@@ -246,12 +276,12 @@
     return (iota((2 * count, 2 * count), 1) == source).astype(F32).astype(BF16)
 
 
-def output_kernel(parts, me, *refs):
+def output_kernel(parts, *refs):
     active = stacked(refs[:parts])
     down, gate, up, out, gate_turned, up_turned, woven = refs[parts:]
     count = active.shape[0]
     out[...] = mm(active, down[...], 1, 1).astype(BF16)
-    woven[...] = weave(count, me[0], count // parts)
+    woven[...] = weave(count, lax.axis_index("dp"), count // parts)
     gate_turned[...] = gate[...].T
     up_turned[...] = up[...].T
 
@@ -281,14 +311,7 @@
 
 
 def run(kernel, outs, args, hbm=(), scratch=()):
-    specs = [
-        IN_SMEM
-        if x.shape == (1,)
-        else IN_HBM
-        if i in hbm
-        else IN_VMEM
-        for i, x in enumerate(args)
-    ]
+    specs = [IN_HBM if i in hbm else IN_VMEM for i in range(len(args))]
     return pl.pallas_call(
         kernel,
         out_shape=tuple(like(shape) for shape in outs),
@@ -308,7 +331,7 @@
     return [blocks[0]] + [moved[k] for k in range(1, parts)]
 
 
-def tiled_middle(me, got, gate, up, down):
+def tiled_middle(got, gate, up, down):
     total, piece = got.shape
     count = total // 2
     hidden = gate.shape[1]
@@ -316,26 +339,37 @@
     group = count // parts
     part = functools.partial
 
-    held = [pltpu.VMEM((piece, hidden), BF16), DMA]
-    rows, *sent = run(
+    rows, up, *sent = run(
         part(rows_kernel, parts),
-        ((count, piece),) + ((group, 2 * hidden),) * parts,
-        (me, got, gate, up),
-        hbm=(3,),
-        scratch=held,
+        ((count, piece), up.shape) + ((group, 2 * hidden),) * parts,
+        (got, gate, up),
+        hbm=(2,),
+        scratch=(DMA,),
     )
     pre = to_all(sent)
-    grads, *sent = run(part(grads_kernel, parts), ((count, piece),) + ((group, hidden),) * parts, (me, got, down))
+    grads, down, *sent = run(
+        part(grads_kernel, parts),
+        ((count, piece), down.shape) + ((group, hidden),) * parts,
+        (got, down, sent[0]),
+        hbm=(1,),
+        scratch=(DMA,),
+    )
     hidden_grad = to_all(sent)
     (active,) = run(part(hidden_kernel, hidden, parts), ((group, hidden),), (*pre, sent[0]))
     actives = to_all([active] * parts)
-    (acts,) = run(part(grad_kernel, hidden, parts), ((group, 2 * hidden),), (*pre, *hidden_grad, active))
+    (acts,) = run(
+        part(grad_kernel, hidden, parts), ((group, 2 * hidden),), (*pre, *hidden_grad, active)
+    )
     acts = to_all([acts] * parts)
     turned = (hidden, piece)
     first, gate_turned, up_turned, woven = run(
-        part(output_kernel, parts), ((count, piece), turned, turned, (total, total)), (me, *actives, down, gate, up)
-    )
-    (back,) = run(part(back_kernel, parts), ((total, piece),), (*acts, gate_turned, up_turned, first, woven))
+        part(output_kernel, parts),
+        ((count, piece), turned, turned, (total, total)),
+        (*actives, down, gate, up),
+    )
+    (back,) = run(
+        part(back_kernel, parts), ((total, piece),), (*acts, gate_turned, up_turned, first, woven)
+    )
 
     step = 2 * LANES
     spec = pl.BlockSpec((step, hidden), lambda d: (d, 0))
@@ -362,13 +396,12 @@
     ids, gates = route_ids.T, gate_weights.T
     block = 2 * CAP
 
-    me = lax.axis_index("dp").astype(jnp.int32).reshape(1)
-    sent, row_hot, grad_hot, row_gate = prep(me, ids, gates, tokens, cotangent, experts, parts)
+    sent, row_hot, grad_hot, row_gate = prep(ids, gates, tokens, cotangent, experts, parts)
     sent = sent.reshape(parts * experts, block, piece)
     got = lax.all_to_all(sent, both, 0, 0, tiled=True)
     got = got.reshape(parts * experts * block, piece)
     tiled = piece % (2 * LANES) == 0 and parts & (parts - 1) == 0
-    back, totals = (tiled_middle if tiled else plain_middle)(me, got, gate, up, down)
+    back, totals = (tiled_middle if tiled else plain_middle)(got, gate, up, down)
     back = lax.all_to_all(back.reshape(parts * experts, block, piece), both, 0, 0, tiled=True)
     back = back.reshape(parts, experts * block, piece)
     output, grad_tokens = finish(row_hot, grad_hot, row_gate, back)

time: 96.2 us -> 95.3 us (level)
  waiting for transfers between devices: 25.7 us -> 24.4 us
    ppermute x12, waiting for transfers between devices: 6.97 us -> 5.61 us  [to_all(): lax.ppermute(blocks[k], 'dp', [(i, i ^ k) for i in range(parts)])]
  transfers between devices with their start and end apart: 13 -> 13, of which waited for: 6 -> 5; matrix products, arithmetic and copies ran while one was open for 0% -> 0% of each run, Pallas kernels for 10% -> 12%
where the time goes in v5:
time: 95.3 us; the launch traced here: 95.1 us
  blocking collectives  31.8 us (33%)
  waiting for transfers between devices  24.4 us (26%)
  Pallas kernels  21.9 us (23%)
  starting transfers between devices  16.2 us (17%)
    all_to_all x1, blocking collectives, body(): got = lax.all_to_all(sent, both, 0, 0, tiled=True)  31.8 us
    all_to_all x1, waiting for transfers between devices, body(): lax.all_to_all(back.reshape(parts * experts, block, piece), both, 0, 0, t...  18.7 us
    ppermute x12, starting transfers between devices, to_all(): lax.ppermute(blocks[k], 'dp', [(i, i ^ k) for i in range(parts)])  13.6 us
    pallas_call x6, Pallas kernels, run(): pl.pallas_call(kernel, out_shape=tuple((like(shape) for shape in outs)),...  10.4 us
    pallas_call x1, Pallas kernels, tiled_middle(): pl.pallas_call(part(weights_kernel, parts), out_shape=(like((piece, hidde...  5.91 us
    ppermute x12, waiting for transfers between devices, to_all(): lax.ppermute(blocks[k], 'dp', [(i, i ^ k) for i in range(parts)])  5.61 us
    pallas_call x1, Pallas kernels, prep(): pl.pallas_call(functools.partial(prep_kernel, experts), out_shape=(like((...  3.27 us
    all_to_all x1, starting transfers between devices, body(): lax.all_to_all(back.reshape(parts * experts, block, piece), both, 0, 0, t...  2.64 us
  transfers between devices with their start and end apart: 13, of which 5 were waited for; matrix products, arithmetic and copies ran while one was open for 0% of the time, Pallas kernels for 12%

profile of v5, /device:TPU:0, one launch (start us, length us, event | category | flops | bytes accessed | tf_op | source)
XLA Modules:
  0.0 95.1 jit_solution(5223706872016701386)
XLA Ops:
  0.6 0.0 copy-start
  0.6 3.3 %prep.1 = (bf16[4,64,1792]{2,1,0:T(8,128)(2,1)S(1)}, bf16[64,128]{1,0:T(8,128)(2,1)S(1)}, bf16[64,128]{1,0:T(8,128)(2,1)S(1)}, f32[64,1]{1,0:T(8,128)S(1)}) custom-call(s32[8,128]{1,0:T(8,128)} %bitcast.20, f32[8,128]{1,0:T(8,128)} %bitcast.21, bf16[128,7168]{1,0:T(8,128)(2,1)} %tokens.1, bf16[128,7168]{1,0:T(8,128)(2,1)} %cotangent.1), custom_call_target="tpu_custom_call" | custom-call | tf_op jit(solution)/shard_map/prep/pallas_call | solution.py:177
  3.9 31.8 %all_to_all.10 = bf16[32,8,1792]{2,1,0:T(8,128)(2,1)S(1)} all-to-all(bf16[32,8,1792]{2,1,0:T(8,128)(2,1)S(1)} %bitcast.17), channel_id=1, replica_groups=mesh['dp'=4,'expert'=8] {'dp','expert'}, dimensions={0} | all-to-all | bytes 1835008 | tf_op jit(solution)/shard_map/all_to_all | solution.py:401
  35.7 0.0 copy-done
  35.7 2.7 %shard_map.110 = (bf16[128,1792]{1,0:T(8,128)(2,1)S(1)}, bf16[1792,1024]{1,0:T(8,128)(2,1)S(1)}, bf16[32,2048]{1,0:T(8,128)(2,1)S(1)}, bf16[32,2048]{1,0:T(8,128...) custom-call(bf16[256,1792]{1,0:T(8,128)(2,1)S(1)} %bitcast.14, bf16[1792,1024]{1,0:T(8,128)(2,1)S(1)} %bitcast.12, ...), custom_call_target="tpu_custom_call" | custom-call | tf_op jit(solution)/shard_map/pallas_call | solution.py:315
  38.4 0.1 collective-permute-start
  38.5 1.1 %collective-permute-start.1 = (bf16[32,2048]{1,0:T(8,128)(2,1)S(1)}, bf16[32,2048]{1,0:T(8,128)(2,1)S(1)}, u32[]{:S(2)}, u32[]{:S(2)}) collective-permute-start(bf16[32,2048]{1,0:T(8,128)(2,1)S(1)} %get-tuple-element.36), channel_id=1, source_target_pairs={{0,16},{8,24},{16,0},{24,8},{1,17},{9,25},{17,1},{25,9},{2,18},{10... | collective-permute-start | bytes 393224 | tf_op jit(solution)/shard_map/ppermute | solution.py:328
  39.6 2.4 %collective-permute-start.2 = (bf16[32,2048]{1,0:T(8,128)(2,1)S(1)}, bf16[32,2048]{1,0:T(8,128)(2,1)S(1)}, u32[]{:S(2)}, u32[]{:S(2)}) collective-permute-start(bf16[32,2048]{1,0:T(8,128)(2,1)S(1)} %get-tuple-element.37), channel_id=1, source_target_pairs={{0,24},{8,16},{16,8},{24,0},{1,25},{9,17},{17,9},{25,1},{2,26},{10... | collective-permute-start | bytes 393224 | tf_op jit(solution)/shard_map/ppermute | solution.py:328
  42.0 2.7 %shard_map.111 = (bf16[128,1792]{1,0:T(8,128)(2,1)S(1)}, bf16[1792,1024]{1,0:T(8,128)(2,1)S(1)}, bf16[32,1024]{1,0:T(8,128)(2,1)S(1)}, bf16[32,1024]{1,0:T(8,128...) custom-call(bf16[256,1792]{1,0:T(8,128)(2,1)S(1)} %bitcast.15, bf16[1792,1024]{1,0:T(8,128)(2,1)} %bitcast.18, ...), custom_call_target="tpu_custom_call" | custom-call | tf_op jit(solution)/shard_map/pallas_call | solution.py:315
  44.7 0.2 collective-permute-start.3
  44.9 1.0 %collective-permute-start.4 = (bf16[32,1024]{1,0:T(8,128)(2,1)S(1)}, bf16[32,1024]{1,0:T(8,128)(2,1)S(1)}, u32[]{:S(2)}, u32[]{:S(2)}) collective-permute-start(bf16[32,1024]{1,0:T(8,128)(2,1)S(1)} %get-tuple-element.40), channel_id=1, source_target_pairs={{0,16},{8,24},{16,0},{24,8},{1,17},{9,25},{17,1},{25,9},{2,18},{10... | collective-permute-start | bytes 196616 | tf_op jit(solution)/shard_map/ppermute | solution.py:328
  45.9 0.0 collective-permute-done.refs_1_
  45.9 2.4 %collective-permute-start.5 = (bf16[32,1024]{1,0:T(8,128)(2,1)S(1)}, bf16[32,1024]{1,0:T(8,128)(2,1)S(1)}, u32[]{:S(2)}, u32[]{:S(2)}) collective-permute-start(bf16[32,1024]{1,0:T(8,128)(2,1)S(1)} %get-tuple-element.41), channel_id=1, source_target_pairs={{0,24},{8,16},{16,8},{24,0},{1,25},{9,17},{17,9},{25,1},{2,26},{10... | collective-permute-start | bytes 196616 | tf_op jit(solution)/shard_map/ppermute | solution.py:328
  48.3 0.0 collective-permute-done.1.refs_2_
  48.3 0.0 collective-permute-done.2.refs_3_
  48.3 0.1 shard_map.112.refs_8_.refs_0_
  48.4 0.7 collective-permute-start.11
  49.1 0.6 collective-permute-done.3.refs_5_
  49.7 0.1 collective-permute-done.4.refs_6_
  49.8 2.0 %collective-permute-done.5.refs_7_ = bf16[32,1024]{1,0:T(8,128)(2,1)S(1)} collective-permute-done((bf16[32,1024]{1,0:T(8,128)(2,1)S(1)}, bf16[32,1024]{1,0:T(8,128)(2,1)S(1)}, u32[]{:S(2)}, u32[]{:S(2)}) %collective-permute-start.5) | collective-permute-done | bytes 65568 | tf_op jit(solution)/shard_map/ppermute | solution.py:328
  51.8 0.1 shard_map.113.refs_0_.refs_4_
  51.9 1.7 %collective-permute-start.8 = (bf16[32,2048]{1,0:T(8,128)(2,1)S(1)}, bf16[32,2048]{1,0:T(8,128)(2,1)S(1)}, u32[]{:S(2)}, u32[]{:S(2)}) collective-permute-start(bf16[32,2048]{1,0:T(8,128)(2,1)S(1)} %shard_map.113.refs_0_.refs_4_), channel_id=1, source_target_pairs={{0,24},{8,16},{16,8},{24,0},{1,25},{9,17},{17,9},{25,1},{2,26},{10... | collective-permute-start | bytes 393224 | tf_op jit(solution)/shard_map/ppermute | solution.py:328
  53.7 0.7 collective-permute-start.7
  54.4 1.1 %collective-permute-start.6 = (bf16[32,2048]{1,0:T(8,128)(2,1)S(1)}, bf16[32,2048]{1,0:T(8,128)(2,1)S(1)}, u32[]{:S(2)}, u32[]{:S(2)}) collective-permute-start(bf16[32,2048]{1,0:T(8,128)(2,1)S(1)} %shard_map.113.refs_0_.refs_4_), channel_id=1, source_target_pairs={{0,8},{8,0},{16,24},{24,16},{1,9},{9,1},{17,25},{25,17},{2,10},{10... | collective-permute-start | bytes 393224 | tf_op jit(solution)/shard_map/ppermute | solution.py:328
  55.5 0.8 collective-permute-start.10
  56.3 0.0 collective-permute-done.11.refs_3_
  56.3 1.4 %collective-permute-start.9 = (bf16[32,1024]{1,0:T(8,128)(2,1)S(1)}, bf16[32,1024]{1,0:T(8,128)(2,1)S(1)}, u32[]{:S(2)}, u32[]{:S(2)}) collective-permute-start(bf16[32,1024]{1,0:T(8,128)(2,1)S(1)} %shard_map.112.refs_8_.refs_0_), channel_id=1, source_target_pairs={{0,8},{8,0},{16,24},{24,16},{1,9},{9,1},{17,25},{25,17},{2,10},{10... | collective-permute-start | bytes 196616 | tf_op jit(solution)/shard_map/ppermute | solution.py:328
  57.7 2.9 %collective-permute-done.10.refs_2_ = bf16[32,1024]{1,0:T(8,128)(2,1)S(1)} collective-permute-done((bf16[32,1024]{1,0:T(8,128)(2,1)S(1)}, bf16[32,1024]{1,0:T(8,128)(2,1)S(1)}, u32[]{:S(2)}, u32[]{:S(2)}) %collective-permute-start.10) | collective-permute-done | bytes 65568 | tf_op jit(solution)/shard_map/ppermute | solution.py:328
  60.6 0.0 collective-permute-done.9.refs_1_
  60.7 2.4 %shard_map.114 = (bf16[128,1792]{1,0:T(8,128)(2,1)S(1)}, bf16[1024,1792]{1,0:T(8,128)(2,1)S(1)}, bf16[1024,1792]{1,0:T(8,128)(2,1)S(1)}, bf16[256,256]{1,0:T(8,128)(2,1)S(1)}) custom-call(bf16[32,1024]{1,0:T(8,128)(2,1)S(1)} %shard_map.112.refs_8_.refs_0_, bf16[32,1024]{1,0:T(8,128)(2,1)S(1)} %collective-permute-done.9.refs_1_, ...), custom_call_target="tpu_custom_call" | custom-call | tf_op jit(solution)/shard_map/pallas_call | solution.py:315
  63.0 0.0 collective-permute-done.8.refs_3_.refs_7_
  63.0 0.0 collective-permute-done.7.refs_2_.refs_6_
  63.0 0.0 collective-permute-done.6.refs_1_.refs_5_
  63.1 2.3 %shard_map.115 = bf16[256,1792]{1,0:T(8,128)(2,1)} custom-call(bf16[32,2048]{1,0:T(8,128)(2,1)S(1)} %shard_map.113.refs_0_.refs_4_, bf16[32,2048]{1,0:T(8,128)(2,1)S(1)} %collective-permute-done.6.refs_1_.refs_5_, bf16[32,2048]{1,0:T(8,128)(2,1)S(1)} %collective-permute-done.7.refs_2_.refs_6_, bf16[32,2048]{1,0:T(8,128)(2,1)S(1)} %collective-permute-done.8.refs_3_.refs_7_, ...), custom_call_target="tpu_custom_call" | custom-call | tf_op jit(solution)/shard_map/pallas_call | solution.py:315
  65.4 2.6 %all-to-all-start.1 = ((bf16[32,8,1792]{2,1,0:T(8,128)(2,1)}), bf16[32,8,1792]{2,1,0:T(8,128)(2,1)S(1)}, u32[]{:S(2)}, u32[]{:S(2)}) async-start(bf16[32,8,1792]{2,1,0:T(8,128)(2,1)} %bitcast.7), calls=%async_computation.1 | async-start | bytes 1835008 | tf_op jit(solution)/shard_map/all_to_all | solution.py:405
  68.0 5.9 %weights.1 = (bf16[1792,1024]{1,0:T(8,128)(2,1)}, bf16[1792,1024]{1,0:T(8,128)(2,1)}, bf16[1792,1024]{1,0:T(8,128)(2,1)}) custom-call(bf16[128,1792]{1,0:T(8,128)(2,1)S(1)} %get-tuple-element.50.rows, bf16[128,1792]{1,0:T(8,128)(2,1)S(1)} %get-tuple-element.51.grads, bf16[32,1024]{1,0:T(8,128)(2,1)S(1)} %shard_map.112.refs_8_.refs_0_, ...), custom_call_target="tpu_custom_call" | custom-call | tf_op jit(solution)/shard_map/weights/pallas_call | solution.py:377
  74.0 18.7 %all-to-all-done.1 = bf16[32,8,1792]{2,1,0:T(8,128)(2,1)S(1)} async-done(((bf16[32,8,1792]{2,1,0:T(8,128)(2,1)}), bf16[32,8,1792]{2,1,0:T(8,128)(2,1)S(1)}, u32[]{:S(2)}, u32[]{:S(2)}) %all-to-all-start.1) | async-done | bytes 917536 | tf_op jit(solution)/shard_map/all_to_all | solution.py:405
  92.7 2.4 %finish.1 = (bf16[128,7168]{1,0:T(8,128)(2,1)}, bf16[128,7168]{1,0:T(8,128)(2,1)}) custom-call(bf16[64,128]{1,0:T(8,128)(2,1)S(1)} %get-tuple-element.30.row_hot, bf16[64,128]{1,0:T(8,128)(2,1)S(1)} %get-tuple-element.31.grad_hot, f32[64,1]{1,0:T(8,128)S(1)} %get-tuple-element.32.row_gate, bf16[4,64,1792]{2,1,0:T(8,128)(2,1)S(1)} %bitcast.16), custom_call_target="tpu_custom_call" | custom-call | tf_op jit(solution)/shard_map/finish/pallas_call | solution.py:215
Async XLA Ops:
  0.6 35.1 %copy-start = (bf16[1,1792,1024]{2,1,0:T(8,128)(2,1)S(1)}, bf16[1,1792,1024]{2,1,0:T(8,128)(2,1)}, u32[]{:S(2)}) copy-start(bf16[1,1792,1024]{2,1,0:T(8,128)(2,1)} %param.10) | copy-start | bytes 11010052
  38.4 7.5 %collective-permute-start = (bf16[32,2048]{1,0:T(8,128)(2,1)S(1)}, bf16[32,2048]{1,0:T(8,128)(2,1)S(1)}, u32[]{:S(2)}, u32[]{:S(2)}) collective-permute-start(bf16[32,2048]{1,0:T(8,128)(2,1)S(1)} %get-tuple-element.35), channel_id=1, source_target_pairs={{0,8},{8,0},{16,24},{24,16},{1,9},{9,1},{17,25},{25,17},{2,10},{10... | collective-permute-start | bytes 393224 | tf_op jit(solution)/shard_map/ppermute | solution.py:328
  38.5 9.8 %collective-permute-start.1 = (bf16[32,2048]{1,0:T(8,128)(2,1)S(1)}, bf16[32,2048]{1,0:T(8,128)(2,1)S(1)}, u32[]{:S(2)}, u32[]{:S(2)}) collective-permute-start(bf16[32,2048]{1,0:T(8,128)(2,1)S(1)} %get-tuple-element.36), channel_id=1, source_target_pairs={{0,16},{8,24},{16,0},{24,8},{1,17},{9,25},{17,1},{25,9},{2,18},{10... | collective-permute-start | bytes 393224 | tf_op jit(solution)/shard_map/ppermute | solution.py:328
  39.6 8.7 %collective-permute-start.2 = (bf16[32,2048]{1,0:T(8,128)(2,1)S(1)}, bf16[32,2048]{1,0:T(8,128)(2,1)S(1)}, u32[]{:S(2)}, u32[]{:S(2)}) collective-permute-start(bf16[32,2048]{1,0:T(8,128)(2,1)S(1)} %get-tuple-element.37), channel_id=1, source_target_pairs={{0,24},{8,16},{16,8},{24,0},{1,25},{9,17},{17,9},{25,1},{2,26},{10... | collective-permute-start | bytes 393224 | tf_op jit(solution)/shard_map/ppermute | solution.py:328
  44.7 5.0 %collective-permute-start.3 = (bf16[32,1024]{1,0:T(8,128)(2,1)S(1)}, bf16[32,1024]{1,0:T(8,128)(2,1)S(1)}, u32[]{:S(2)}, u32[]{:S(2)}) collective-permute-start(bf16[32,1024]{1,0:T(8,128)(2,1)S(1)} %get-tuple-element.39), channel_id=1, source_target_pairs={{0,8},{8,0},{16,24},{24,16},{1,9},{9,1},{17,25},{25,17},{2,10},{10... | collective-permute-start | bytes 196616 | tf_op jit(solution)/shard_map/ppermute | solution.py:328
  44.9 4.9 %collective-permute-start.4 = (bf16[32,1024]{1,0:T(8,128)(2,1)S(1)}, bf16[32,1024]{1,0:T(8,128)(2,1)S(1)}, u32[]{:S(2)}, u32[]{:S(2)}) collective-permute-start(bf16[32,1024]{1,0:T(8,128)(2,1)S(1)} %get-tuple-element.40), channel_id=1, source_target_pairs={{0,16},{8,24},{16,0},{24,8},{1,17},{9,25},{17,1},{25,9},{2,18},{10... | collective-permute-start | bytes 196616 | tf_op jit(solution)/shard_map/ppermute | solution.py:328
  45.9 5.9 %collective-permute-start.5 = (bf16[32,1024]{1,0:T(8,128)(2,1)S(1)}, bf16[32,1024]{1,0:T(8,128)(2,1)S(1)}, u32[]{:S(2)}, u32[]{:S(2)}) collective-permute-start(bf16[32,1024]{1,0:T(8,128)(2,1)S(1)} %get-tuple-element.41), channel_id=1, source_target_pairs={{0,24},{8,16},{16,8},{24,0},{1,25},{9,17},{17,9},{25,1},{2,26},{10... | collective-permute-start | bytes 196616 | tf_op jit(solution)/shard_map/ppermute | solution.py:328
  48.4 7.9 %collective-permute-start.11 = (bf16[32,1024]{1,0:T(8,128)(2,1)S(1)}, bf16[32,1024]{1,0:T(8,128)(2,1)S(1)}, u32[]{:S(2)}, u32[]{:S(2)}) collective-permute-start(bf16[32,1024]{1,0:T(8,128)(2,1)S(1)} %shard_map.112.refs_8_.refs_0_), channel_id=1, source_target_pairs={{0,24},{8,16},{16,8},{24,0},{1,25},{9,17},{17,9},{25,1},{2,26},{10... | collective-permute-start | bytes 196616 | tf_op jit(solution)/shard_map/ppermute | solution.py:328
  51.9 11.1 %collective-permute-start.8 = (bf16[32,2048]{1,0:T(8,128)(2,1)S(1)}, bf16[32,2048]{1,0:T(8,128)(2,1)S(1)}, u32[]{:S(2)}, u32[]{:S(2)}) collective-permute-start(bf16[32,2048]{1,0:T(8,128)(2,1)S(1)} %shard_map.113.refs_0_.refs_4_), channel_id=1, source_target_pairs={{0,24},{8,16},{16,8},{24,0},{1,25},{9,17},{17,9},{25,1},{2,26},{10... | collective-permute-start | bytes 393224 | tf_op jit(solution)/shard_map/ppermute | solution.py:328
  53.7 9.4 %collective-permute-start.7 = (bf16[32,2048]{1,0:T(8,128)(2,1)S(1)}, bf16[32,2048]{1,0:T(8,128)(2,1)S(1)}, u32[]{:S(2)}, u32[]{:S(2)}) collective-permute-start(bf16[32,2048]{1,0:T(8,128)(2,1)S(1)} %shard_map.113.refs_0_.refs_4_), channel_id=1, source_target_pairs={{0,16},{8,24},{16,0},{24,8},{1,17},{9,25},{17,1},{25,9},{2,18},{10... | collective-permute-start | bytes 393224 | tf_op jit(solution)/shard_map/ppermute | solution.py:328
  54.4 8.7 %collective-permute-start.6 = (bf16[32,2048]{1,0:T(8,128)(2,1)S(1)}, bf16[32,2048]{1,0:T(8,128)(2,1)S(1)}, u32[]{:S(2)}, u32[]{:S(2)}) collective-permute-start(bf16[32,2048]{1,0:T(8,128)(2,1)S(1)} %shard_map.113.refs_0_.refs_4_), channel_id=1, source_target_pairs={{0,8},{8,0},{16,24},{24,16},{1,9},{9,1},{17,25},{25,17},{2,10},{10... | collective-permute-start | bytes 393224 | tf_op jit(solution)/shard_map/ppermute | solution.py:328
  55.5 5.2 %collective-permute-start.10 = (bf16[32,1024]{1,0:T(8,128)(2,1)S(1)}, bf16[32,1024]{1,0:T(8,128)(2,1)S(1)}, u32[]{:S(2)}, u32[]{:S(2)}) collective-permute-start(bf16[32,1024]{1,0:T(8,128)(2,1)S(1)} %shard_map.112.refs_8_.refs_0_), channel_id=1, source_target_pairs={{0,16},{8,24},{16,0},{24,8},{1,17},{9,25},{17,1},{25,9},{2,18},{10... | collective-permute-start | bytes 196616 | tf_op jit(solution)/shard_map/ppermute | solution.py:328
  56.3 4.3 %collective-permute-start.9 = (bf16[32,1024]{1,0:T(8,128)(2,1)S(1)}, bf16[32,1024]{1,0:T(8,128)(2,1)S(1)}, u32[]{:S(2)}, u32[]{:S(2)}) collective-permute-start(bf16[32,1024]{1,0:T(8,128)(2,1)S(1)} %shard_map.112.refs_8_.refs_0_), channel_id=1, source_target_pairs={{0,8},{8,0},{16,24},{24,16},{1,9},{9,1},{17,25},{25,17},{2,10},{10... | collective-permute-start | bytes 196616 | tf_op jit(solution)/shard_map/ppermute | solution.py:328
  65.4 27.3 %all-to-all-start.1 = ((bf16[32,8,1792]{2,1,0:T(8,128)(2,1)}), bf16[32,8,1792]{2,1,0:T(8,128)(2,1)S(1)}, u32[]{:S(2)}, u32[]{:S(2)}) async-start(bf16[32,8,1792]{2,1,0:T(8,128)(2,1)} %bitcast.7), calls=%async_computation.1 | async-start | bytes 1835008 | tf_op jit(solution)/shard_map/all_to_all | solution.py:405

commit v6 on v5

--- a/solution.py
+++ b/solution.py
@@ -278,19 +278,19 @@
 
 def output_kernel(parts, *refs):
     active = stacked(refs[:parts])
-    down, gate, up, out, gate_turned, up_turned, woven = refs[parts:]
+    down, gate, up, out, turned, woven = refs[parts:]
+    hidden = gate.shape[1]
     count = active.shape[0]
     out[...] = mm(active, down[...], 1, 1).astype(BF16)
     woven[...] = weave(count, lax.axis_index("dp"), count // parts)
-    gate_turned[...] = gate[...].T
-    up_turned[...] = up[...].T
+    turned[:hidden] = gate[...].T
+    turned[hidden:] = up[...].T
 
 
 def back_kernel(parts, *refs):
     acts = stacked(refs[:parts])
-    gate_turned, up_turned, first, woven, out = refs[parts:]
-    hidden = gate_turned.shape[0]
-    total = mm(acts[:, :hidden], gate_turned[...]) + mm(acts[:, hidden:], up_turned[...])
+    turned, first, woven, out = refs[parts:]
+    total = mm(acts, turned[...])
     both = jnp.concatenate([first[...], total.astype(BF16)], axis=0)
     out[...] = mm(woven[...], both).astype(BF16)
 
@@ -361,15 +361,12 @@
         part(grad_kernel, hidden, parts), ((group, 2 * hidden),), (*pre, *hidden_grad, active)
     )
     acts = to_all([acts] * parts)
-    turned = (hidden, piece)
-    first, gate_turned, up_turned, woven = run(
+    first, turned, woven = run(
         part(output_kernel, parts),
-        ((count, piece), turned, turned, (total, total)),
+        ((count, piece), (2 * hidden, piece), (total, total)),
         (*actives, down, gate, up),
     )
-    (back,) = run(
-        part(back_kernel, parts), ((total, piece),), (*acts, gate_turned, up_turned, first, woven)
-    )
+    (back,) = run(part(back_kernel, parts), ((total, piece),), (*acts, turned, first, woven))
 
     step = 2 * LANES
     spec = pl.BlockSpec((step, hidden), lambda d: (d, 0))

time: 95.3 us -> 95.3 us (level)
  no operation moved by 1% of the time
where the time goes in v6:
time: 95.3 us; the launch traced here: 95.1 us
  blocking collectives  31.8 us (33%)
  waiting for transfers between devices  24.4 us (26%)
  Pallas kernels  21.9 us (23%)
  starting transfers between devices  16.2 us (17%)
    all_to_all x1, blocking collectives, body(): got = lax.all_to_all(sent, both, 0, 0, tiled=True)  31.8 us
    all_to_all x1, waiting for transfers between devices, body(): lax.all_to_all(back.reshape(parts * experts, block, piece), both, 0, 0, t...  18.7 us
    ppermute x12, starting transfers between devices, to_all(): lax.ppermute(blocks[k], 'dp', [(i, i ^ k) for i in range(parts)])  13.6 us
    pallas_call x6, Pallas kernels, run(): pl.pallas_call(kernel, out_shape=tuple((like(shape) for shape in outs)),...  10.4 us
    pallas_call x1, Pallas kernels, tiled_middle(): pl.pallas_call(part(weights_kernel, parts), out_shape=(like((piece, hidde...  5.92 us
    ppermute x12, waiting for transfers between devices, to_all(): lax.ppermute(blocks[k], 'dp', [(i, i ^ k) for i in range(parts)])  5.61 us
    pallas_call x1, Pallas kernels, prep(): pl.pallas_call(functools.partial(prep_kernel, experts), out_shape=(like((...  3.27 us
    all_to_all x1, starting transfers between devices, body(): lax.all_to_all(back.reshape(parts * experts, block, piece), both, 0, 0, t...  2.64 us
  transfers between devices with their start and end apart: 13, of which 5 were waited for; matrix products, arithmetic and copies ran while one was open for 0% of the time, Pallas kernels for 12%

profile of v6, /device:TPU:0, one launch (start us, length us, event | category | flops | bytes accessed | tf_op | source)
XLA Modules:
  0.0 95.1 jit_solution(14276997152469313807)
XLA Ops:
  0.6 0.0 copy-start
  0.6 3.3 %prep.1 = (bf16[4,64,1792]{2,1,0:T(8,128)(2,1)S(1)}, bf16[64,128]{1,0:T(8,128)(2,1)S(1)}, bf16[64,128]{1,0:T(8,128)(2,1)S(1)}, f32[64,1]{1,0:T(8,128)S(1)}) custom-call(s32[8,128]{1,0:T(8,128)} %bitcast.20, f32[8,128]{1,0:T(8,128)} %bitcast.21, bf16[128,7168]{1,0:T(8,128)(2,1)} %tokens.1, bf16[128,7168]{1,0:T(8,128)(2,1)} %cotangent.1), custom_call_target="tpu_custom_call" | custom-call | tf_op jit(solution)/shard_map/prep/pallas_call | solution.py:177
  3.9 31.8 %all_to_all.10 = bf16[32,8,1792]{2,1,0:T(8,128)(2,1)S(1)} all-to-all(bf16[32,8,1792]{2,1,0:T(8,128)(2,1)S(1)} %bitcast.17), channel_id=1, replica_groups=mesh['dp'=4,'expert'=8] {'dp','expert'}, dimensions={0} | all-to-all | bytes 1835008 | tf_op jit(solution)/shard_map/all_to_all | solution.py:398
  35.7 0.0 copy-done
  35.7 2.7 %shard_map.110 = (bf16[128,1792]{1,0:T(8,128)(2,1)S(1)}, bf16[1792,1024]{1,0:T(8,128)(2,1)S(1)}, bf16[32,2048]{1,0:T(8,128)(2,1)S(1)}, bf16[32,2048]{1,0:T(8,128...) custom-call(bf16[256,1792]{1,0:T(8,128)(2,1)S(1)} %bitcast.14, bf16[1792,1024]{1,0:T(8,128)(2,1)S(1)} %bitcast.12, ...), custom_call_target="tpu_custom_call" | custom-call | tf_op jit(solution)/shard_map/pallas_call | solution.py:315
  38.4 0.1 collective-permute-start
  38.5 1.1 %collective-permute-start.1 = (bf16[32,2048]{1,0:T(8,128)(2,1)S(1)}, bf16[32,2048]{1,0:T(8,128)(2,1)S(1)}, u32[]{:S(2)}, u32[]{:S(2)}) collective-permute-start(bf16[32,2048]{1,0:T(8,128)(2,1)S(1)} %get-tuple-element.35), channel_id=1, source_target_pairs={{0,16},{8,24},{16,0},{24,8},{1,17},{9,25},{17,1},{25,9},{2,18},{10... | collective-permute-start | bytes 393224 | tf_op jit(solution)/shard_map/ppermute | solution.py:328
  39.6 2.4 %collective-permute-start.2 = (bf16[32,2048]{1,0:T(8,128)(2,1)S(1)}, bf16[32,2048]{1,0:T(8,128)(2,1)S(1)}, u32[]{:S(2)}, u32[]{:S(2)}) collective-permute-start(bf16[32,2048]{1,0:T(8,128)(2,1)S(1)} %get-tuple-element.36), channel_id=1, source_target_pairs={{0,24},{8,16},{16,8},{24,0},{1,25},{9,17},{17,9},{25,1},{2,26},{10... | collective-permute-start | bytes 393224 | tf_op jit(solution)/shard_map/ppermute | solution.py:328
  42.0 2.7 %shard_map.111 = (bf16[128,1792]{1,0:T(8,128)(2,1)S(1)}, bf16[1792,1024]{1,0:T(8,128)(2,1)S(1)}, bf16[32,1024]{1,0:T(8,128)(2,1)S(1)}, bf16[32,1024]{1,0:T(8,128...) custom-call(bf16[256,1792]{1,0:T(8,128)(2,1)S(1)} %bitcast.15, bf16[1792,1024]{1,0:T(8,128)(2,1)} %bitcast.18, ...), custom_call_target="tpu_custom_call" | custom-call | tf_op jit(solution)/shard_map/pallas_call | solution.py:315
  44.7 0.2 collective-permute-start.3
  44.9 1.0 %collective-permute-start.4 = (bf16[32,1024]{1,0:T(8,128)(2,1)S(1)}, bf16[32,1024]{1,0:T(8,128)(2,1)S(1)}, u32[]{:S(2)}, u32[]{:S(2)}) collective-permute-start(bf16[32,1024]{1,0:T(8,128)(2,1)S(1)} %get-tuple-element.39), channel_id=1, source_target_pairs={{0,16},{8,24},{16,0},{24,8},{1,17},{9,25},{17,1},{25,9},{2,18},{10... | collective-permute-start | bytes 196616 | tf_op jit(solution)/shard_map/ppermute | solution.py:328
  45.9 0.0 collective-permute-done.refs_1_
  45.9 2.4 %collective-permute-start.5 = (bf16[32,1024]{1,0:T(8,128)(2,1)S(1)}, bf16[32,1024]{1,0:T(8,128)(2,1)S(1)}, u32[]{:S(2)}, u32[]{:S(2)}) collective-permute-start(bf16[32,1024]{1,0:T(8,128)(2,1)S(1)} %get-tuple-element.40), channel_id=1, source_target_pairs={{0,24},{8,16},{16,8},{24,0},{1,25},{9,17},{17,9},{25,1},{2,26},{10... | collective-permute-start | bytes 196616 | tf_op jit(solution)/shard_map/ppermute | solution.py:328
  48.3 0.0 collective-permute-done.1.refs_2_
  48.3 0.0 collective-permute-done.2.refs_3_
  48.3 0.1 shard_map.112.refs_8_.refs_0_
  48.4 0.7 collective-permute-start.11
  49.1 0.6 collective-permute-done.3.refs_5_
  49.7 0.1 collective-permute-done.4.refs_6_
  49.8 2.0 %collective-permute-done.5.refs_7_ = bf16[32,1024]{1,0:T(8,128)(2,1)S(1)} collective-permute-done((bf16[32,1024]{1,0:T(8,128)(2,1)S(1)}, bf16[32,1024]{1,0:T(8,128)(2,1)S(1)}, u32[]{:S(2)}, u32[]{:S(2)}) %collective-permute-start.5) | collective-permute-done | bytes 65568 | tf_op jit(solution)/shard_map/ppermute | solution.py:328
  51.8 0.1 shard_map.113.refs_0_.refs_4_
  51.9 1.7 %collective-permute-start.8 = (bf16[32,2048]{1,0:T(8,128)(2,1)S(1)}, bf16[32,2048]{1,0:T(8,128)(2,1)S(1)}, u32[]{:S(2)}, u32[]{:S(2)}) collective-permute-start(bf16[32,2048]{1,0:T(8,128)(2,1)S(1)} %shard_map.113.refs_0_.refs_4_), channel_id=1, source_target_pairs={{0,24},{8,16},{16,8},{24,0},{1,25},{9,17},{17,9},{25,1},{2,26},{10... | collective-permute-start | bytes 393224 | tf_op jit(solution)/shard_map/ppermute | solution.py:328
  53.7 0.7 collective-permute-start.7
  54.4 1.1 %collective-permute-start.6 = (bf16[32,2048]{1,0:T(8,128)(2,1)S(1)}, bf16[32,2048]{1,0:T(8,128)(2,1)S(1)}, u32[]{:S(2)}, u32[]{:S(2)}) collective-permute-start(bf16[32,2048]{1,0:T(8,128)(2,1)S(1)} %shard_map.113.refs_0_.refs_4_), channel_id=1, source_target_pairs={{0,8},{8,0},{16,24},{24,16},{1,9},{9,1},{17,25},{25,17},{2,10},{10... | collective-permute-start | bytes 393224 | tf_op jit(solution)/shard_map/ppermute | solution.py:328
  55.5 0.8 collective-permute-start.10
  56.3 0.0 collective-permute-done.11.refs_3_
  56.3 1.4 %collective-permute-start.9 = (bf16[32,1024]{1,0:T(8,128)(2,1)S(1)}, bf16[32,1024]{1,0:T(8,128)(2,1)S(1)}, u32[]{:S(2)}, u32[]{:S(2)}) collective-permute-start(bf16[32,1024]{1,0:T(8,128)(2,1)S(1)} %shard_map.112.refs_8_.refs_0_), channel_id=1, source_target_pairs={{0,8},{8,0},{16,24},{24,16},{1,9},{9,1},{17,25},{25,17},{2,10},{10... | collective-permute-start | bytes 196616 | tf_op jit(solution)/shard_map/ppermute | solution.py:328
  57.7 2.9 %collective-permute-done.10.refs_2_ = bf16[32,1024]{1,0:T(8,128)(2,1)S(1)} collective-permute-done((bf16[32,1024]{1,0:T(8,128)(2,1)S(1)}, bf16[32,1024]{1,0:T(8,128)(2,1)S(1)}, u32[]{:S(2)}, u32[]{:S(2)}) %collective-permute-start.10) | collective-permute-done | bytes 65568 | tf_op jit(solution)/shard_map/ppermute | solution.py:328
  60.6 0.0 collective-permute-done.9.refs_1_
  60.7 2.4 %shard_map.114 = (bf16[128,1792]{1,0:T(8,128)(2,1)S(1)}, bf16[2048,1792]{1,0:T(8,128)(2,1)S(1)}, bf16[256,256]{1,0:T(8,128)(2,1)S(1)}) custom-call(bf16[32,1024]{1,0:T(8,128)(2,1)S(1)} %shard_map.112.refs_8_.refs_0_, bf16[32,1024]{1,0:T(8,128)(2,1)S(1)} %collective-permute-done.9.refs_1_, bf16[32,1024]{1,0:T(8,128)(2,1)S(1)} %collective-permute-done.10.refs_2_, ...), custom_call_target="tpu_custom_call" | custom-call | tf_op jit(solution)/shard_map/pallas_call | solution.py:315
  63.0 0.0 collective-permute-done.8.refs_3_.refs_7_
  63.0 0.0 collective-permute-done.7.refs_2_.refs_6_
  63.0 0.0 collective-permute-done.6.refs_1_.refs_5_
  63.1 2.3 %shard_map.115 = bf16[256,1792]{1,0:T(8,128)(2,1)} custom-call(bf16[32,2048]{1,0:T(8,128)(2,1)S(1)} %shard_map.113.refs_0_.refs_4_, bf16[32,2048]{1,0:T(8,128)(2,1)S(1)} %collective-permute-done.6.refs_1_.refs_5_, bf16[32,2048]{1,0:T(8,128)(2,1)S(1)} %collective-permute-done.7.refs_2_.refs_6_, bf16[32,2048]{1,0:T(8,128)(2,1)S(1)} %collective-permute-done.8.refs_3_.refs_7_, ...), custom_call_target="tpu_custom_call" | custom-call | tf_op jit(solution)/shard_map/pallas_call | solution.py:315
  65.4 2.6 %all-to-all-start.1 = ((bf16[32,8,1792]{2,1,0:T(8,128)(2,1)}), bf16[32,8,1792]{2,1,0:T(8,128)(2,1)S(1)}, u32[]{:S(2)}, u32[]{:S(2)}) async-start(bf16[32,8,1792]{2,1,0:T(8,128)(2,1)} %bitcast.7), calls=%async_computation.1 | async-start | bytes 1835008 | tf_op jit(solution)/shard_map/all_to_all | solution.py:402
  68.0 5.9 %weights.1 = (bf16[1792,1024]{1,0:T(8,128)(2,1)}, bf16[1792,1024]{1,0:T(8,128)(2,1)}, bf16[1792,1024]{1,0:T(8,128)(2,1)}) custom-call(bf16[128,1792]{1,0:T(8,128)(2,1)S(1)} %get-tuple-element.48.rows, bf16[128,1792]{1,0:T(8,128)(2,1)S(1)} %get-tuple-element.49.grads, bf16[32,1024]{1,0:T(8,128)(2,1)S(1)} %shard_map.112.refs_8_.refs_0_, ...), custom_call_target="tpu_custom_call" | custom-call | tf_op jit(solution)/shard_map/weights/pallas_call | solution.py:374
  74.0 18.7 %all-to-all-done.1 = bf16[32,8,1792]{2,1,0:T(8,128)(2,1)S(1)} async-done(((bf16[32,8,1792]{2,1,0:T(8,128)(2,1)}), bf16[32,8,1792]{2,1,0:T(8,128)(2,1)S(1)}, u32[]{:S(2)}, u32[]{:S(2)}) %all-to-all-start.1) | async-done | bytes 917536 | tf_op jit(solution)/shard_map/all_to_all | solution.py:402
  92.7 2.4 %finish.1 = (bf16[128,7168]{1,0:T(8,128)(2,1)}, bf16[128,7168]{1,0:T(8,128)(2,1)}) custom-call(bf16[64,128]{1,0:T(8,128)(2,1)S(1)} %get-tuple-element.29.row_hot, bf16[64,128]{1,0:T(8,128)(2,1)S(1)} %get-tuple-element.30.grad_hot, f32[64,1]{1,0:T(8,128)S(1)} %get-tuple-element.31.row_gate, bf16[4,64,1792]{2,1,0:T(8,128)(2,1)S(1)} %bitcast.16), custom_call_target="tpu_custom_call" | custom-call | tf_op jit(solution)/shard_map/finish/pallas_call | solution.py:215
Async XLA Ops:
  0.6 35.1 %copy-start = (bf16[1,1792,1024]{2,1,0:T(8,128)(2,1)S(1)}, bf16[1,1792,1024]{2,1,0:T(8,128)(2,1)}, u32[]{:S(2)}) copy-start(bf16[1,1792,1024]{2,1,0:T(8,128)(2,1)} %param.10) | copy-start | bytes 11010052
  38.4 7.5 %collective-permute-start = (bf16[32,2048]{1,0:T(8,128)(2,1)S(1)}, bf16[32,2048]{1,0:T(8,128)(2,1)S(1)}, u32[]{:S(2)}, u32[]{:S(2)}) collective-permute-start(bf16[32,2048]{1,0:T(8,128)(2,1)S(1)} %get-tuple-element.34), channel_id=1, source_target_pairs={{0,8},{8,0},{16,24},{24,16},{1,9},{9,1},{17,25},{25,17},{2,10},{10... | collective-permute-start | bytes 393224 | tf_op jit(solution)/shard_map/ppermute | solution.py:328
  38.5 9.8 %collective-permute-start.1 = (bf16[32,2048]{1,0:T(8,128)(2,1)S(1)}, bf16[32,2048]{1,0:T(8,128)(2,1)S(1)}, u32[]{:S(2)}, u32[]{:S(2)}) collective-permute-start(bf16[32,2048]{1,0:T(8,128)(2,1)S(1)} %get-tuple-element.35), channel_id=1, source_target_pairs={{0,16},{8,24},{16,0},{24,8},{1,17},{9,25},{17,1},{25,9},{2,18},{10... | collective-permute-start | bytes 393224 | tf_op jit(solution)/shard_map/ppermute | solution.py:328
  39.6 8.7 %collective-permute-start.2 = (bf16[32,2048]{1,0:T(8,128)(2,1)S(1)}, bf16[32,2048]{1,0:T(8,128)(2,1)S(1)}, u32[]{:S(2)}, u32[]{:S(2)}) collective-permute-start(bf16[32,2048]{1,0:T(8,128)(2,1)S(1)} %get-tuple-element.36), channel_id=1, source_target_pairs={{0,24},{8,16},{16,8},{24,0},{1,25},{9,17},{17,9},{25,1},{2,26},{10... | collective-permute-start | bytes 393224 | tf_op jit(solution)/shard_map/ppermute | solution.py:328
  44.7 5.0 %collective-permute-start.3 = (bf16[32,1024]{1,0:T(8,128)(2,1)S(1)}, bf16[32,1024]{1,0:T(8,128)(2,1)S(1)}, u32[]{:S(2)}, u32[]{:S(2)}) collective-permute-start(bf16[32,1024]{1,0:T(8,128)(2,1)S(1)} %get-tuple-element.38), channel_id=1, source_target_pairs={{0,8},{8,0},{16,24},{24,16},{1,9},{9,1},{17,25},{25,17},{2,10},{10... | collective-permute-start | bytes 196616 | tf_op jit(solution)/shard_map/ppermute | solution.py:328
  44.9 4.9 %collective-permute-start.4 = (bf16[32,1024]{1,0:T(8,128)(2,1)S(1)}, bf16[32,1024]{1,0:T(8,128)(2,1)S(1)}, u32[]{:S(2)}, u32[]{:S(2)}) collective-permute-start(bf16[32,1024]{1,0:T(8,128)(2,1)S(1)} %get-tuple-element.39), channel_id=1, source_target_pairs={{0,16},{8,24},{16,0},{24,8},{1,17},{9,25},{17,1},{25,9},{2,18},{10... | collective-permute-start | bytes 196616 | tf_op jit(solution)/shard_map/ppermute | solution.py:328
  45.9 5.9 %collective-permute-start.5 = (bf16[32,1024]{1,0:T(8,128)(2,1)S(1)}, bf16[32,1024]{1,0:T(8,128)(2,1)S(1)}, u32[]{:S(2)}, u32[]{:S(2)}) collective-permute-start(bf16[32,1024]{1,0:T(8,128)(2,1)S(1)} %get-tuple-element.40), channel_id=1, source_target_pairs={{0,24},{8,16},{16,8},{24,0},{1,25},{9,17},{17,9},{25,1},{2,26},{10... | collective-permute-start | bytes 196616 | tf_op jit(solution)/shard_map/ppermute | solution.py:328
  48.4 7.9 %collective-permute-start.11 = (bf16[32,1024]{1,0:T(8,128)(2,1)S(1)}, bf16[32,1024]{1,0:T(8,128)(2,1)S(1)}, u32[]{:S(2)}, u32[]{:S(2)}) collective-permute-start(bf16[32,1024]{1,0:T(8,128)(2,1)S(1)} %shard_map.112.refs_8_.refs_0_), channel_id=1, source_target_pairs={{0,24},{8,16},{16,8},{24,0},{1,25},{9,17},{17,9},{25,1},{2,26},{10... | collective-permute-start | bytes 196616 | tf_op jit(solution)/shard_map/ppermute | solution.py:328
  51.9 11.1 %collective-permute-start.8 = (bf16[32,2048]{1,0:T(8,128)(2,1)S(1)}, bf16[32,2048]{1,0:T(8,128)(2,1)S(1)}, u32[]{:S(2)}, u32[]{:S(2)}) collective-permute-start(bf16[32,2048]{1,0:T(8,128)(2,1)S(1)} %shard_map.113.refs_0_.refs_4_), channel_id=1, source_target_pairs={{0,24},{8,16},{16,8},{24,0},{1,25},{9,17},{17,9},{25,1},{2,26},{10... | collective-permute-start | bytes 393224 | tf_op jit(solution)/shard_map/ppermute | solution.py:328
  53.7 9.4 %collective-permute-start.7 = (bf16[32,2048]{1,0:T(8,128)(2,1)S(1)}, bf16[32,2048]{1,0:T(8,128)(2,1)S(1)}, u32[]{:S(2)}, u32[]{:S(2)}) collective-permute-start(bf16[32,2048]{1,0:T(8,128)(2,1)S(1)} %shard_map.113.refs_0_.refs_4_), channel_id=1, source_target_pairs={{0,16},{8,24},{16,0},{24,8},{1,17},{9,25},{17,1},{25,9},{2,18},{10... | collective-permute-start | bytes 393224 | tf_op jit(solution)/shard_map/ppermute | solution.py:328
  54.4 8.7 %collective-permute-start.6 = (bf16[32,2048]{1,0:T(8,128)(2,1)S(1)}, bf16[32,2048]{1,0:T(8,128)(2,1)S(1)}, u32[]{:S(2)}, u32[]{:S(2)}) collective-permute-start(bf16[32,2048]{1,0:T(8,128)(2,1)S(1)} %shard_map.113.refs_0_.refs_4_), channel_id=1, source_target_pairs={{0,8},{8,0},{16,24},{24,16},{1,9},{9,1},{17,25},{25,17},{2,10},{10... | collective-permute-start | bytes 393224 | tf_op jit(solution)/shard_map/ppermute | solution.py:328
  55.5 5.2 %collective-permute-start.10 = (bf16[32,1024]{1,0:T(8,128)(2,1)S(1)}, bf16[32,1024]{1,0:T(8,128)(2,1)S(1)}, u32[]{:S(2)}, u32[]{:S(2)}) collective-permute-start(bf16[32,1024]{1,0:T(8,128)(2,1)S(1)} %shard_map.112.refs_8_.refs_0_), channel_id=1, source_target_pairs={{0,16},{8,24},{16,0},{24,8},{1,17},{9,25},{17,1},{25,9},{2,18},{10... | collective-permute-start | bytes 196616 | tf_op jit(solution)/shard_map/ppermute | solution.py:328
  56.3 4.3 %collective-permute-start.9 = (bf16[32,1024]{1,0:T(8,128)(2,1)S(1)}, bf16[32,1024]{1,0:T(8,128)(2,1)S(1)}, u32[]{:S(2)}, u32[]{:S(2)}) collective-permute-start(bf16[32,1024]{1,0:T(8,128)(2,1)S(1)} %shard_map.112.refs_8_.refs_0_), channel_id=1, source_target_pairs={{0,8},{8,0},{16,24},{24,16},{1,9},{9,1},{17,25},{25,17},{2,10},{10... | collective-permute-start | bytes 196616 | tf_op jit(solution)/shard_map/ppermute | solution.py:328
  65.4 27.3 %all-to-all-start.1 = ((bf16[32,8,1792]{2,1,0:T(8,128)(2,1)}), bf16[32,8,1792]{2,1,0:T(8,128)(2,1)S(1)}, u32[]{:S(2)}, u32[]{:S(2)}) async-start(bf16[32,8,1792]{2,1,0:T(8,128)(2,1)} %bitcast.7), calls=%async_computation.1 | async-start | bytes 1835008 | tf_op jit(solution)/shard_map/all_to_all | solution.py:402
